TPU v7x, 128 devices: a whole 4x4x4 slice. The times are simulated.
128 devices in a mesh: branch: 8 (over x_hi, y), dp: 16 (over z, x_lo, core).
Axes of the slice: x: 4 (x_hi: 2, x_lo: 2; x = x_hi * 2 + x_lo), y: 4, z: 4, core: 2. Of those that a mesh axis runs over, the one named last changes fastest.
Arguments:
- hidden_in: bfloat16 [2048, 4096], P('dp', 'branch'), may hold values from -6 to 6
- context: bfloat16 [2048, 4096], P('dp'), may hold values from -6 to 6
- branch_wo: bfloat16 [8, 4096, 4096], P('branch', 'dp'), may hold values from -0.09375 to 0.09375
- expert_ids: int32 [2048, 2], P('dp'), may hold values from 0 to 7, all different within a row; in each aligned block of 128 rows (0 to 127, 128 to 255, ...) at most 48 rows name the same one
- gate_num: int32 [2048, 2], P('dp'), may hold values from 1 to 16
- w_gate: bfloat16 [8, 4096, 7168], P('branch', None, 'dp'), may hold values from -0.09375 to 0.09375
- w_up: bfloat16 [8, 4096, 7168], P('branch', None, 'dp'), may hold values from -0.09375 to 0.09375
- w_down: bfloat16 [8, 7168, 4096], P('branch', 'dp'), may hold values from -0.0625 to 0.0625
- cotangent: bfloat16 [2048, 4096], P('dp', 'branch'), may hold values from -6 to 6
Outputs:
- mixed: bfloat16 [2048, 4096], P('dp', 'branch')
- input_grad: bfloat16 [2048, 4096], P('dp', 'branch')
- grad_gate: bfloat16 [8, 4096, 7168], P('branch', None, 'dp')
- grad_up: bfloat16 [8, 4096, 7168], P('branch', None, 'dp')
- grad_down: bfloat16 [8, 7168, 4096], P('branch', 'dp')
Inputs may be any that keep to these rules, and one draw needn't show every extreme that they name: `expert_ids`: the two ids of a row differ. In each aligned block of 128 rows no expert is named by more than 48 rows, and in some block one expert is named by exactly 48 rows.
All inputs are finite; a program needn't handle non-finite values.
Results may differ from a plain program's by a relative error of at most 0.019.
Values may be sent and summed in bfloat16 or wider, within the bound.
A program may use at most 128 MiB of HBM per device.

v0:
```python
import jax
import jax.numpy as jnp
from jax import lax
from jax.sharding import PartitionSpec as P


def swiglu_parts(gate_pre, up_pre, d_act):
    sigma = jax.nn.sigmoid(gate_pre)
    silu = gate_pre * sigma
    act = (silu * up_pre).astype(jnp.bfloat16)
    d_gate = (d_act * up_pre * sigma * (1.0 + gate_pre * (1.0 - sigma))).astype(jnp.bfloat16)
    d_up = (d_act * silu).astype(jnp.bfloat16)
    return (act, d_gate, d_up)


def shards(hidden_in, context, branch_wo, expert_ids, gate_num, w_gate, w_up, w_down, cotangent):
    n_branch = lax.axis_size("branch")
    rows_tok, width = hidden_in.shape
    model_width = context.shape[1]
    capacity = 3 * rows_tok // n_branch
    summed = lax.psum_scatter(
        branch_wo[0].astype(jnp.float32).astype(jnp.bfloat16),
        "branch",
        scatter_dimension=1,
        tiled=True,
    ).astype(jnp.float32)
    mean_block = (summed / n_branch).astype(jnp.bfloat16)
    attended = jnp.dot(
        context,
        lax.all_gather(mean_block, "dp", axis=0, tiled=True),
        preferred_element_type=jnp.float32,
    )
    hidden = (hidden_in.astype(jnp.float32) + attended).astype(jnp.bfloat16)
    flat_ids = expert_ids.reshape(-1)
    labels = jnp.arange(n_branch, dtype=jnp.int32)
    onehot = (flat_ids[:, None] == labels[None, :]).astype(jnp.int32)
    before = jnp.cumsum(onehot, axis=0) - onehot
    slot = flat_ids * capacity + jnp.sum(before * onehot, axis=1)
    placing = (jnp.arange(n_branch * capacity, dtype=jnp.int32)[:, None] == slot[None, :]).astype(
        jnp.bfloat16
    )
    share = gate_num.astype(jnp.float32)
    share = share / jnp.sum(share, axis=1, keepdims=True)
    doubled = jnp.repeat(hidden, 2, axis=0)
    weighted = (
        share.reshape(-1)[:, None] * jnp.repeat(cotangent.astype(jnp.float32), 2, axis=0)
    ).astype(jnp.bfloat16)
    send_rows = (
        jnp.dot(placing, doubled, preferred_element_type=jnp.float32)
        .astype(jnp.bfloat16)
        .reshape(n_branch, capacity, width)
    )
    send_grads = (
        jnp.dot(placing, weighted, preferred_element_type=jnp.float32)
        .astype(jnp.bfloat16)
        .reshape(n_branch, capacity, width)
    )
    weight_gate = w_gate[0]
    weight_up = w_up[0]
    weight_down = w_down[0]
    got_rows, got_grads = (
        lax.all_to_all(send_rows, "branch", split_axis=0, concat_axis=2, tiled=True),
        lax.all_to_all(send_grads, "branch", split_axis=0, concat_axis=2, tiled=True),
    )
    all_rows, all_grads = (
        lax.all_gather(got_rows, "dp", axis=1, tiled=True),
        lax.all_gather(got_grads, "dp", axis=1, tiled=True),
    )
    rows_two = all_rows[0]
    grads_two = all_grads[0]
    gate_pre = jnp.dot(rows_two, weight_gate, preferred_element_type=jnp.float32)
    up_pre = jnp.dot(rows_two, weight_up, preferred_element_type=jnp.float32)
    d_act = jnp.einsum("rd,fd->rf", grads_two, weight_down, preferred_element_type=jnp.float32)
    act, d_gate, d_up = swiglu_parts(gate_pre, up_pre, d_act)
    grad_gate = jnp.einsum("rd,rf->df", rows_two, d_gate, preferred_element_type=jnp.float32)
    grad_up = jnp.einsum("rd,rf->df", rows_two, d_up, preferred_element_type=jnp.float32)
    grad_down = jnp.einsum("rf,rd->fd", act, grads_two, preferred_element_type=jnp.float32)
    output_term = jnp.dot(act, weight_down, preferred_element_type=jnp.float32)
    input_term = jnp.einsum(
        "rf,df->rd", d_gate, weight_gate, preferred_element_type=jnp.float32
    ) + jnp.einsum("rf,df->rd", d_up, weight_up, preferred_element_type=jnp.float32)
    folded = lax.psum_scatter(
        jnp.concatenate([output_term, input_term], axis=1).astype(jnp.bfloat16),
        "dp",
        scatter_dimension=0,
        tiled=True,
    )
    packed = folded.reshape(1, capacity, 2, model_width)
    returned = lax.all_to_all(packed, "branch", split_axis=3, concat_axis=0, tiled=True)
    picked = jnp.einsum(
        "sr,sc->rc",
        placing,
        returned.reshape(n_branch * capacity, 2 * width),
        preferred_element_type=jnp.float32,
    )
    picked = picked.reshape(rows_tok, 2, 2, width)
    mixed = (
        hidden.astype(jnp.float32) + jnp.sum(share[:, :, None] * picked[:, :, 0], axis=1)
    ).astype(jnp.bfloat16)
    input_grad = (cotangent.astype(jnp.float32) + jnp.sum(picked[:, :, 1], axis=1)).astype(
        jnp.bfloat16
    )
    return (
        mixed,
        input_grad,
        grad_gate.astype(jnp.bfloat16)[None],
        grad_up.astype(jnp.bfloat16)[None],
        grad_down.astype(jnp.bfloat16)[None],
    )


def solution(mesh):
    return jax.shard_map(
        shards,
        mesh=mesh,
        in_specs=(
            P("dp", "branch"),
            P("dp", None),
            P("branch", "dp", None),
            P("dp", None),
            P("dp", None),
            P("branch", None, "dp"),
            P("branch", None, "dp"),
            P("branch", "dp", None),
            P("dp", "branch"),
        ),
        out_specs=(
            P("dp", "branch"),
            P("dp", "branch"),
            P("branch", None, "dp"),
            P("branch", None, "dp"),
            P("branch", "dp", None),
        ),
        check_vma=False,
    )
```

profile of v0, /device:TPU:0, one launch (start us, length us, event | category | flops | bytes accessed | tf_op | source)
XLA Modules:
  0.0 441.6 jit_solution(16380945174118612632)
XLA Ops:
  8.0 82.4 %reduce-scatter.3.cloned.1.call-done = bf16[256,512]{1,0:T(8,128)(2,1)} async-done(((bf16[256,4096]{1,0:T(8,128)(2,1)}), bf16[256,512]{1,0:T(8,128)(2,1)}) %reduce-scatter.3.cloned.1.call-update) | async-done | bytes 262160 | tf_op jit(solution)/shard_map/reduce_scatter | solution.py:21
  90.3 1.7 multiply_convert_fusion.4
  92.1 0.8 copy.41
  95.7 1.0 broadcast_in_dim.21
  97.6 17.3 %all_to_all.51 = bf16[8,48,512]{2,1,0:T(8,128)(2,1)S(1)} all-to-all(bf16[8,48,512]{2,1,0:T(8,128)(2,1)S(1)} %bitcast.117), channel_id=1, replica_groups=mesh['branch'=8,'dp'=16] {'branch'}, dimensions={0} | all-to-all | bytes 786432 | tf_op jit(solution)/shard_map/all_to_all | solution.py:63
  114.9 0.8 copy.59
  115.9 15.9 %all-gather.4.cloned.1.call-done = bf16[4096,512]{1,0:T(8,128)(2,1)} async-done(((bf16[256,512]{1,0:T(8,128)(2,1)}), bf16[4096,512]{1,0:T(8,128)(2,1)}) %all-gather.4.cloned.1.call-update) | async-done | bytes 4194320 | tf_op jit(solution)/shard_map/all_gather | solution.py:30
  131.7 3.5 fusion.39
  135.9 21.2 %all_to_all.52 = bf16[8,48,512]{2,1,0:T(8,128)(2,1)S(1)} all-to-all(bf16[8,48,512]{2,1,0:T(8,128)(2,1)S(1)} %bitcast.119), channel_id=1, replica_groups=mesh['branch'=8,'dp'=16] {'branch'}, dimensions={0} | all-to-all | bytes 786432 | tf_op jit(solution)/shard_map/all_to_all | solution.py:62
  157.1 0.8 copy.58
  158.1 21.1 %all-gather.8.cloned.1.call-done = bf16[1,768,4096]{2,1,0:T(8,128)(2,1)} async-done(((bf16[1,48,4096]{2,1,0:T(8,128)(2,1)}), bf16[1,768,4096]{2,1,0:T(8,128)(2,1)}) %all-gather.8.cloned.1.call-update) | async-done | bytes 6291472 | tf_op jit(solution)/shard_map/all_gather | solution.py:67
  179.2 6.9 %fusion.2 = f32[768,448]{0,1:T(8,128)S(1)} fusion(bf16[1,768,4096]{2,1,0:T(8,128)(2,1)} %all-gather.8.cloned.1.call-done, bf16[1,448,4096]{2,1,0:T(8,128)(2,1)} %param.16), kind=kOutput, calls=%fused_computation.5 | convolution fusion | flops 2818572288 | bytes 11337728 | tf_op jit(solution)/shard_map/rd,fd->rf/dot_general | solution.py:73
  186.1 38.3 %all-gather.6.cloned.1.call-done = bf16[1,768,4096]{2,1,0:T(8,128)(2,1)} async-done(((bf16[1,48,4096]{2,1,0:T(8,128)(2,1)}), bf16[1,768,4096]{2,1,0:T(8,128)(2,1)}) %all-gather.6.cloned.1.call-update) | async-done | bytes 6291472 | tf_op jit(solution)/shard_map/all_gather | solution.py:66
  224.4 7.0 %fusion.10 = f32[768,448]{0,1:T(8,128)S(1)} fusion(bf16[1,768,4096]{2,1,0:T(8,128)(2,1)} %all-gather.6.cloned.1.call-done, bf16[1,4096,448]{1,2,0:T(8,128)(2,1)} %param.14), kind=kOutput, calls=%fused_computation.13 | convolution fusion | flops 2818572288 | bytes 11337728 | tf_op jit(solution)/shard_map/dot_general | solution.py:71
  231.5 4.4 multiply_convert_fusion.2
  235.9 3.9 convolution_convert_fusion
  239.9 3.5 fusion.34
  243.4 8.8 %add_convert_fusion = bf16[768,4096]{1,0:T(8,128)(2,1)} fusion(f32[768,4096]{1,0:T(8,128)S(1)} %fusion.34, bf16[768,448]{0,1:T(8,128)(2,1)} %get-tuple-element.27, bf16[1,4096,448]{1,2,0:T(8,128)(2,1)} %param.15), kind=kOutput, calls=%fused_computation.1 | convolution fusion | flops 2824863744 | bytes 23232512 | tf_op jit(solution)/shard_map/rf,df->rd/dot_general | solution.py:81
  252.2 8.2 %pad_maximum_fusion = bf16[768,8192]{1,0:T(8,128)(2,1)} fusion(bf16[768,4096]{1,0:T(8,128)(2,1)} %add_convert_fusion, bf16[768,4096]{1,0:T(8,128)(2,1)S(1)} %convolution_convert_fusion), kind=kLoop, calls=%fused_computation | loop fusion | flops 25165824 | bytes 25165824 | tf_op jit(solution)/shard_map/concatenate | solution.py:83
  260.7 0.8 copy-done.11
  261.5 7.4 %fusion.21 = bf16[1,448,4096]{2,1,0:T(8,128)(2,1)} fusion(bf16[768,448]{0,1:T(8,128)(2,1)S(1)} %copy-done.11, bf16[1,768,4096]{2,1,0:T(8,128)(2,1)} %all-gather.8.cloned.1.call-done), kind=kOutput, calls=%fused_computation.18 | convolution fusion | flops 2820407296 | bytes 10649600 | tf_op jit(solution)/shard_map/rf,rd->fd/dot_general | solution.py:77
  268.9 4.5 %fusion.24 = bf16[1,4096,448]{1,2,0:T(8,128)(2,1)} fusion(bf16[768,448]{0,1:T(8,128)(2,1)S(1)} %copy-done.4, bf16[1,768,4096]{2,1,0:T(8,128)(2,1)S(1)} %bitcast.123), kind=kOutput, calls=%fused_computation.19 | convolution fusion | flops 2820407296 | bytes 10649600 | tf_op jit(solution)/shard_map/rd,rf->df/dot_general | solution.py:75
  273.4 128.1 %reduce-scatter.5.cloned.1.call-done = bf16[48,8192]{1,0:T(8,128)(2,1)} async-done(((bf16[768,8192]{1,0:T(8,128)(2,1)}), bf16[48,8192]{1,0:T(8,128)(2,1)}) %reduce-scatter.5.cloned.1.call-update) | async-done | bytes 786448 | tf_op jit(solution)/shard_map/reduce_scatter | solution.py:82
  401.5 2.6 reshape.93
  404.0 1.7 copy.47
  405.8 4.0 reshape.98
  409.7 6.4 %all-to-all-start.2 = ((bf16[8,2,24576]{2,1,0:T(2,128)(2,1)}), bf16[8,2,24576]{2,1,0:T(2,128)(2,1)S(1)}, u32[]{:S(2)}, u32[]{:S(2)}) async-start(bf16[8,2,24576]{2,1,0:T(2,128)(2,1)} %reshape.98), calls=%async_computation.4 | async-start | bytes 1572864 | tf_op jit(solution)/shard_map/all_to_all | solution.py:89
  416.2 7.9 %fusion.27 = bf16[1,4096,448]{1,2,0:T(8,128)(2,1)} fusion(bf16[768,448]{0,1:T(8,128)(2,1)} %get-tuple-element.27, bf16[1,768,4096]{2,1,0:T(8,128)(2,1)} %all-gather.6.cloned.1.call-done), kind=kOutput, calls=%fused_computation.20 | convolution fusion | flops 2820407296 | bytes 10649600 | tf_op jit(solution)/shard_map/rd,rf->df/dot_general | solution.py:76
  424.0 4.0 all-to-all-done.2
  428.0 2.1 reshape.99
  430.1 1.3 copy.57
  431.4 0.8 copy.49
  (69 shorter events, 8.5 us)
Async XLA Ops:
  7.2 124.6 %copy-start = (bf16[128,4096]{1,0:T(8,128)(2,1)S(1)}, bf16[128,4096]{1,0:T(8,128)(2,1)}, u32[]{:S(2)}) copy-start(bf16[128,4096]{1,0:T(8,128)(2,1)} %param.10) | copy-start | bytes 3145732
  7.2 83.2 %reduce-scatter.3.cloned.1.call-start = ((), (), s32[]{:S(2)}) async-start(), calls=%async_computation.5 | async-start | bytes 2359296 | tf_op jit(solution)/shard_map/reduce_scatter | solution.py:21
  7.2 108.5 %copy-start.6 = (bf16[128,512]{1,0:T(8,128)(2,1)S(1)}, bf16[128,512]{1,0:T(8,128)(2,1)}, u32[]{:S(2)}) copy-start(bf16[128,512]{1,0:T(8,128)(2,1)} %param.9) | copy-start | bytes 393220
  7.9 123.8 %all-gather.4.cloned.1.call-start = ((), (), s32[]{:S(2)}) async-start(), calls=%async_computation.6 | async-start | bytes 4456448 | tf_op jit(solution)/shard_map/all_gather | solution.py:30
  92.1 87.1 %all-gather.8.cloned.1.call-start = ((), (), s32[]{:S(2)}) async-start(), calls=%async_computation.8 | async-start | bytes 6684672 | tf_op jit(solution)/shard_map/all_gather | solution.py:67
  115.7 108.7 %all-gather.6.cloned.1.call-start = ((), (), s32[]{:S(2)}) async-start(), calls=%async_computation.7 | async-start | bytes 6684672 | tf_op jit(solution)/shard_map/all_gather | solution.py:66
  157.9 243.6 %reduce-scatter.5.cloned.1.call-start = ((), (), s32[]{:S(2)}) async-start(), calls=%async_computation.9 | async-start | bytes 13369344 | tf_op jit(solution)/shard_map/reduce_scatter | solution.py:82
  224.4 7.1 %copy-start.7 = (bf16[1,768,4096]{2,1,0:T(8,128)(2,1)S(1)}, bf16[1,768,4096]{2,1,0:T(8,128)(2,1)}, u32[]{:S(2)}) copy-start(bf16[1,768,4096]{2,1,0:T(8,128)(2,1)} %all-gather.6.cloned.1.call-done) | copy-start | bytes 18874372
  224.4 7.1 %copy-start.9 = (bf16[1,4096,448]{1,2,0:T(8,128)(2,1)S(1)}, bf16[1,4096,448]{1,2,0:T(8,128)(2,1)}, u32[]{:S(2)}) copy-start(bf16[1,4096,448]{1,2,0:T(8,128)(2,1)} %param.15) | copy-start | bytes 11010052
  231.5 4.4 copy-start.8
  235.9 4.0 copy-start.10
  235.9 4.0 copy-start.3
  235.9 4.0 copy-start.2
  260.4 1.1 copy-start.11
  260.4 8.5 %slice-start = ((s8[6291456]{0:T(1024)(128)(4,1)}), s8[2097152]{0:T(1024)(128)(4,1)S(1)}, s32[]{:S(2)}) async-start(s8[6291456]{0:T(1024)(128)(4,1)} %bitcast.122), calls=%async_computation.10 | async-start | bytes 4194304
  261.5 7.4 %copy-start.4 = (bf16[768,448]{0,1:T(8,128)(2,1)S(1)}, bf16[768,448]{0,1:T(8,128)(2,1)}, u32[]{:S(2)}) copy-start(bf16[768,448]{0,1:T(8,128)(2,1)} %copy-done.3) | copy-start | bytes 2064388
  261.5 7.4 %slice-start.1 = ((s8[6291456]{0:T(1024)(128)(4,1)}), s8[4194304]{0:T(1024)(128)(4,1)S(1)}, s32[]{:S(2)}) async-start(s8[6291456]{0:T(1024)(128)(4,1)} %bitcast.122), calls=%async_computation.11 | async-start | bytes 8388608
  409.7 18.3 %all-to-all-start.2 = ((bf16[8,2,24576]{2,1,0:T(2,128)(2,1)}), bf16[8,2,24576]{2,1,0:T(2,128)(2,1)S(1)}, u32[]{:S(2)}, u32[]{:S(2)}) async-start(bf16[8,2,24576]{2,1,0:T(2,128)(2,1)} %reshape.98), calls=%async_computation.4 | async-start | bytes 1572864 | tf_op jit(solution)/shard_map/all_to_all | solution.py:89
  432.3 1.2 copy-start.5
  432.3 2.8 copy-start.1
Sparse Core Ops, SparseCore 0:
  11.7 78.6 reduce-scatter.2
  92.6 39.0 all-gather.3
  134.0 45.1 all-gather.7
  181.3 43.0 all-gather.5
  260.5 140.8 reduce-scatter.4
where the time goes:
time: 442 us
  waiting for transfers between devices  291 us (66%)
  matrix products  58.9 us (13%)
  blocking collectives  38.5 us (9%)
  local copies, waits for them, and re-layouts  19.8 us (4%)
  between operations  14.1 us (3%)
  other arithmetic  13 us (3%)
  starting transfers between devices  6.8 us (2%)
    reduce_scatter x1, waiting for transfers between devices, shards(): lax.psum_scatter(jnp.concatenate([output_term, input_term], axis=1).astyp...  128 us
    reduce_scatter x1, waiting for transfers between devices, shards(): lax.psum_scatter(branch_wo[0].astype(jnp.float32).astype(jnp.bfloat16), '...  82.4 us
    all_gather x1, waiting for transfers between devices, shards(): lax.all_gather(got_rows, 'dp', axis=1, tiled=True)  38.3 us
    all_to_all x1, blocking collectives, shards(): lax.all_to_all(send_rows, 'branch', split_axis=0, concat_axis=2, tiled=True)  21.2 us
    all_gather x1, waiting for transfers between devices, shards(): lax.all_gather(got_grads, 'dp', axis=1, tiled=True)  21.1 us
    all_to_all x1, blocking collectives, shards(): lax.all_to_all(send_grads, 'branch', split_axis=0, concat_axis=2, tiled=T...  17.3 us
    all_gather x1, waiting for transfers between devices, shards(): lax.all_gather(mean_block, 'dp', axis=0, tiled=True)  15.9 us
  transfers between devices with their start and end apart: 6, of which 6 were waited for; matrix products, arithmetic and copies ran while one was open for 9% of the time, Pallas kernels for 0%

commit v1 on v0

--- a/solution.py
+++ b/solution.py
@@ -18,19 +18,6 @@
     rows_tok, width = hidden_in.shape
     model_width = context.shape[1]
     capacity = 3 * rows_tok // n_branch
-    summed = lax.psum_scatter(
-        branch_wo[0].astype(jnp.float32).astype(jnp.bfloat16),
-        "branch",
-        scatter_dimension=1,
-        tiled=True,
-    ).astype(jnp.float32)
-    mean_block = (summed / n_branch).astype(jnp.bfloat16)
-    attended = jnp.dot(
-        context,
-        lax.all_gather(mean_block, "dp", axis=0, tiled=True),
-        preferred_element_type=jnp.float32,
-    )
-    hidden = (hidden_in.astype(jnp.float32) + attended).astype(jnp.bfloat16)
     flat_ids = expert_ids.reshape(-1)
     labels = jnp.arange(n_branch, dtype=jnp.int32)
     onehot = (flat_ids[:, None] == labels[None, :]).astype(jnp.int32)
@@ -41,31 +28,40 @@
     )
     share = gate_num.astype(jnp.float32)
     share = share / jnp.sum(share, axis=1, keepdims=True)
-    doubled = jnp.repeat(hidden, 2, axis=0)
     weighted = (
         share.reshape(-1)[:, None] * jnp.repeat(cotangent.astype(jnp.float32), 2, axis=0)
     ).astype(jnp.bfloat16)
-    send_rows = (
-        jnp.dot(placing, doubled, preferred_element_type=jnp.float32)
+    send_grads = (
+        jnp.dot(placing, weighted, preferred_element_type=jnp.float32)
         .astype(jnp.bfloat16)
         .reshape(n_branch, capacity, width)
     )
-    send_grads = (
-        jnp.dot(placing, weighted, preferred_element_type=jnp.float32)
+    got_grads = lax.all_to_all(send_grads, "branch", split_axis=0, concat_axis=2, tiled=True)
+    all_grads = lax.all_gather(got_grads, "dp", axis=1, tiled=True)
+    got_grads, wo_local = lax.optimization_barrier((got_grads, branch_wo[0]))
+    pieces = lax.all_to_all(wo_local, "branch", split_axis=1, concat_axis=0, tiled=True)
+    summed = jnp.sum(
+        pieces.reshape(n_branch, -1, width).astype(jnp.float32), axis=0
+    )
+    mean_block = (summed / n_branch).astype(jnp.bfloat16)
+    mean_block, all_grads = lax.optimization_barrier((mean_block, all_grads))
+    attended = jnp.dot(
+        context,
+        lax.all_gather(mean_block, "dp", axis=0, tiled=True),
+        preferred_element_type=jnp.float32,
+    )
+    hidden = (hidden_in.astype(jnp.float32) + attended).astype(jnp.bfloat16)
+    doubled = jnp.repeat(hidden, 2, axis=0)
+    send_rows = (
+        jnp.dot(placing, doubled, preferred_element_type=jnp.float32)
         .astype(jnp.bfloat16)
         .reshape(n_branch, capacity, width)
     )
     weight_gate = w_gate[0]
     weight_up = w_up[0]
     weight_down = w_down[0]
-    got_rows, got_grads = (
-        lax.all_to_all(send_rows, "branch", split_axis=0, concat_axis=2, tiled=True),
-        lax.all_to_all(send_grads, "branch", split_axis=0, concat_axis=2, tiled=True),
-    )
-    all_rows, all_grads = (
-        lax.all_gather(got_rows, "dp", axis=1, tiled=True),
-        lax.all_gather(got_grads, "dp", axis=1, tiled=True),
-    )
+    got_rows = lax.all_to_all(send_rows, "branch", split_axis=0, concat_axis=2, tiled=True)
+    all_rows = lax.all_gather(got_rows, "dp", axis=1, tiled=True)
     rows_two = all_rows[0]
     grads_two = all_grads[0]
     gate_pre = jnp.dot(rows_two, weight_gate, preferred_element_type=jnp.float32)

time: 442 us -> 413 us (0.934)
  waiting for transfers between devices: 291 us -> 205 us
  blocking collectives: 38.5 us -> 87 us
  local copies, waits for them, and re-layouts: 19.8 us -> 26.2 us
    reduce_scatter x1 -> x0, waiting for transfers between devices: 82.4 us -> none  [shards(): lax.psum_scatter(branch_wo[0].astype(jnp.float32).astype(jnp.bfloat16), '...]
    all_to_all x0 -> x1, blocking collectives: none -> 53.2 us  [shards(): lax.all_to_all(wo_local, 'branch', split_axis=1, concat_axis=0, tiled=True)]
    all_gather x2, waiting for transfers between devices: 59.4 us -> 32.3 us  [the longest x1 30.7 us: shards(): all_rows = lax.all_gather(got_rows, 'dp', axis=1, tiled=True)]
    all_gather x1, waiting for transfers between devices: 15.9 us -> 40.3 us  [shards(): lax.all_gather(mean_block, 'dp', axis=0, tiled=True)]
    unnamed x34 -> x33, local copies, waits for them, and re-layouts: 8.76 us -> 12.3 us
  transfers between devices with their start and end apart: 6 -> 5, of which waited for: 6 -> 5; matrix products, arithmetic and copies ran while one was open for 9% -> 9% of each run, Pallas kernels for 0% -> 0%
where the time goes in v1:
time: 413 us; the launch traced here: 412 us
  waiting for transfers between devices  205 us (50%)
  blocking collectives  87 us (21%)
  matrix products  58.4 us (14%)
  local copies, waits for them, and re-layouts  26.2 us (6%)
  other arithmetic  14.5 us (4%)
  between operations  14.1 us (3%)
  starting transfers between devices  6.74 us (2%)
    reduce_scatter x1, waiting for transfers between devices, shards(): lax.psum_scatter(jnp.concatenate([output_term, input_term], axis=1).astyp...  128 us
    all_to_all x1, blocking collectives, shards(): lax.all_to_all(wo_local, 'branch', split_axis=1, concat_axis=0, tiled=True)  53.2 us
    all_gather x1, waiting for transfers between devices, shards(): lax.all_gather(mean_block, 'dp', axis=0, tiled=True)  40.3 us
    all_gather x1, waiting for transfers between devices, shards(): all_rows = lax.all_gather(got_rows, 'dp', axis=1, tiled=True)  30.7 us
    all_to_all x1, blocking collectives, shards(): lax.all_to_all(send_grads, 'branch', split_axis=0, concat_axis=2, tiled=T...  17 us
    all_to_all x1, blocking collectives, shards(): lax.all_to_all(send_rows, 'branch', split_axis=0, concat_axis=2, tiled=True)  16.8 us
    unnamed x33, local copies, waits for them, and re-layouts  12.3 us
    concatenate x1, other arithmetic, shards(): jnp.concatenate([output_term, input_term], axis=1).astype(jnp.bfloat16)  10.4 us
  transfers between devices with their start and end apart: 5, of which 5 were waited for; matrix products, arithmetic and copies ran while one was open for 9% of the time, Pallas kernels for 0%

profile of v1, /device:TPU:0, one launch (start us, length us, event | category | flops | bytes accessed | tf_op | source)
XLA Modules:
  0.0 411.9 jit_solution(10386298555089873201)
XLA Ops:
  7.2 0.9 copy.55
  11.0 1.0 broadcast_in_dim.20
  12.7 17.0 %all_to_all.64 = bf16[8,48,512]{2,1,0:T(8,128)(2,1)S(1)} all-to-all(bf16[8,48,512]{2,1,0:T(8,128)(2,1)S(1)} %bitcast.118), channel_id=1, replica_groups=mesh['branch'=8,'dp'=16] {'branch'}, dimensions={0} | all-to-all | bytes 786432 | tf_op jit(solution)/shard_map/all_to_all | solution.py:39
  29.7 0.8 copy.74
  30.6 4.1 copy.59
  34.7 2.9 copy.60
  37.6 53.2 %all_to_all.65 = bf16[256,8,512]{2,0,1:T(8,128)(2,1)S(1)} all-to-all(bf16[256,8,512]{2,0,1:T(8,128)(2,1)S(1)} %copy.60), channel_id=1, replica_groups=mesh['branch'=8,'dp'=16] {'branch'}, dimensions={1} | all-to-all | bytes 4194304 | tf_op jit(solution)/shard_map/all_to_all | solution.py:42
  91.8 1.6 all-gather.4.cloned.1.call-done
  93.6 40.3 %all-gather.6.cloned.1.call-done = bf16[4096,512]{1,0:T(8,128)(2,1)} async-done(((bf16[256,512]{1,0:T(8,128)(2,1)}), bf16[4096,512]{1,0:T(8,128)(2,1)}) %all-gather.6.cloned.1.call-update) | async-done | bytes 4194320 | tf_op jit(solution)/shard_map/all_gather | solution.py:50
  133.9 3.5 fusion.39
  138.0 16.8 %all_to_all.66 = bf16[8,48,512]{2,1,0:T(8,128)(2,1)S(1)} all-to-all(bf16[8,48,512]{2,1,0:T(8,128)(2,1)S(1)} %bitcast.120), channel_id=1, replica_groups=mesh['branch'=8,'dp'=16] {'branch'}, dimensions={0} | all-to-all | bytes 786432 | tf_op jit(solution)/shard_map/all_to_all | solution.py:63
  154.8 0.8 copy.75
  155.9 8.0 %fusion.2 = f32[768,448]{0,1:T(8,128)} fusion(bf16[1,768,4096]{2,1,0:T(8,128)(2,1)} %all-gather.4.cloned.1.call-done, bf16[1,448,4096]{2,1,0:T(8,128)(2,1)} %param.16), kind=kOutput, calls=%fused_computation.5 | convolution fusion | flops 2818572288 | bytes 11337728 | tf_op jit(solution)/shard_map/rd,fd->rf/dot_general | solution.py:69
  163.8 30.7 %all-gather.8.cloned.1.call-done = bf16[1,768,4096]{2,1,0:T(8,128)(2,1)} async-done(((bf16[1,48,4096]{2,1,0:T(8,128)(2,1)}), bf16[1,768,4096]{2,1,0:T(8,128)(2,1)}) %all-gather.8.cloned.1.call-update) | async-done | bytes 6291472 | tf_op jit(solution)/shard_map/all_gather | solution.py:64
  194.6 7.0 %fusion.10 = f32[768,448]{0,1:T(8,128)S(1)} fusion(bf16[1,768,4096]{2,1,0:T(8,128)(2,1)} %all-gather.8.cloned.1.call-done, bf16[1,4096,448]{1,2,0:T(8,128)(2,1)} %param.14), kind=kOutput, calls=%fused_computation.13 | convolution fusion | flops 2818572288 | bytes 11337728 | tf_op jit(solution)/shard_map/dot_general | solution.py:67
  201.7 3.6 multiply_convert_fusion.2
  205.3 5.7 %convolution_convert_fusion = bf16[768,4096]{1,0:T(8,128)(2,1)} fusion(bf16[768,448]{0,1:T(8,128)(2,1)S(1)} %get-tuple-element.36, bf16[1,448,4096]{2,1,0:T(8,128)(2,1)S(1)} %copy-done.6), kind=kOutput, calls=%fused_computation.2 | convolution fusion | flops 2821718016 | bytes 10649600 | tf_op jit(solution)/shard_map/dot_general | solution.py:74
  211.0 3.5 fusion.34
  214.5 5.7 %add_convert_fusion = bf16[768,4096]{1,0:T(8,128)(2,1)} fusion(f32[768,4096]{1,0:T(8,128)S(1)} %fusion.34, bf16[768,448]{0,1:T(8,128)(2,1)S(1)} %get-tuple-element.38, bf16[1,4096,448]{1,2,0:T(8,128)(2,1)S(1)} %copy-done.7), kind=kOutput, calls=%fused_computation.1 | convolution fusion | flops 2824863744 | bytes 23232512 | tf_op jit(solution)/shard_map/rf,df->rd/dot_general | solution.py:77
  220.2 10.4 %pad_maximum_fusion = bf16[768,8192]{1,0:T(8,128)(2,1)} fusion(bf16[768,4096]{1,0:T(8,128)(2,1)} %add_convert_fusion, bf16[768,4096]{1,0:T(8,128)(2,1)} %convolution_convert_fusion), kind=kLoop, calls=%fused_computation | loop fusion | flops 25165824 | bytes 25165824 | tf_op jit(solution)/shard_map/concatenate | solution.py:79
  230.9 8.0 %fusion.21 = bf16[1,448,4096]{2,1,0:T(8,128)(2,1)} fusion(bf16[768,448]{0,1:T(8,128)(2,1)} %copy-done.9, bf16[1,768,4096]{2,1,0:T(8,128)(2,1)} %all-gather.4.cloned.1.call-done), kind=kOutput, calls=%fused_computation.18 | convolution fusion | flops 2820407296 | bytes 10649600 | tf_op jit(solution)/shard_map/rf,rd->fd/dot_general | solution.py:73
  238.9 4.4 %fusion.24 = bf16[1,4096,448]{1,2,0:T(8,128)(2,1)} fusion(bf16[768,448]{0,1:T(8,128)(2,1)S(1)} %get-tuple-element.37, bf16[1,768,4096]{2,1,0:T(8,128)(2,1)S(1)} %bitcast.124), kind=kOutput, calls=%fused_computation.19 | convolution fusion | flops 2820407296 | bytes 10649600 | tf_op jit(solution)/shard_map/rd,rf->df/dot_general | solution.py:71
  243.3 128.2 %reduce-scatter.2.cloned.1.call-done = bf16[48,8192]{1,0:T(8,128)(2,1)} async-done(((bf16[768,8192]{1,0:T(8,128)(2,1)}), bf16[48,8192]{1,0:T(8,128)(2,1)}) %reduce-scatter.2.cloned.1.call-update) | async-done | bytes 786448 | tf_op jit(solution)/shard_map/reduce_scatter | solution.py:78
  371.6 2.6 reshape.98
  374.1 1.7 copy.63
  375.8 4.2 %reshape.103 = bf16[8,2,24576]{2,1,0:T(2,128)(2,1)} reshape(bf16[4096,1,2,48]{3,2,1,0:T(2,128)(2,1)S(1)} %bitcast.109) | data formatting | bytes 1572864
  380.1 6.4 %all-to-all-start.3 = ((bf16[8,2,24576]{2,1,0:T(2,128)(2,1)}), bf16[8,2,24576]{2,1,0:T(2,128)(2,1)S(1)}, u32[]{:S(2)}, u32[]{:S(2)}) async-start(bf16[8,2,24576]{2,1,0:T(2,128)(2,1)} %reshape.103), calls=%async_computation.4 | async-start | bytes 1572864 | tf_op jit(solution)/shard_map/all_to_all | solution.py:85
  386.5 7.9 %fusion.27 = bf16[1,4096,448]{1,2,0:T(8,128)(2,1)} fusion(bf16[768,448]{0,1:T(8,128)(2,1)} %copy-done.8, bf16[1,768,4096]{2,1,0:T(8,128)(2,1)} %all-gather.8.cloned.1.call-done), kind=kOutput, calls=%fused_computation.20 | convolution fusion | flops 2820407296 | bytes 10649600 | tf_op jit(solution)/shard_map/rd,rf->df/dot_general | solution.py:72
  394.4 4.0 all-to-all-done.3
  398.3 2.1 reshape.104
  400.5 1.3 copy.73
  401.8 0.8 copy.65
  (68 shorter events, 8.7 us)
Async XLA Ops:
  7.2 126.7 %copy-start = (bf16[128,4096]{1,0:T(8,128)(2,1)S(1)}, bf16[128,4096]{1,0:T(8,128)(2,1)}, u32[]{:S(2)}) copy-start(bf16[128,4096]{1,0:T(8,128)(2,1)} %param.10) | copy-start | bytes 3145732
  7.2 86.3 %all-gather.4.cloned.1.call-start = ((), (), s32[]{:S(2)}) async-start(), calls=%async_computation.5 | async-start | bytes 6684672 | tf_op jit(solution)/shard_map/all_gather | solution.py:40
  30.5 103.4 %all-gather.6.cloned.1.call-start = ((), (), s32[]{:S(2)}) async-start(), calls=%async_computation.6 | async-start | bytes 4456448 | tf_op jit(solution)/shard_map/all_gather | solution.py:50
  37.5 56.0 %copy-start.4 = (bf16[128,512]{1,0:T(8,128)(2,1)S(1)}, bf16[128,512]{1,0:T(8,128)(2,1)}, u32[]{:S(2)}) copy-start(bf16[128,512]{1,0:T(8,128)(2,1)} %param.9) | copy-start | bytes 393220
  93.5 101.1 %all-gather.8.cloned.1.call-start = ((), (), s32[]{:S(2)}) async-start(), calls=%async_computation.7 | async-start | bytes 6684672 | tf_op jit(solution)/shard_map/all_gather | solution.py:64
  155.6 215.9 %reduce-scatter.2.cloned.1.call-start = ((), (), s32[]{:S(2)}) async-start(), calls=%async_computation.8 | async-start | bytes 13369344 | tf_op jit(solution)/shard_map/reduce_scatter | solution.py:78
  194.6 7.1 %copy-start.5 = (bf16[1,768,4096]{2,1,0:T(8,128)(2,1)S(1)}, bf16[1,768,4096]{2,1,0:T(8,128)(2,1)}, u32[]{:S(2)}) copy-start(bf16[1,768,4096]{2,1,0:T(8,128)(2,1)} %all-gather.8.cloned.1.call-done) | copy-start | bytes 18874372
  194.6 7.1 %copy-start.7 = (bf16[1,4096,448]{1,2,0:T(8,128)(2,1)S(1)}, bf16[1,4096,448]{1,2,0:T(8,128)(2,1)}, u32[]{:S(2)}) copy-start(bf16[1,4096,448]{1,2,0:T(8,128)(2,1)} %param.15) | copy-start | bytes 11010052
  194.6 7.1 %copy-start.10 = (f32[768,448]{0,1:T(8,128)S(1)}, f32[768,448]{0,1:T(8,128)}, u32[]{:S(2)}) copy-start(f32[768,448]{0,1:T(8,128)} %fusion.2) | copy-start | bytes 4128772
  201.7 3.6 copy-start.6
  205.3 5.7 %copy-start.9 = (bf16[768,448]{0,1:T(8,128)(2,1)}, bf16[768,448]{0,1:T(8,128)(2,1)S(1)}, u32[]{:S(2)}) copy-start(bf16[768,448]{0,1:T(8,128)(2,1)S(1)} %get-tuple-element.36) | copy-start | bytes 2064388
  205.3 9.2 %copy-start.8 = (bf16[768,448]{0,1:T(8,128)(2,1)}, bf16[768,448]{0,1:T(8,128)(2,1)S(1)}, u32[]{:S(2)}) copy-start(bf16[768,448]{0,1:T(8,128)(2,1)S(1)} %get-tuple-element.38) | copy-start | bytes 2064388
  205.3 5.7 %copy-start.2 = (bf16[1,4096,448]{1,2,0:T(8,128)(2,1)S(1)}, bf16[1,4096,448]{1,2,0:T(8,128)(2,1)}, u32[]{:S(2)}) copy-start(bf16[1,4096,448]{1,2,0:T(8,128)(2,1)} %param.14) | copy-start | bytes 11010052
  230.6 8.3 %slice-start = ((s8[6291456]{0:T(1024)(128)(4,1)}), s8[2097152]{0:T(1024)(128)(4,1)S(1)}, s32[]{:S(2)}) async-start(s8[6291456]{0:T(1024)(128)(4,1)} %bitcast.123), calls=%async_computation.9 | async-start | bytes 4194304
  230.8 8.0 %slice-start.1 = ((s8[6291456]{0:T(1024)(128)(4,1)}), s8[4194304]{0:T(1024)(128)(4,1)S(1)}, s32[]{:S(2)}) async-start(s8[6291456]{0:T(1024)(128)(4,1)} %bitcast.123), calls=%async_computation.10 | async-start | bytes 8388608
  380.1 18.3 %all-to-all-start.3 = ((bf16[8,2,24576]{2,1,0:T(2,128)(2,1)}), bf16[8,2,24576]{2,1,0:T(2,128)(2,1)S(1)}, u32[]{:S(2)}, u32[]{:S(2)}) async-start(bf16[8,2,24576]{2,1,0:T(2,128)(2,1)} %reshape.103), calls=%async_computation.4 | async-start | bytes 1572864 | tf_op jit(solution)/shard_map/all_to_all | solution.py:85
  402.6 1.2 copy-start.3
  402.6 2.8 copy-start.1
Sparse Core Ops, SparseCore 0:
  30.7 62.7 all-gather.3
  95.7 38.1 all-gather.5
  155.8 38.7 all-gather.7
  230.7 140.8 reduce-scatter.1

commit v2 on v1

--- a/solution.py
+++ b/solution.py
@@ -1,7 +1,9 @@
 import jax
 import jax.numpy as jnp
 from jax import lax
-from jax.sharding import PartitionSpec as P
+from jax.sharding import Mesh, PartitionSpec as P
+
+DP = ("dpo", "core")
 
 
 def swiglu_parts(gate_pre, up_pre, d_act):
@@ -37,7 +39,7 @@
         .reshape(n_branch, capacity, width)
     )
     got_grads = lax.all_to_all(send_grads, "branch", split_axis=0, concat_axis=2, tiled=True)
-    all_grads = lax.all_gather(got_grads, "dp", axis=1, tiled=True)
+    all_grads = lax.all_gather(got_grads, DP, axis=1, tiled=True)
     got_grads, wo_local = lax.optimization_barrier((got_grads, branch_wo[0]))
     pieces = lax.all_to_all(wo_local, "branch", split_axis=1, concat_axis=0, tiled=True)
     summed = jnp.sum(
@@ -47,7 +49,7 @@
     mean_block, all_grads = lax.optimization_barrier((mean_block, all_grads))
     attended = jnp.dot(
         context,
-        lax.all_gather(mean_block, "dp", axis=0, tiled=True),
+        lax.all_gather(mean_block, DP, axis=0, tiled=True),
         preferred_element_type=jnp.float32,
     )
     hidden = (hidden_in.astype(jnp.float32) + attended).astype(jnp.bfloat16)
@@ -61,7 +63,7 @@
     weight_up = w_up[0]
     weight_down = w_down[0]
     got_rows = lax.all_to_all(send_rows, "branch", split_axis=0, concat_axis=2, tiled=True)
-    all_rows = lax.all_gather(got_rows, "dp", axis=1, tiled=True)
+    all_rows = lax.all_gather(got_rows, DP, axis=1, tiled=True)
     rows_two = all_rows[0]
     grads_two = all_grads[0]
     gate_pre = jnp.dot(rows_two, weight_gate, preferred_element_type=jnp.float32)
@@ -75,9 +77,16 @@
     input_term = jnp.einsum(
         "rf,df->rd", d_gate, weight_gate, preferred_element_type=jnp.float32
     ) + jnp.einsum("rf,df->rd", d_up, weight_up, preferred_element_type=jnp.float32)
+    both = jnp.concatenate([output_term, input_term], axis=1).astype(jnp.bfloat16)
+    both = both.reshape(-1, 2, capacity, 2 * model_width)
+    core = lax.axis_index("core")
+    mine = lax.dynamic_index_in_dim(both, core, axis=1, keepdims=False)
+    other = lax.dynamic_index_in_dim(both, 1 - core, axis=1, keepdims=False)
+    partner = lax.ppermute(other, "core", perm=[(0, 1), (1, 0)])
+    paired = (mine.astype(jnp.float32) + partner.astype(jnp.float32)).astype(jnp.bfloat16)
     folded = lax.psum_scatter(
-        jnp.concatenate([output_term, input_term], axis=1).astype(jnp.bfloat16),
-        "dp",
+        paired.reshape(-1, 2 * model_width),
+        "dpo",
         scatter_dimension=0,
         tiled=True,
     )
@@ -106,26 +115,30 @@
 
 
 def solution(mesh):
+    split = Mesh(
+        mesh.devices.reshape(mesh.shape["branch"], mesh.shape["dp"] // 2, 2),
+        ("branch", "dpo", "core"),
+    )
     return jax.shard_map(
         shards,
-        mesh=mesh,
+        mesh=split,
         in_specs=(
-            P("dp", "branch"),
-            P("dp", None),
-            P("branch", "dp", None),
-            P("dp", None),
-            P("dp", None),
-            P("branch", None, "dp"),
-            P("branch", None, "dp"),
-            P("branch", "dp", None),
-            P("dp", "branch"),
+            P(DP, "branch"),
+            P(DP, None),
+            P("branch", DP, None),
+            P(DP, None),
+            P(DP, None),
+            P("branch", None, DP),
+            P("branch", None, DP),
+            P("branch", DP, None),
+            P(DP, "branch"),
         ),
         out_specs=(
-            P("dp", "branch"),
-            P("dp", "branch"),
-            P("branch", None, "dp"),
-            P("branch", None, "dp"),
-            P("branch", "dp", None),
+            P(DP, "branch"),
+            P(DP, "branch"),
+            P("branch", None, DP),
+            P("branch", None, DP),
+            P("branch", DP, None),
         ),
         check_vma=False,
     )

time: 413 us -> 431 us (1.044)
  waiting for transfers between devices: 205 us -> 211 us
  matrix products: 58.4 us -> 63.7 us
    reduce_scatter x1, waiting for transfers between devices: 128 us -> 115 us  [shards(): lax.psum_scatter(paired.reshape(-1, 2 * model_width), 'dpo', scatter_dime...]
    concatenate x1 -> x0, other arithmetic: 10.4 us -> none  [shards(): jnp.concatenate([output_term, input_term], axis=1).astype(jnp.bfloat16)]
    ppermute x0 -> x1, waiting for transfers between devices: none -> 10.3 us  [shards(): partner = lax.ppermute(other, 'core', perm=[(0, 1), (1, 0)])]
    convert_element_type x0 -> x1, other arithmetic: none -> 8.37 us  [shards(): (mine.astype(jnp.float32) + partner.astype(jnp.float32)).astype(jnp.bfloa...]
    all_gather x3, waiting for transfers between devices: 72.6 us -> 80.6 us  [the longest x1 40.3 us: shards(): lax.all_gather(mean_block, DP, axis=0, tiled=True)]
    squeeze x0 -> x1, other arithmetic: none -> 5.25 us  [shards(): other = lax.dynamic_index_in_dim(both, 1 - core, axis=1, keepdims=False)]
    dot_general x1, matrix products: 7.98 us -> 3.55 us  [shards(): jnp.einsum('rd,fd->rf', grads_two, weight_down, preferred_element_type=jn...]
  transfers between devices with their start and end apart: 5 -> 6, of which waited for: 5 -> 6; matrix products, arithmetic and copies ran while one was open for 9% -> 7% of each run, Pallas kernels for 0% -> 0%
where the time goes in v2:
time: 431 us; the launch traced here: 430 us
  waiting for transfers between devices  211 us (49%)
  blocking collectives  86.9 us (20%)
  matrix products  63.7 us (15%)
  local copies, waits for them, and re-layouts  29.1 us (7%)
  other arithmetic  17.7 us (4%)
  between operations  14.1 us (3%)
  starting transfers between devices  6.97 us (2%)
    reduce_scatter x1, waiting for transfers between devices, shards(): lax.psum_scatter(paired.reshape(-1, 2 * model_width), 'dpo', scatter_dime...  115 us
    all_to_all x1, blocking collectives, shards(): lax.all_to_all(wo_local, 'branch', split_axis=1, concat_axis=0, tiled=True)  53.1 us
    all_gather x1, waiting for transfers between devices, shards(): lax.all_gather(mean_block, DP, axis=0, tiled=True)  40.3 us
    all_gather x1, waiting for transfers between devices, shards(): all_rows = lax.all_gather(got_rows, DP, axis=1, tiled=True)  38.6 us
    all_to_all x1, blocking collectives, shards(): lax.all_to_all(send_grads, 'branch', split_axis=0, concat_axis=2, tiled=T...  17 us
    all_to_all x1, blocking collectives, shards(): lax.all_to_all(send_rows, 'branch', split_axis=0, concat_axis=2, tiled=True)  16.8 us
    unnamed x33, local copies, waits for them, and re-layouts  12.1 us
    ppermute x1, waiting for transfers between devices, shards(): partner = lax.ppermute(other, 'core', perm=[(0, 1), (1, 0)])  10.3 us
  transfers between devices with their start and end apart: 6, of which 6 were waited for; matrix products, arithmetic and copies ran while one was open for 7% of the time, Pallas kernels for 0%

profile of v2, /device:TPU:0, one launch (start us, length us, event | category | flops | bytes accessed | tf_op | source)
XLA Modules:
  0.0 429.8 jit_solution(18144140094379031427)
XLA Ops:
  11.0 1.0 broadcast_in_dim.20
  12.7 17.0 %all_to_all.64 = bf16[8,48,512]{2,1,0:T(8,128)(2,1)S(1)} all-to-all(bf16[8,48,512]{2,1,0:T(8,128)(2,1)S(1)} %bitcast.135), channel_id=1, replica_groups=mesh['branch'=8,'dpo'=8,'core'=2] {'branch'}, dimensions={0} | all-to-all | bytes 786432 | tf_op jit(solution)/shard_map/all_to_all | solution.py:41
  30.6 4.1 copy.92
  34.7 2.9 copy.93
  37.6 53.1 %all_to_all.65 = bf16[256,8,512]{2,0,1:T(8,128)(2,1)S(1)} all-to-all(bf16[256,8,512]{2,0,1:T(8,128)(2,1)S(1)} %copy.93), channel_id=1, replica_groups=mesh['branch'=8,'dpo'=8,'core'=2] {'branch'}, dimensions={1} | all-to-all | bytes 4194304 | tf_op jit(solution)/shard_map/all_to_all | solution.py:44
  91.7 1.7 all-gather.4.cloned.1.call-done
  93.6 40.3 %all-gather.6.cloned.1.call-done = bf16[4096,512]{1,0:T(8,128)(2,1)} async-done(((bf16[256,512]{1,0:T(8,128)(2,1)}), bf16[4096,512]{1,0:T(8,128)(2,1)}) %all-gather.6.cloned.1.call-update) | async-done | bytes 4194320 | tf_op jit(solution)/shard_map/all_gather | solution.py:52
  133.9 3.5 fusion.44
  138.0 16.8 %all_to_all.66 = bf16[8,48,512]{2,1,0:T(8,128)(2,1)S(1)} all-to-all(bf16[8,48,512]{2,1,0:T(8,128)(2,1)S(1)} %bitcast.137), channel_id=1, replica_groups=mesh['branch'=8,'dpo'=8,'core'=2] {'branch'}, dimensions={0} | all-to-all | bytes 786432 | tf_op jit(solution)/shard_map/all_to_all | solution.py:65
  155.9 38.6 %all-gather.8.cloned.1.call-done = bf16[1,768,4096]{2,1,0:T(8,128)(2,1)} async-done(((bf16[1,48,4096]{2,1,0:T(8,128)(2,1)}), bf16[1,768,4096]{2,1,0:T(8,128)(2,1)}) %all-gather.8.cloned.1.call-update) | async-done | bytes 6291472 | tf_op jit(solution)/shard_map/all_gather | solution.py:66
  194.5 7.0 %fusion.13 = f32[768,448]{0,1:T(8,128)S(1)} fusion(bf16[1,768,4096]{2,1,0:T(8,128)(2,1)} %all-gather.8.cloned.1.call-done, bf16[1,4096,448]{1,2,0:T(8,128)(2,1)} %param.15), kind=kOutput, calls=%fused_computation.20 | convolution fusion | flops 2818572288 | bytes 11337728 | tf_op jit(solution)/shard_map/dot_general | solution.py:70
  201.6 3.1 fusion.15
  204.7 3.6 multiply_convert_fusion
  208.6 6.0 %convolution_convert_fusion = bf16[8,2,48,4096]{3,2,1,0:T(8,128)(2,1)S(1)} fusion(bf16[8,2,48,448]{3,2,1,0:T(8,128)(2,1)S(1)} %bitcast.139, bf16[1,448,4096]{2,1,0:T(8,128)(2,1)} %param.16), kind=kOutput, calls=%fused_computation.7 | convolution fusion | flops 2821718016 | bytes 10649600 | tf_op jit(solution)/shard_map/dot_general | solution.py:76
  214.6 6.4 %fusion.39 = f32[768,4096]{1,0:T(8,128)} fusion(bf16[768,448]{0,1:T(8,128)(2,1)S(1)} %get-tuple-element.47, bf16[1,4096,448]{1,2,0:T(8,128)(2,1)S(1)} %copy-done.4), kind=kOutput, calls=%fused_computation.35 | convolution fusion | flops 2818572288 | bytes 16941056 | tf_op jit(solution)/shard_map/rf,df->rd/dot_general | solution.py:77
  221.1 9.2 %add_convert_fusion = bf16[768,4096]{1,0:T(8,128)(2,1)} fusion(f32[768,4096]{1,0:T(8,128)} %fusion.39, bf16[768,448]{0,1:T(8,128)(2,1)S(1)} %get-tuple-element.46, bf16[1,4096,448]{1,2,0:T(8,128)(2,1)S(1)} %copy-done.10), kind=kOutput, calls=%fused_computation.6 | convolution fusion | flops 2824863744 | bytes 23232512 | tf_op jit(solution)/shard_map/rf,df->rd/dot_general | solution.py:79
  230.3 5.2 %fusion.2 = bf16[8,48,8192]{2,1,0:T(8,128)(2,1)} fusion(s32[]{:T(128)S(6)} %select_n.8, bf16[8,2,48,4096]{3,2,1,0:T(8,128)(2,1)S(1)} %convolution_convert_fusion, bf16[8,2,48,4096]{3,2,1,0:T(8,128)(2,1)} %bitcast.124), kind=kLoop, calls=%fused_computation.9 | loop fusion | flops 12582912 | bytes 18874372 | tf_op jit(solution)/shard_map/jit(dynamic_index_in_dim)/squeeze | solution.py:84
  235.8 10.3 %collective-permute-done = bf16[8,48,8192]{2,1,0:T(8,128)(2,1)} collective-permute-done((bf16[8,48,8192]{2,1,0:T(8,128)(2,1)}, bf16[8,48,8192]{2,1,0:T(8,128)(2,1)}, u32[]{:S(2)}, u32[]{:S(2)}) %collective-permute-start) | collective-permute-done | bytes 6291488 | tf_op jit(solution)/shard_map/ppermute | solution.py:85
  246.0 8.4 %fusion = bf16[8,48,8192]{2,1,0:T(8,128)(2,1)} fusion(bf16[8,48,8192]{2,1,0:T(8,128)(2,1)} %collective-permute-done, s32[]{:T(128)S(6)} %select_n.7, bf16[8,2,48,4096]{3,2,1,0:T(8,128)(2,1)} %copy-done.2, bf16[8,2,48,4096]{3,2,1,0:T(8,128)(2,1)} %bitcast.125), kind=kLoop, calls=%fused_computation.5 | loop fusion | flops 25165824 | bytes 25165828 | tf_op jit(solution)/shard_map/convert_element_type | solution.py:86
  255.4 7.2 %fusion.26 = bf16[1,448,4096]{2,1,0:T(8,128)(2,1)} fusion(bf16[768,448]{0,1:T(8,128)(2,1)S(1)} %get-tuple-element.48, bf16[1,768,4096]{2,1,0:T(8,128)(2,1)} %all-gather.4.cloned.1.call-done), kind=kOutput, calls=%fused_computation.27 | convolution fusion | flops 2820407296 | bytes 10649600 | tf_op jit(solution)/shard_map/rf,rd->fd/dot_general | solution.py:75
  262.6 7.8 %fusion.32 = bf16[1,4096,448]{1,2,0:T(8,128)(2,1)} fusion(bf16[768,448]{0,1:T(8,128)(2,1)S(1)} %get-tuple-element.46, bf16[1,768,4096]{2,1,0:T(8,128)(2,1)} %all-gather.8.cloned.1.call-done), kind=kOutput, calls=%fused_computation.29 | convolution fusion | flops 2820407296 | bytes 10649600 | tf_op jit(solution)/shard_map/rd,rf->df/dot_general | solution.py:74
  270.4 115.2 %reduce-scatter.2.cloned.1.call-done = bf16[48,8192]{1,0:T(8,128)(2,1)} async-done(((bf16[384,8192]{1,0:T(8,128)(2,1)}), bf16[48,8192]{1,0:T(8,128)(2,1)}) %reduce-scatter.2.cloned.1.call-update) | async-done | bytes 786448 | tf_op jit(solution)/shard_map/reduce_scatter | solution.py:87
  385.6 2.6 reshape.109
  388.2 1.7 copy.97
  389.9 4.0 reshape.116
  393.9 6.4 %all-to-all-start.3 = ((bf16[8,2,24576]{2,1,0:T(2,128)(2,1)}), bf16[8,2,24576]{2,1,0:T(2,128)(2,1)S(1)}, u32[]{:S(2)}, u32[]{:S(2)}) async-start(bf16[8,2,24576]{2,1,0:T(2,128)(2,1)} %reshape.116), calls=%async_computation.4 | async-start | bytes 1572864 | tf_op jit(solution)/shard_map/all_to_all | solution.py:94
  400.3 7.9 %fusion.29 = bf16[1,4096,448]{1,2,0:T(8,128)(2,1)} fusion(bf16[768,448]{0,1:T(8,128)(2,1)} %copy-done.5, bf16[1,768,4096]{2,1,0:T(8,128)(2,1)} %all-gather.8.cloned.1.call-done), kind=kOutput, calls=%fused_computation.28 | convolution fusion | flops 2820407296 | bytes 10649600 | tf_op jit(solution)/shard_map/rd,rf->df/dot_general | solution.py:73
  408.2 5.1 %all-to-all-done.3 = bf16[8,2,24576]{2,1,0:T(2,128)(2,1)S(1)} async-done(((bf16[8,2,24576]{2,1,0:T(2,128)(2,1)}), bf16[8,2,24576]{2,1,0:T(2,128)(2,1)S(1)}, u32[]{:S(2)}, u32[]{:S(2)}) %all-to-all-start.3) | async-done | bytes 786464 | tf_op jit(solution)/shard_map/all_to_all | solution.py:94
  413.3 2.1 reshape.117
  415.4 2.2 copy.108
  417.6 1.9 copy.99
  420.1 1.4 fusion.47
  (72 shorter events, 11.9 us)
Async XLA Ops:
  7.2 126.7 %copy-start = (bf16[128,4096]{1,0:T(8,128)(2,1)S(1)}, bf16[128,4096]{1,0:T(8,128)(2,1)}, u32[]{:S(2)}) copy-start(bf16[128,4096]{1,0:T(8,128)(2,1)} %param.10) | copy-start | bytes 3145732
  7.2 86.3 %all-gather.4.cloned.1.call-start = ((), (), s32[]{:S(2)}) async-start(), calls=%async_computation.5 | async-start | bytes 6684672 | tf_op jit(solution)/shard_map/all_gather | solution.py:42
  30.5 103.4 %all-gather.6.cloned.1.call-start = ((), (), s32[]{:S(2)}) async-start(), calls=%async_computation.6 | async-start | bytes 4456448 | tf_op jit(solution)/shard_map/all_gather | solution.py:52
  34.7 58.8 %copy-start.7 = (bf16[128,512]{1,0:T(8,128)(2,1)S(1)}, bf16[128,512]{1,0:T(8,128)(2,1)}, u32[]{:S(2)}) copy-start(bf16[128,512]{1,0:T(8,128)(2,1)} %param.9) | copy-start | bytes 393220
  93.5 101.0 %all-gather.8.cloned.1.call-start = ((), (), s32[]{:S(2)}) async-start(), calls=%async_computation.7 | async-start | bytes 6684672 | tf_op jit(solution)/shard_map/all_gather | solution.py:66
  155.6 230.0 %reduce-scatter.2.cloned.1.call-start = ((), (), s32[]{:S(2)}) async-start(), calls=%async_computation.8 | async-start | bytes 7077888 | tf_op jit(solution)/shard_map/reduce_scatter | solution.py:87
  194.5 7.0 %copy-start.3 = (bf16[1,4096,448]{1,2,0:T(8,128)(2,1)S(1)}, bf16[1,4096,448]{1,2,0:T(8,128)(2,1)}, u32[]{:S(2)}) copy-start(bf16[1,4096,448]{1,2,0:T(8,128)(2,1)} %param.14) | copy-start | bytes 11010052
  194.5 7.1 %copy-start.8 = (bf16[1,768,4096]{2,1,0:T(8,128)(2,1)S(1)}, bf16[1,768,4096]{2,1,0:T(8,128)(2,1)}, u32[]{:S(2)}) copy-start(bf16[1,768,4096]{2,1,0:T(8,128)(2,1)} %all-gather.8.cloned.1.call-done) | copy-start | bytes 18874372
  194.5 10.2 %slice-start = ((s8[6291456]{0:T(1024)(128)(4,1)}), s8[4194304]{0:T(1024)(128)(4,1)S(1)}, s32[]{:S(2)}) async-start(s8[6291456]{0:T(1024)(128)(4,1)} %bitcast.141), calls=%async_computation.9 | async-start | bytes 8388608
  201.6 3.1 slice-start.1
  201.6 3.1 copy-start.9
  208.3 6.4 %copy-start.5 = (bf16[768,448]{0,1:T(8,128)(2,1)}, bf16[768,448]{0,1:T(8,128)(2,1)S(1)}, u32[]{:S(2)}) copy-start(bf16[768,448]{0,1:T(8,128)(2,1)S(1)} %get-tuple-element.47) | copy-start | bytes 2064388
  208.5 6.1 %copy-start.4 = (bf16[1,4096,448]{1,2,0:T(8,128)(2,1)S(1)}, bf16[1,4096,448]{1,2,0:T(8,128)(2,1)}, u32[]{:S(2)}) copy-start(bf16[1,4096,448]{1,2,0:T(8,128)(2,1)} %param.14) | copy-start | bytes 11010052
  214.6 15.7 %copy-start.2 = (bf16[8,2,48,4096]{3,2,1,0:T(8,128)(2,1)}, bf16[8,2,48,4096]{3,2,1,0:T(8,128)(2,1)S(1)}, u32[]{:S(2)}) copy-start(bf16[8,2,48,4096]{3,2,1,0:T(8,128)(2,1)S(1)} %convolution_convert_fusion) | copy-start | bytes 18874372
  214.6 6.5 %copy-start.10 = (bf16[1,4096,448]{1,2,0:T(8,128)(2,1)S(1)}, bf16[1,4096,448]{1,2,0:T(8,128)(2,1)}, u32[]{:S(2)}) copy-start(bf16[1,4096,448]{1,2,0:T(8,128)(2,1)} %param.15) | copy-start | bytes 11010052
  235.5 10.5 %collective-permute-start = (bf16[8,48,8192]{2,1,0:T(8,128)(2,1)}, bf16[8,48,8192]{2,1,0:T(8,128)(2,1)}, u32[]{:S(2)}, u32[]{:S(2)}) collective-permute-start(bf16[8,48,8192]{2,1,0:T(8,128)(2,1)} %fusion.2), channel_id=1, source_target_pairs={{0,1},{1,0},{2,3},{3,2},{4,5},{5,4},{6,7},{7,6},{8,9},{9,8},{10,11... | collective-permute-start | bytes 18874376 | tf_op jit(solution)/shard_map/ppermute | solution.py:85
  393.9 19.4 %all-to-all-start.3 = ((bf16[8,2,24576]{2,1,0:T(2,128)(2,1)}), bf16[8,2,24576]{2,1,0:T(2,128)(2,1)S(1)}, u32[]{:S(2)}, u32[]{:S(2)}) async-start(bf16[8,2,24576]{2,1,0:T(2,128)(2,1)} %reshape.116), calls=%async_computation.4 | async-start | bytes 1572864 | tf_op jit(solution)/shard_map/all_to_all | solution.py:94
  408.2 13.5 %copy-start.6 = (bf16[128,512]{1,0:T(8,128)(2,1)S(1)}, bf16[128,512]{1,0:T(8,128)(2,1)}, u32[]{:S(2)}) copy-start(bf16[128,512]{1,0:T(8,128)(2,1)} %param.17) | copy-start | bytes 393220
  415.4 7.9 %copy-start.1 = (bf16[128,4096]{1,0:T(8,128)(2,1)S(1)}, bf16[128,4096]{1,0:T(8,128)(2,1)}, u32[]{:S(2)}) copy-start(bf16[128,4096]{1,0:T(8,128)(2,1)} %param.10) | copy-start | bytes 3145732
Sparse Core Ops, SparseCore 0:
  30.7 62.7 all-gather.3
  95.7 38.1 all-gather.5
  155.8 38.6 all-gather.7
  254.6 131.0 reduce-scatter.1

commit v3 on v1

--- a/solution.py
+++ b/solution.py
@@ -75,13 +75,13 @@
     input_term = jnp.einsum(
         "rf,df->rd", d_gate, weight_gate, preferred_element_type=jnp.float32
     ) + jnp.einsum("rf,df->rd", d_up, weight_up, preferred_element_type=jnp.float32)
-    folded = lax.psum_scatter(
-        jnp.concatenate([output_term, input_term], axis=1).astype(jnp.bfloat16),
-        "dp",
-        scatter_dimension=0,
-        tiled=True,
+    out_part = lax.psum_scatter(
+        output_term.astype(jnp.bfloat16), "dp", scatter_dimension=0, tiled=True
     )
-    packed = folded.reshape(1, capacity, 2, model_width)
+    in_part = lax.psum_scatter(
+        input_term.astype(jnp.bfloat16), "dp", scatter_dimension=0, tiled=True
+    )
+    packed = jnp.stack([out_part, in_part], axis=1)[None]
     returned = lax.all_to_all(packed, "branch", split_axis=3, concat_axis=0, tiled=True)
     picked = jnp.einsum(
         "sr,sc->rc",

time: 413 us -> 412 us (level)
  other arithmetic: 14.5 us -> 5.3 us
  waiting for transfers between devices: 205 us -> 211 us
    concatenate x1 -> x0, other arithmetic: 10.4 us -> none  [shards(): jnp.concatenate([output_term, input_term], axis=1).astype(jnp.bfloat16)]
    reduce_scatter x1 -> x2, waiting for transfers between devices: 128 us -> 135 us  [the longest x1 79.7 us: shards(): lax.psum_scatter(input_term.astype(jnp.bfloat16), 'dp', scatter_dimension...]
    reshape x2 -> x0, local copies, waits for them, and re-layouts: 4.27 us -> none  [shards(): packed = folded.reshape(1, capacity, 2, model_width)]
  transfers between devices with their start and end apart: 5 -> 6, of which waited for: 5 -> 6; matrix products, arithmetic and copies ran while one was open for 9% -> 12% of each run, Pallas kernels for 0% -> 0%
where the time goes in v3:
time: 412 us
  waiting for transfers between devices  211 us (51%)
  blocking collectives  87 us (21%)
  matrix products  60.3 us (15%)
  local copies, waits for them, and re-layouts  27.1 us (7%)
  between operations  14.1 us (3%)
  starting transfers between devices  6.89 us (2%)
  other arithmetic  5.3 us (1%)
    reduce_scatter x1, waiting for transfers between devices, shards(): lax.psum_scatter(input_term.astype(jnp.bfloat16), 'dp', scatter_dimension...  79.7 us
    reduce_scatter x1, waiting for transfers between devices, shards(): lax.psum_scatter(output_term.astype(jnp.bfloat16), 'dp', scatter_dimensio...  55.1 us
    all_to_all x1, blocking collectives, shards(): lax.all_to_all(wo_local, 'branch', split_axis=1, concat_axis=0, tiled=True)  53.2 us
    all_gather x1, waiting for transfers between devices, shards(): lax.all_gather(mean_block, 'dp', axis=0, tiled=True)  40.3 us
    all_gather x1, waiting for transfers between devices, shards(): all_rows = lax.all_gather(got_rows, 'dp', axis=1, tiled=True)  30.7 us
    all_to_all x1, blocking collectives, shards(): lax.all_to_all(send_grads, 'branch', split_axis=0, concat_axis=2, tiled=T...  17 us
    all_to_all x1, blocking collectives, shards(): lax.all_to_all(send_rows, 'branch', split_axis=0, concat_axis=2, tiled=True)  16.8 us
    unnamed x33, local copies, waits for them, and re-layouts  13.3 us
  transfers between devices with their start and end apart: 6, of which 6 were waited for; matrix products, arithmetic and copies ran while one was open for 12% of the time, Pallas kernels for 0%

profile of v3, /device:TPU:0, one launch (start us, length us, event | category | flops | bytes accessed | tf_op | source)
XLA Modules:
  0.0 411.6 jit_solution(16934307124928452939)
XLA Ops:
  7.2 0.9 copy.42
  11.0 1.0 broadcast_in_dim.23
  12.7 17.0 %all_to_all.64 = bf16[8,48,512]{2,1,0:T(8,128)(2,1)S(1)} all-to-all(bf16[8,48,512]{2,1,0:T(8,128)(2,1)S(1)} %bitcast.121), channel_id=1, replica_groups=mesh['branch'=8,'dp'=16] {'branch'}, dimensions={0} | all-to-all | bytes 786432 | tf_op jit(solution)/shard_map/all_to_all | solution.py:39
  29.7 0.8 copy.59
  30.6 4.1 copy.46
  34.7 2.9 copy.47
  37.6 53.2 %all_to_all.65 = bf16[256,8,512]{2,0,1:T(8,128)(2,1)S(1)} all-to-all(bf16[256,8,512]{2,0,1:T(8,128)(2,1)S(1)} %copy.47), channel_id=1, replica_groups=mesh['branch'=8,'dp'=16] {'branch'}, dimensions={1} | all-to-all | bytes 4194304 | tf_op jit(solution)/shard_map/all_to_all | solution.py:42
  91.8 1.6 all-gather.4.cloned.1.call-done
  93.6 40.3 %all-gather.6.cloned.1.call-done = bf16[4096,512]{1,0:T(8,128)(2,1)} async-done(((bf16[256,512]{1,0:T(8,128)(2,1)}), bf16[4096,512]{1,0:T(8,128)(2,1)}) %all-gather.6.cloned.1.call-update) | async-done | bytes 4194320 | tf_op jit(solution)/shard_map/all_gather | solution.py:50
  133.9 3.5 fusion.39
  138.0 16.8 %all_to_all.66 = bf16[8,48,512]{2,1,0:T(8,128)(2,1)S(1)} all-to-all(bf16[8,48,512]{2,1,0:T(8,128)(2,1)S(1)} %bitcast.123), channel_id=1, replica_groups=mesh['branch'=8,'dp'=16] {'branch'}, dimensions={0} | all-to-all | bytes 786432 | tf_op jit(solution)/shard_map/all_to_all | solution.py:63
  154.8 0.8 copy.60
  155.9 8.0 %fusion.2 = f32[768,448]{0,1:T(8,128)} fusion(bf16[1,768,4096]{2,1,0:T(8,128)(2,1)} %all-gather.4.cloned.1.call-done, bf16[1,448,4096]{2,1,0:T(8,128)(2,1)} %param.16), kind=kOutput, calls=%fused_computation.4 | convolution fusion | flops 2818572288 | bytes 11337728 | tf_op jit(solution)/shard_map/rd,fd->rf/dot_general | solution.py:69
  163.8 30.7 %all-gather.8.cloned.1.call-done = bf16[1,768,4096]{2,1,0:T(8,128)(2,1)} async-done(((bf16[1,48,4096]{2,1,0:T(8,128)(2,1)}), bf16[1,768,4096]{2,1,0:T(8,128)(2,1)}) %all-gather.8.cloned.1.call-update) | async-done | bytes 6291472 | tf_op jit(solution)/shard_map/all_gather | solution.py:64
  194.6 7.0 %fusion.10 = f32[768,448]{0,1:T(8,128)S(1)} fusion(bf16[1,768,4096]{2,1,0:T(8,128)(2,1)} %all-gather.8.cloned.1.call-done, bf16[1,4096,448]{1,2,0:T(8,128)(2,1)} %param.14), kind=kOutput, calls=%fused_computation.12 | convolution fusion | flops 2818572288 | bytes 11337728 | tf_op jit(solution)/shard_map/dot_general | solution.py:67
  201.7 3.6 multiply_convert_fusion.2
  205.3 5.4 %convolution_convert_fusion = bf16[768,4096]{1,0:T(8,128)(2,1)} fusion(bf16[768,448]{0,1:T(8,128)(2,1)S(1)} %get-tuple-element.31, bf16[1,448,4096]{2,1,0:T(8,128)(2,1)S(1)} %copy-done.5), kind=kOutput, calls=%fused_computation.1 | convolution fusion | flops 2821718016 | bytes 10649600 | tf_op jit(solution)/shard_map/dot_general | solution.py:74
  211.0 5.7 %fusion.34 = f32[768,4096]{1,0:T(8,128)S(1)} fusion(bf16[768,448]{0,1:T(8,128)(2,1)S(1)} %get-tuple-element.32, bf16[1,4096,448]{1,2,0:T(8,128)(2,1)} %param.14), kind=kOutput, calls=%fused_computation.25 | convolution fusion | flops 2818572288 | bytes 16941056 | tf_op jit(solution)/shard_map/rf,df->rd/dot_general | solution.py:75
  216.7 5.7 %add_convert_fusion = bf16[768,4096]{1,0:T(8,128)(2,1)} fusion(f32[768,4096]{1,0:T(8,128)S(1)} %fusion.34, bf16[768,448]{0,1:T(8,128)(2,1)S(1)} %get-tuple-element.33, bf16[1,4096,448]{1,2,0:T(8,128)(2,1)S(1)} %copy-done.7), kind=kOutput, calls=%fused_computation | convolution fusion | flops 2824863744 | bytes 23232512 | tf_op jit(solution)/shard_map/rf,df->rd/dot_general | solution.py:77
  222.7 8.0 %fusion.21 = bf16[1,448,4096]{2,1,0:T(8,128)(2,1)} fusion(bf16[768,448]{0,1:T(8,128)(2,1)} %copy-done.9, bf16[1,768,4096]{2,1,0:T(8,128)(2,1)} %all-gather.4.cloned.1.call-done), kind=kOutput, calls=%fused_computation.17 | convolution fusion | flops 2820407296 | bytes 10649600 | tf_op jit(solution)/shard_map/rf,rd->fd/dot_general | solution.py:73
  230.7 4.4 %fusion.24 = bf16[1,4096,448]{1,2,0:T(8,128)(2,1)} fusion(bf16[768,448]{0,1:T(8,128)(2,1)S(1)} %get-tuple-element.32, bf16[1,768,4096]{2,1,0:T(8,128)(2,1)S(1)} %bitcast.129), kind=kOutput, calls=%fused_computation.18 | convolution fusion | flops 2820407296 | bytes 10649600 | tf_op jit(solution)/shard_map/rd,rf->df/dot_general | solution.py:71
  235.2 55.1 %reduce-scatter.3.cloned.1.call-done = bf16[48,4096]{1,0:T(8,128)(2,1)} async-done(((bf16[768,4096]{1,0:T(8,128)(2,1)}), bf16[48,4096]{1,0:T(8,128)(2,1)}) %reduce-scatter.3.cloned.1.call-update) | async-done | bytes 393232 | tf_op jit(solution)/shard_map/reduce_scatter | solution.py:78
  290.3 79.7 %reduce-scatter.5.cloned.1.call-done = bf16[48,4096]{1,0:T(8,128)(2,1)} async-done(((bf16[768,4096]{1,0:T(8,128)(2,1)}), bf16[48,4096]{1,0:T(8,128)(2,1)}) %reduce-scatter.5.cloned.1.call-update) | async-done | bytes 393232 | tf_op jit(solution)/shard_map/reduce_scatter | solution.py:81
  370.0 1.2 maximum_bitcast_fusion
  371.2 2.8 copy.50
  374.0 4.0 reshape.99
  378.0 6.3 %all-to-all-start.3 = ((bf16[8,2,24576]{2,1,0:T(2,128)(2,1)}), bf16[8,2,24576]{2,1,0:T(2,128)(2,1)S(1)}, u32[]{:S(2)}, u32[]{:S(2)}) async-start(bf16[8,2,24576]{2,1,0:T(2,128)(2,1)} %reshape.99), calls=%async_computation.5 | async-start | bytes 1572864 | tf_op jit(solution)/shard_map/all_to_all | solution.py:85
  384.3 7.9 %fusion.27 = bf16[1,4096,448]{1,2,0:T(8,128)(2,1)} fusion(bf16[768,448]{0,1:T(8,128)(2,1)} %copy-done.8, bf16[1,768,4096]{2,1,0:T(8,128)(2,1)} %all-gather.8.cloned.1.call-done), kind=kOutput, calls=%fused_computation.19 | convolution fusion | flops 2820407296 | bytes 10649600 | tf_op jit(solution)/shard_map/rd,rf->df/dot_general | solution.py:72
  392.1 3.4 all-to-all-done.3
  395.5 2.1 reshape.100
  397.6 3.5 copy.51
  401.1 1.4 copy.61
  (69 shorter events, 8.9 us)
Async XLA Ops:
  7.2 126.7 %copy-start = (bf16[128,4096]{1,0:T(8,128)(2,1)S(1)}, bf16[128,4096]{1,0:T(8,128)(2,1)}, u32[]{:S(2)}) copy-start(bf16[128,4096]{1,0:T(8,128)(2,1)} %param.10) | copy-start | bytes 3145732
  7.2 86.3 %all-gather.4.cloned.1.call-start = ((), (), s32[]{:S(2)}) async-start(), calls=%async_computation.6 | async-start | bytes 6684672 | tf_op jit(solution)/shard_map/all_gather | solution.py:40
  30.5 103.4 %all-gather.6.cloned.1.call-start = ((), (), s32[]{:S(2)}) async-start(), calls=%async_computation.7 | async-start | bytes 4456448 | tf_op jit(solution)/shard_map/all_gather | solution.py:50
  37.5 56.0 %copy-start.3 = (bf16[128,512]{1,0:T(8,128)(2,1)S(1)}, bf16[128,512]{1,0:T(8,128)(2,1)}, u32[]{:S(2)}) copy-start(bf16[128,512]{1,0:T(8,128)(2,1)} %param.9) | copy-start | bytes 393220
  93.5 101.1 %all-gather.8.cloned.1.call-start = ((), (), s32[]{:S(2)}) async-start(), calls=%async_computation.8 | async-start | bytes 6684672 | tf_op jit(solution)/shard_map/all_gather | solution.py:64
  155.6 134.6 %reduce-scatter.3.cloned.1.call-start = ((), (), s32[]{:S(2)}) async-start(), calls=%async_computation.9 | async-start | bytes 6684672 | tf_op jit(solution)/shard_map/reduce_scatter | solution.py:78
  194.6 7.1 %copy-start.4 = (bf16[1,768,4096]{2,1,0:T(8,128)(2,1)S(1)}, bf16[1,768,4096]{2,1,0:T(8,128)(2,1)}, u32[]{:S(2)}) copy-start(bf16[1,768,4096]{2,1,0:T(8,128)(2,1)} %all-gather.8.cloned.1.call-done) | copy-start | bytes 18874372
  194.6 7.1 %copy-start.6 = (bf16[1,4096,448]{1,2,0:T(8,128)(2,1)S(1)}, bf16[1,4096,448]{1,2,0:T(8,128)(2,1)}, u32[]{:S(2)}) copy-start(bf16[1,4096,448]{1,2,0:T(8,128)(2,1)} %param.15) | copy-start | bytes 11010052
  194.6 7.1 %copy-start.10 = (f32[768,448]{0,1:T(8,128)S(1)}, f32[768,448]{0,1:T(8,128)}, u32[]{:S(2)}) copy-start(f32[768,448]{0,1:T(8,128)} %fusion.2) | copy-start | bytes 4128772
  201.7 3.6 copy-start.5
  205.2 5.4 %copy-start.9 = (bf16[768,448]{0,1:T(8,128)(2,1)}, bf16[768,448]{0,1:T(8,128)(2,1)S(1)}, u32[]{:S(2)}) copy-start(bf16[768,448]{0,1:T(8,128)(2,1)S(1)} %get-tuple-element.31) | copy-start | bytes 2064388
  205.3 11.5 %copy-start.8 = (bf16[768,448]{0,1:T(8,128)(2,1)}, bf16[768,448]{0,1:T(8,128)(2,1)S(1)}, u32[]{:S(2)}) copy-start(bf16[768,448]{0,1:T(8,128)(2,1)S(1)} %get-tuple-element.33) | copy-start | bytes 2064388
  210.7 159.3 %reduce-scatter.5.cloned.1.call-start = ((), (), s32[]{:S(2)}) async-start(), calls=%async_computation.10 | async-start | bytes 6684672 | tf_op jit(solution)/shard_map/reduce_scatter | solution.py:81
  211.0 5.7 %copy-start.7 = (bf16[1,4096,448]{1,2,0:T(8,128)(2,1)S(1)}, bf16[1,4096,448]{1,2,0:T(8,128)(2,1)}, u32[]{:S(2)}) copy-start(bf16[1,4096,448]{1,2,0:T(8,128)(2,1)} %param.15) | copy-start | bytes 11010052
  222.4 8.3 %slice-start = ((s8[6291456]{0:T(1024)(128)(4,1)}), s8[2097152]{0:T(1024)(128)(4,1)S(1)}, s32[]{:S(2)}) async-start(s8[6291456]{0:T(1024)(128)(4,1)} %bitcast.128), calls=%async_computation.11 | async-start | bytes 4194304
  222.7 8.0 %slice-start.1 = ((s8[6291456]{0:T(1024)(128)(4,1)}), s8[4194304]{0:T(1024)(128)(4,1)S(1)}, s32[]{:S(2)}) async-start(s8[6291456]{0:T(1024)(128)(4,1)} %bitcast.128), calls=%async_computation.12 | async-start | bytes 8388608
  378.0 17.5 %all-to-all-start.3 = ((bf16[8,2,24576]{2,1,0:T(2,128)(2,1)}), bf16[8,2,24576]{2,1,0:T(2,128)(2,1)S(1)}, u32[]{:S(2)}, u32[]{:S(2)}) async-start(bf16[8,2,24576]{2,1,0:T(2,128)(2,1)} %reshape.99), calls=%async_computation.5 | async-start | bytes 1572864 | tf_op jit(solution)/shard_map/all_to_all | solution.py:85
  401.1 2.4 copy-start.2
  401.1 4.0 copy-start.1
Sparse Core Ops, SparseCore 0:
  30.7 62.7 all-gather.3
  95.7 38.1 all-gather.5
  155.8 38.7 all-gather.7
  210.8 79.4 reduce-scatter.2
  292.5 77.4 reduce-scatter.4

commit v4 on v1

--- a/solution.py
+++ b/solution.py
@@ -39,10 +39,12 @@
     got_grads = lax.all_to_all(send_grads, "branch", split_axis=0, concat_axis=2, tiled=True)
     all_grads = lax.all_gather(got_grads, "dp", axis=1, tiled=True)
     got_grads, wo_local = lax.optimization_barrier((got_grads, branch_wo[0]))
-    pieces = lax.all_to_all(wo_local, "branch", split_axis=1, concat_axis=0, tiled=True)
-    summed = jnp.sum(
-        pieces.reshape(n_branch, -1, width).astype(jnp.float32), axis=0
-    )
+    me = lax.axis_index("branch")
+    summed = lax.dynamic_slice_in_dim(wo_local, me * width, width, axis=1).astype(jnp.float32)
+    for k in range(1, n_branch):
+        piece = lax.dynamic_slice_in_dim(wo_local, ((me + k) % n_branch) * width, width, axis=1)
+        got = lax.ppermute(piece, "branch", perm=[(i, (i + k) % n_branch) for i in range(n_branch)])
+        summed = summed + got.astype(jnp.float32)
     mean_block = (summed / n_branch).astype(jnp.bfloat16)
     mean_block, all_grads = lax.optimization_barrier((mean_block, all_grads))
     attended = jnp.dot(

time: 413 us -> 413 us (level)
  blocking collectives: 87 us -> 33.8 us
  waiting for transfers between devices: 205 us -> 258 us
  starting transfers between devices: 6.74 us -> 16.2 us
    all_to_all x1 -> x0, blocking collectives: 53.2 us -> none  [shards(): lax.all_to_all(wo_local, 'branch', split_axis=1, concat_axis=0, tiled=True)]
    ppermute x0 -> x7, waiting for transfers between devices: none -> 43.2 us  [shards(): lax.ppermute(piece, 'branch', perm=[(i, (i + k) % n_branch) for i in rang...]
    ppermute x0 -> x7, starting transfers between devices: none -> 9.47 us  [shards(): lax.ppermute(piece, 'branch', perm=[(i, (i + k) % n_branch) for i in rang...]
    all_gather x1, waiting for transfers between devices: 30.7 us -> 38.6 us  [shards(): all_rows = lax.all_gather(got_rows, 'dp', axis=1, tiled=True)]
    unnamed x33 -> x36, local copies, waits for them, and re-layouts: 12.3 us -> 8.83 us
  transfers between devices with their start and end apart: 5 -> 12, of which waited for: 5 -> 11; matrix products, arithmetic and copies ran while one was open for 9% -> 6% of each run, Pallas kernels for 0% -> 0%
where the time goes in v4:
time: 413 us
  waiting for transfers between devices  258 us (62%)
  matrix products  55 us (13%)
  blocking collectives  33.8 us (8%)
  local copies, waits for them, and re-layouts  22.3 us (5%)
  starting transfers between devices  16.2 us (4%)
  between operations  14.2 us (3%)
  other arithmetic  13.2 us (3%)
    reduce_scatter x1, waiting for transfers between devices, shards(): lax.psum_scatter(jnp.concatenate([output_term, input_term], axis=1).astyp...  128 us
    ppermute x7, waiting for transfers between devices, shards(): lax.ppermute(piece, 'branch', perm=[(i, (i + k) % n_branch) for i in rang...  43.2 us
    all_gather x1, waiting for transfers between devices, shards(): lax.all_gather(mean_block, 'dp', axis=0, tiled=True)  40.3 us
    all_gather x1, waiting for transfers between devices, shards(): all_rows = lax.all_gather(got_rows, 'dp', axis=1, tiled=True)  38.6 us
    all_to_all x1, blocking collectives, shards(): lax.all_to_all(send_grads, 'branch', split_axis=0, concat_axis=2, tiled=T...  17 us
    all_to_all x1, blocking collectives, shards(): lax.all_to_all(send_rows, 'branch', split_axis=0, concat_axis=2, tiled=True)  16.8 us
    ppermute x7, starting transfers between devices, shards(): lax.ppermute(piece, 'branch', perm=[(i, (i + k) % n_branch) for i in rang...  9.47 us
    unnamed x36, local copies, waits for them, and re-layouts  8.83 us
  transfers between devices with their start and end apart: 12, of which 11 were waited for; matrix products, arithmetic and copies ran while one was open for 6% of the time, Pallas kernels for 0%

profile of v4, /device:TPU:0, one launch (start us, length us, event | category | flops | bytes accessed | tf_op | source)
XLA Modules:
  0.0 412.8 jit_solution(2891218296397292972)
XLA Ops:
  12.7 17.0 %all_to_all.51 = bf16[8,48,512]{2,1,0:T(8,128)(2,1)S(1)} all-to-all(bf16[8,48,512]{2,1,0:T(8,128)(2,1)S(1)} %bitcast.118), channel_id=1, replica_groups=mesh['branch'=8,'dp'=16] {'branch'}, dimensions={0} | all-to-all | bytes 786432 | tf_op jit(solution)/shard_map/all_to_all | solution.py:39
  30.7 2.4 constant_dynamic-slice_fusion.6
  33.6 5.1 %collective-permute-start.6 = (bf16[256,512]{1,0:T(8,128)(2,1)S(1)}, bf16[256,512]{1,0:T(8,128)(2,1)S(1)}, u32[]{:S(2)}, u32[]{:S(2)}) collective-permute-start(bf16[256,512]{1,0:T(8,128)(2,1)S(1)} %get-tuple-element.35), channel_id=1, source_target_pairs={{0,112},{16,0},{32,16},{48,32},{64,48},{80,64},{96,80},{112,96},{1... | collective-permute-start | bytes 786440 | tf_op jit(solution)/shard_map/ppermute | solution.py:46
  39.7 2.8 collective-permute-start.3
  43.5 7.6 %collective-permute-done.6 = bf16[256,512]{1,0:T(8,128)(2,1)S(1)} collective-permute-done((bf16[256,512]{1,0:T(8,128)(2,1)S(1)}, bf16[256,512]{1,0:T(8,128)(2,1)S(1)}, u32[]{:S(2)}, u32[]{:S(2)}) %collective-permute-start.6) | collective-permute-done | bytes 262176 | tf_op jit(solution)/shard_map/ppermute | solution.py:46
  51.1 11.3 %collective-permute-done.5 = bf16[256,512]{1,0:T(8,128)(2,1)S(1)} collective-permute-done((bf16[256,512]{1,0:T(8,128)(2,1)}, bf16[256,512]{1,0:T(8,128)(2,1)S(1)}, u32[]{:S(2)}, u32[]{:S(2)}) %collective-permute-start.5) | collective-permute-done | bytes 262176 | tf_op jit(solution)/shard_map/ppermute | solution.py:46
  62.4 11.2 %collective-permute-done.4 = bf16[256,512]{1,0:T(8,128)(2,1)S(1)} collective-permute-done((bf16[256,512]{1,0:T(8,128)(2,1)}, bf16[256,512]{1,0:T(8,128)(2,1)S(1)}, u32[]{:S(2)}, u32[]{:S(2)}) %collective-permute-start.4) | collective-permute-done | bytes 262176 | tf_op jit(solution)/shard_map/ppermute | solution.py:46
  73.6 9.6 %collective-permute-done.3 = bf16[256,512]{1,0:T(8,128)(2,1)S(1)} collective-permute-done((bf16[256,512]{1,0:T(8,128)(2,1)}, bf16[256,512]{1,0:T(8,128)(2,1)S(1)}, u32[]{:S(2)}, u32[]{:S(2)}) %collective-permute-start.3) | collective-permute-done | bytes 262176 | tf_op jit(solution)/shard_map/ppermute | solution.py:46
  83.3 2.5 collective-permute-done.1
  85.8 1.9 multiply_convert_fusion.3
  87.7 3.8 all-gather.4.cloned.1.call-done
  91.7 40.3 %all-gather.6.cloned.1.call-done = bf16[4096,512]{1,0:T(8,128)(2,1)} async-done(((bf16[256,512]{1,0:T(8,128)(2,1)}), bf16[4096,512]{1,0:T(8,128)(2,1)}) %all-gather.6.cloned.1.call-update) | async-done | bytes 4194320 | tf_op jit(solution)/shard_map/all_gather | solution.py:52
  132.0 3.5 fusion.39
  136.2 16.8 %all_to_all.52 = bf16[8,48,512]{2,1,0:T(8,128)(2,1)S(1)} all-to-all(bf16[8,48,512]{2,1,0:T(8,128)(2,1)S(1)} %bitcast.120), channel_id=1, replica_groups=mesh['branch'=8,'dp'=16] {'branch'}, dimensions={0} | all-to-all | bytes 786432 | tf_op jit(solution)/shard_map/all_to_all | solution.py:65
  154.0 38.6 %all-gather.8.cloned.1.call-done = bf16[1,768,4096]{2,1,0:T(8,128)(2,1)} async-done(((bf16[1,48,4096]{2,1,0:T(8,128)(2,1)}), bf16[1,768,4096]{2,1,0:T(8,128)(2,1)}) %all-gather.8.cloned.1.call-update) | async-done | bytes 6291472 | tf_op jit(solution)/shard_map/all_gather | solution.py:66
  192.6 7.0 %fusion.8 = f32[768,448]{0,1:T(8,128)S(1)} fusion(bf16[1,768,4096]{2,1,0:T(8,128)(2,1)} %all-gather.8.cloned.1.call-done, bf16[1,4096,448]{1,2,0:T(8,128)(2,1)} %param.15), kind=kOutput, calls=%fused_computation.11 | convolution fusion | flops 2818572288 | bytes 11337728 | tf_op jit(solution)/shard_map/dot_general | solution.py:70
  199.7 3.2 fusion.10
  203.0 4.4 %multiply_convert_fusion.2 = (bf16[768,448]{0,1:T(8,128)(2,1)S(1)}, bf16[768,448]{0,1:T(8,128)(2,1)S(1)}, bf16[768,448]{0,1:T(8,128)(2,1)}) fusion(f32[768,448]{0,1:T(8,128)S(1)} %fusion.8, f32[768,448]{0,1:T(8,128)S(1)} %fusion.10, bf16[1,448,4096]{2,1,0:T(8,128)(2,1)S(1)} %copy-done.8, bf16[1,768,4096]{2,1,0:T(8,128)(2,1)S(1)} %bitcast.124), kind=kOutput, calls=%fused_computation.30 | convolution fusion | flops 2823733248 | bytes 14778368 | tf_op jit(solution)/shard_map/rd,fd->rf/dot_general | solution.py:71
  207.4 3.7 convolution_convert_fusion
  211.1 3.5 fusion.34
  214.6 8.8 %add_convert_fusion = bf16[768,4096]{1,0:T(8,128)(2,1)} fusion(f32[768,4096]{1,0:T(8,128)S(1)} %fusion.34, bf16[768,448]{0,1:T(8,128)(2,1)} %get-tuple-element.33, bf16[1,4096,448]{1,2,0:T(8,128)(2,1)} %param.15), kind=kOutput, calls=%fused_computation.1 | convolution fusion | flops 2824863744 | bytes 23232512 | tf_op jit(solution)/shard_map/rf,df->rd/dot_general | solution.py:79
  223.4 8.2 %pad_maximum_fusion = bf16[768,8192]{1,0:T(8,128)(2,1)} fusion(bf16[768,4096]{1,0:T(8,128)(2,1)} %add_convert_fusion, bf16[768,4096]{1,0:T(8,128)(2,1)S(1)} %convolution_convert_fusion), kind=kLoop, calls=%fused_computation | loop fusion | flops 25165824 | bytes 25165824 | tf_op jit(solution)/shard_map/concatenate | solution.py:81
  232.7 7.4 %fusion.21 = bf16[1,448,4096]{2,1,0:T(8,128)(2,1)} fusion(bf16[768,448]{0,1:T(8,128)(2,1)S(1)} %copy-done.10, bf16[1,768,4096]{2,1,0:T(8,128)(2,1)} %all-gather.4.cloned.1.call-done), kind=kOutput, calls=%fused_computation.18 | convolution fusion | flops 2820407296 | bytes 10649600 | tf_op jit(solution)/shard_map/rf,rd->fd/dot_general | solution.py:75
  240.1 4.5 %fusion.24 = bf16[1,4096,448]{1,2,0:T(8,128)(2,1)} fusion(bf16[768,448]{0,1:T(8,128)(2,1)S(1)} %copy-done.4, bf16[1,768,4096]{2,1,0:T(8,128)(2,1)S(1)} %bitcast.126), kind=kOutput, calls=%fused_computation.19 | convolution fusion | flops 2820407296 | bytes 10649600 | tf_op jit(solution)/shard_map/rd,rf->df/dot_general | solution.py:73
  244.6 128.1 %reduce-scatter.2.cloned.1.call-done = bf16[48,8192]{1,0:T(8,128)(2,1)} async-done(((bf16[768,8192]{1,0:T(8,128)(2,1)}), bf16[48,8192]{1,0:T(8,128)(2,1)}) %reduce-scatter.2.cloned.1.call-update) | async-done | bytes 786448 | tf_op jit(solution)/shard_map/reduce_scatter | solution.py:80
  372.7 2.6 reshape.93
  375.3 1.7 copy.47
  377.0 4.0 reshape.98
  381.0 6.4 %all-to-all-start.2 = ((bf16[8,2,24576]{2,1,0:T(2,128)(2,1)}), bf16[8,2,24576]{2,1,0:T(2,128)(2,1)S(1)}, u32[]{:S(2)}, u32[]{:S(2)}) async-start(bf16[8,2,24576]{2,1,0:T(2,128)(2,1)} %reshape.98), calls=%async_computation.3 | async-start | bytes 1572864 | tf_op jit(solution)/shard_map/all_to_all | solution.py:87
  387.4 7.9 %fusion.27 = bf16[1,4096,448]{1,2,0:T(8,128)(2,1)} fusion(bf16[768,448]{0,1:T(8,128)(2,1)} %get-tuple-element.33, bf16[1,768,4096]{2,1,0:T(8,128)(2,1)} %all-gather.8.cloned.1.call-done), kind=kOutput, calls=%fused_computation.20 | convolution fusion | flops 2820407296 | bytes 10649600 | tf_op jit(solution)/shard_map/rd,rf->df/dot_general | solution.py:74
  395.3 4.0 all-to-all-done.2
  399.3 2.1 reshape.99
  (84 shorter events, 16.5 us)
Async XLA Ops:
  7.2 124.9 %copy-start = (bf16[128,4096]{1,0:T(8,128)(2,1)S(1)}, bf16[128,4096]{1,0:T(8,128)(2,1)}, u32[]{:S(2)}) copy-start(bf16[128,4096]{1,0:T(8,128)(2,1)} %param.10) | copy-start | bytes 3145732
  7.2 84.3 %all-gather.4.cloned.1.call-start = ((), (), s32[]{:S(2)}) async-start(), calls=%async_computation.4 | async-start | bytes 6684672 | tf_op jit(solution)/shard_map/all_gather | solution.py:40
  30.5 61.1 %copy-start.6 = (bf16[128,512]{1,0:T(8,128)(2,1)S(1)}, bf16[128,512]{1,0:T(8,128)(2,1)}, u32[]{:S(2)}) copy-start(bf16[128,512]{1,0:T(8,128)(2,1)} %param.9) | copy-start | bytes 393220
  30.5 101.5 %all-gather.6.cloned.1.call-start = ((), (), s32[]{:S(2)}) async-start(), calls=%async_computation.5 | async-start | bytes 4456448 | tf_op jit(solution)/shard_map/all_gather | solution.py:52
  33.1 10.4 %collective-permute-start = (bf16[256,512]{1,0:T(8,128)(2,1)S(1)}, bf16[256,512]{1,0:T(8,128)(2,1)S(1)}, u32[]{:S(2)}, u32[]{:S(2)}) collective-permute-start(bf16[256,512]{1,0:T(8,128)(2,1)S(1)} %get-tuple-element.34), channel_id=1, source_target_pairs={{0,16},{16,32},{32,48},{48,64},{64,80},{80,96},{96,112},{112,0},{1... | collective-permute-start | bytes 786440 | tf_op jit(solution)/shard_map/ppermute | solution.py:46
  33.6 17.4 %collective-permute-start.6 = (bf16[256,512]{1,0:T(8,128)(2,1)S(1)}, bf16[256,512]{1,0:T(8,128)(2,1)S(1)}, u32[]{:S(2)}, u32[]{:S(2)}) collective-permute-start(bf16[256,512]{1,0:T(8,128)(2,1)S(1)} %get-tuple-element.35), channel_id=1, source_target_pairs={{0,112},{16,0},{32,16},{48,32},{64,48},{80,64},{96,80},{112,96},{1... | collective-permute-start | bytes 786440 | tf_op jit(solution)/shard_map/ppermute | solution.py:46
  38.8 23.6 %collective-permute-start.5 = (bf16[256,512]{1,0:T(8,128)(2,1)}, bf16[256,512]{1,0:T(8,128)(2,1)S(1)}, u32[]{:S(2)}, u32[]{:S(2)}) collective-permute-start(bf16[256,512]{1,0:T(8,128)(2,1)} %get-tuple-element.36), channel_id=1, source_target_pairs={{0,96},{16,112},{32,0},{48,16},{64,32},{80,48},{96,64},{112,80},{1... | collective-permute-start | bytes 786440 | tf_op jit(solution)/shard_map/ppermute | solution.py:46
  38.8 34.9 %collective-permute-start.4 = (bf16[256,512]{1,0:T(8,128)(2,1)}, bf16[256,512]{1,0:T(8,128)(2,1)S(1)}, u32[]{:S(2)}, u32[]{:S(2)}) collective-permute-start(bf16[256,512]{1,0:T(8,128)(2,1)} %get-tuple-element.37), channel_id=1, source_target_pairs={{0,80},{16,96},{32,112},{48,0},{64,16},{80,32},{96,48},{112,64},{1... | collective-permute-start | bytes 786440 | tf_op jit(solution)/shard_map/ppermute | solution.py:46
  39.7 43.6 %collective-permute-start.3 = (bf16[256,512]{1,0:T(8,128)(2,1)}, bf16[256,512]{1,0:T(8,128)(2,1)S(1)}, u32[]{:S(2)}, u32[]{:S(2)}) collective-permute-start(bf16[256,512]{1,0:T(8,128)(2,1)} %get-tuple-element.38), channel_id=1, source_target_pairs={{0,64},{16,80},{32,96},{48,112},{64,0},{80,16},{96,32},{112,48},{1... | collective-permute-start | bytes 786440 | tf_op jit(solution)/shard_map/ppermute | solution.py:46
  43.5 39.8 %collective-permute-start.2 = (bf16[256,512]{1,0:T(8,128)(2,1)S(1)}, bf16[256,512]{1,0:T(8,128)(2,1)S(1)}, u32[]{:S(2)}, u32[]{:S(2)}) collective-permute-start(bf16[256,512]{1,0:T(8,128)(2,1)S(1)} %get-tuple-element.39), channel_id=1, source_target_pairs={{0,48},{16,64},{32,80},{48,96},{64,112},{80,0},{96,16},{112,32},{1... | collective-permute-start | bytes 786440 | tf_op jit(solution)/shard_map/ppermute | solution.py:46
  51.1 34.7 %collective-permute-start.1 = (bf16[256,512]{1,0:T(8,128)(2,1)S(1)}, bf16[256,512]{1,0:T(8,128)(2,1)S(1)}, u32[]{:S(2)}, u32[]{:S(2)}) collective-permute-start(bf16[256,512]{1,0:T(8,128)(2,1)S(1)} %get-tuple-element.40), channel_id=1, source_target_pairs={{0,32},{16,48},{32,64},{48,80},{64,96},{80,112},{96,0},{112,16},{1... | collective-permute-start | bytes 786440 | tf_op jit(solution)/shard_map/ppermute | solution.py:46
  91.5 101.0 %all-gather.8.cloned.1.call-start = ((), (), s32[]{:S(2)}) async-start(), calls=%async_computation.6 | async-start | bytes 6684672 | tf_op jit(solution)/shard_map/all_gather | solution.py:66
  153.7 219.0 %reduce-scatter.2.cloned.1.call-start = ((), (), s32[]{:S(2)}) async-start(), calls=%async_computation.7 | async-start | bytes 13369344 | tf_op jit(solution)/shard_map/reduce_scatter | solution.py:80
  192.6 7.1 %copy-start.2 = (bf16[1,4096,448]{1,2,0:T(8,128)(2,1)S(1)}, bf16[1,4096,448]{1,2,0:T(8,128)(2,1)}, u32[]{:S(2)}) copy-start(bf16[1,4096,448]{1,2,0:T(8,128)(2,1)} %param.14) | copy-start | bytes 11010052
  192.6 7.1 %copy-start.7 = (bf16[1,768,4096]{2,1,0:T(8,128)(2,1)S(1)}, bf16[1,768,4096]{2,1,0:T(8,128)(2,1)}, u32[]{:S(2)}) copy-start(bf16[1,768,4096]{2,1,0:T(8,128)(2,1)} %all-gather.8.cloned.1.call-done) | copy-start | bytes 18874372
  192.6 10.3 %slice-start = ((s8[6291456]{0:T(1024)(128)(4,1)}), s8[4194304]{0:T(1024)(128)(4,1)S(1)}, s32[]{:S(2)}) async-start(s8[6291456]{0:T(1024)(128)(4,1)} %bitcast.123), calls=%async_computation.8 | async-start | bytes 8388608
  199.7 3.3 slice-start.1
  199.7 3.3 copy-start.8
  207.4 3.7 copy-start.9
  207.4 3.7 copy-start.3
  231.6 1.1 copy-start.10
  231.6 8.5 %slice-start.2 = ((s8[6291456]{0:T(1024)(128)(4,1)}), s8[2097152]{0:T(1024)(128)(4,1)S(1)}, s32[]{:S(2)}) async-start(s8[6291456]{0:T(1024)(128)(4,1)} %bitcast.125), calls=%async_computation.10 | async-start | bytes 4194304
  232.7 7.4 %copy-start.4 = (bf16[768,448]{0,1:T(8,128)(2,1)S(1)}, bf16[768,448]{0,1:T(8,128)(2,1)}, u32[]{:S(2)}) copy-start(bf16[768,448]{0,1:T(8,128)(2,1)} %copy-done.3) | copy-start | bytes 2064388
  232.7 7.4 %slice-start.3 = ((s8[6291456]{0:T(1024)(128)(4,1)}), s8[4194304]{0:T(1024)(128)(4,1)S(1)}, s32[]{:S(2)}) async-start(s8[6291456]{0:T(1024)(128)(4,1)} %bitcast.125), calls=%async_computation.11 | async-start | bytes 8388608
  381.0 18.3 %all-to-all-start.2 = ((bf16[8,2,24576]{2,1,0:T(2,128)(2,1)}), bf16[8,2,24576]{2,1,0:T(2,128)(2,1)S(1)}, u32[]{:S(2)}, u32[]{:S(2)}) async-start(bf16[8,2,24576]{2,1,0:T(2,128)(2,1)} %reshape.98), calls=%async_computation.3 | async-start | bytes 1572864 | tf_op jit(solution)/shard_map/all_to_all | solution.py:87
  403.5 1.2 copy-start.5
  403.5 2.8 copy-start.1
Sparse Core Ops, SparseCore 0:
  30.7 60.8 all-gather.3
  93.8 38.1 all-gather.5
  153.9 38.6 all-gather.7
  231.8 140.8 reduce-scatter.1

commit v5 on v3

--- a/solution.py
+++ b/solution.py
@@ -75,14 +75,18 @@
     input_term = jnp.einsum(
         "rf,df->rd", d_gate, weight_gate, preferred_element_type=jnp.float32
     ) + jnp.einsum("rf,df->rd", d_up, weight_up, preferred_element_type=jnp.float32)
-    out_part = lax.psum_scatter(
-        output_term.astype(jnp.bfloat16), "dp", scatter_dimension=0, tiled=True
+    both = jnp.stack(
+        [
+            output_term.astype(jnp.bfloat16).reshape(-1, n_branch, width),
+            input_term.astype(jnp.bfloat16).reshape(-1, n_branch, width),
+        ],
+        axis=2,
     )
-    in_part = lax.psum_scatter(
-        input_term.astype(jnp.bfloat16), "dp", scatter_dimension=0, tiled=True
+    folded = lax.psum_scatter(
+        both.reshape(-1, 2 * model_width), "dp", scatter_dimension=0, tiled=True
     )
-    packed = jnp.stack([out_part, in_part], axis=1)[None]
-    returned = lax.all_to_all(packed, "branch", split_axis=3, concat_axis=0, tiled=True)
+    packed = folded.reshape(capacity, n_branch, 2 * width).transpose(1, 0, 2)
+    returned = lax.all_to_all(packed, "branch", split_axis=0, concat_axis=0, tiled=True)
     picked = jnp.einsum(
         "sr,sc->rc",
         placing,

time: 412 us -> 440 us (1.068)
  local copies, waits for them, and re-layouts: 27.1 us -> 51 us
  other arithmetic: 5.3 us -> 14.9 us
  waiting for transfers between devices: 211 us -> 205 us
    reduce_scatter x2 -> x0, waiting for transfers between devices: 135 us -> none  [the longest x1 79.7 us: shards(): lax.psum_scatter(input_term.astype(jnp.bfloat16), 'dp', scatter_dimension...]
    unnamed x5, waiting for transfers between devices: 0.08 us -> 128 us
    another operation x1 -> x3, local copies, waits for them, and re-layouts: 0.01 us -> 17.4 us  [the longest x2 17.4 us: shards(): jnp.stack([output_term.astype(jnp.bfloat16).reshape(-1, n_branch, width),...]
    unnamed x33 -> x32, local copies, waits for them, and re-layouts: 13.3 us -> 24.6 us
    another operation x2 -> x3, other arithmetic: 0.61 us -> 11.4 us  [the longest x1 10.8 us: shards(): jnp.stack([output_term.astype(jnp.bfloat16).reshape(-1, n_branch, width),...]
  transfers between devices with their start and end apart: 6 -> 5, of which waited for: 6 -> 5; matrix products, arithmetic and copies ran while one was open for 12% -> 8% of each run, Pallas kernels for 0% -> 0%
where the time goes in v5:
time: 440 us; the launch traced here: 439 us
  waiting for transfers between devices  205 us (47%)
  blocking collectives  87 us (20%)
  matrix products  60.5 us (14%)
  local copies, waits for them, and re-layouts  51 us (12%)
  other arithmetic  14.9 us (3%)
  between operations  14.1 us (3%)
  starting transfers between devices  6.74 us (2%)
    unnamed x5, waiting for transfers between devices  128 us
    all_to_all x1, blocking collectives, shards(): lax.all_to_all(wo_local, 'branch', split_axis=1, concat_axis=0, tiled=True)  53.2 us
    all_gather x1, waiting for transfers between devices, shards(): lax.all_gather(mean_block, 'dp', axis=0, tiled=True)  40.3 us
    all_gather x1, waiting for transfers between devices, shards(): all_rows = lax.all_gather(got_rows, 'dp', axis=1, tiled=True)  30.7 us
    unnamed x32, local copies, waits for them, and re-layouts  24.6 us
    another operation x2, local copies, waits for them, and re-layouts, shards(): jnp.stack([output_term.astype(jnp.bfloat16).reshape(-1, n_branch, width),...  17.4 us
    all_to_all x1, blocking collectives, shards(): lax.all_to_all(send_grads, 'branch', split_axis=0, concat_axis=2, tiled=T...  17 us
    all_to_all x1, blocking collectives, shards(): lax.all_to_all(send_rows, 'branch', split_axis=0, concat_axis=2, tiled=True)  16.8 us
  transfers between devices with their start and end apart: 5, of which 5 were waited for; matrix products, arithmetic and copies ran while one was open for 8% of the time, Pallas kernels for 0%

profile of v5, /device:TPU:0, one launch (start us, length us, event | category | flops | bytes accessed | tf_op | source)
XLA Modules:
  0.0 439.1 jit_solution(9998367080737436636)
XLA Ops:
  7.2 0.9 copy.47
  11.0 1.0 broadcast_in_dim.20
  12.7 17.0 %all_to_all.54 = bf16[8,48,512]{2,1,0:T(8,128)(2,1)S(1)} all-to-all(bf16[8,48,512]{2,1,0:T(8,128)(2,1)S(1)} %bitcast.119), channel_id=1, replica_groups=mesh['branch'=8,'dp'=16] {'branch'}, dimensions={0} | all-to-all | bytes 786432 | tf_op jit(solution)/shard_map/all_to_all | solution.py:39
  29.7 0.8 copy.72
  30.6 4.1 copy.51
  34.7 2.9 copy.52
  37.6 53.2 %all_to_all.55 = bf16[256,8,512]{2,0,1:T(8,128)(2,1)S(1)} all-to-all(bf16[256,8,512]{2,0,1:T(8,128)(2,1)S(1)} %copy.52), channel_id=1, replica_groups=mesh['branch'=8,'dp'=16] {'branch'}, dimensions={1} | all-to-all | bytes 4194304 | tf_op jit(solution)/shard_map/all_to_all | solution.py:42
  91.8 1.6 all-gather.4.cloned.1.call-done
  93.6 40.3 %all-gather.6.cloned.1.call-done = bf16[4096,512]{1,0:T(8,128)(2,1)} async-done(((bf16[256,512]{1,0:T(8,128)(2,1)}), bf16[4096,512]{1,0:T(8,128)(2,1)}) %all-gather.6.cloned.1.call-update) | async-done | bytes 4194320 | tf_op jit(solution)/shard_map/all_gather | solution.py:50
  133.9 3.5 fusion.39
  138.0 16.8 %all_to_all.56 = bf16[8,48,512]{2,1,0:T(8,128)(2,1)S(1)} all-to-all(bf16[8,48,512]{2,1,0:T(8,128)(2,1)S(1)} %bitcast.121), channel_id=1, replica_groups=mesh['branch'=8,'dp'=16] {'branch'}, dimensions={0} | all-to-all | bytes 786432 | tf_op jit(solution)/shard_map/all_to_all | solution.py:63
  154.8 0.8 copy.73
  155.9 8.0 %fusion.2 = f32[768,448]{0,1:T(8,128)} fusion(bf16[1,768,4096]{2,1,0:T(8,128)(2,1)} %all-gather.4.cloned.1.call-done, bf16[1,448,4096]{2,1,0:T(8,128)(2,1)} %param.16), kind=kOutput, calls=%fused_computation.5 | convolution fusion | flops 2818572288 | bytes 11337728 | tf_op jit(solution)/shard_map/rd,fd->rf/dot_general | solution.py:69
  163.8 30.7 %all-gather.8.cloned.1.call-done = bf16[1,768,4096]{2,1,0:T(8,128)(2,1)} async-done(((bf16[1,48,4096]{2,1,0:T(8,128)(2,1)}), bf16[1,768,4096]{2,1,0:T(8,128)(2,1)}) %all-gather.8.cloned.1.call-update) | async-done | bytes 6291472 | tf_op jit(solution)/shard_map/all_gather | solution.py:64
  194.6 7.0 %fusion.10 = f32[768,448]{0,1:T(8,128)S(1)} fusion(bf16[1,768,4096]{2,1,0:T(8,128)(2,1)} %all-gather.8.cloned.1.call-done, bf16[1,4096,448]{1,2,0:T(8,128)(2,1)} %param.14), kind=kOutput, calls=%fused_computation.13 | convolution fusion | flops 2818572288 | bytes 11337728 | tf_op jit(solution)/shard_map/dot_general | solution.py:67
  201.7 3.6 multiply_convert_fusion.2
  205.3 5.6 %convolution_convert_fusion = bf16[768,4096]{1,0:T(8,128)(2,1)} fusion(bf16[768,448]{0,1:T(8,128)(2,1)S(1)} %get-tuple-element.31, bf16[1,448,4096]{2,1,0:T(8,128)(2,1)S(1)} %copy-done.5), kind=kOutput, calls=%fused_computation.2 | convolution fusion | flops 2821718016 | bytes 10649600 | tf_op jit(solution)/shard_map/dot_general | solution.py:74
  210.9 8.7 %copy.66 = bf16[768,4096]{0,1:T(8,128)(2,1)} copy(bf16[768,4096]{1,0:T(8,128)(2,1)} %convolution_convert_fusion) | data formatting | bytes 12582912 | tf_op jit(solution)/shard_map/stack;reshape | solution.py:78
  219.5 5.7 %fusion.34 = f32[768,4096]{1,0:T(8,128)S(1)} fusion(bf16[768,448]{0,1:T(8,128)(2,1)S(1)} %get-tuple-element.32, bf16[1,4096,448]{1,2,0:T(8,128)(2,1)} %param.14), kind=kOutput, calls=%fused_computation.26 | convolution fusion | flops 2818572288 | bytes 16941056 | tf_op jit(solution)/shard_map/rf,df->rd/dot_general | solution.py:75
  225.3 5.7 %add_convert_fusion = bf16[768,4096]{1,0:T(8,128)(2,1)} fusion(f32[768,4096]{1,0:T(8,128)S(1)} %fusion.34, bf16[768,448]{0,1:T(8,128)(2,1)S(1)} %get-tuple-element.33, bf16[1,4096,448]{1,2,0:T(8,128)(2,1)S(1)} %copy-done.7), kind=kOutput, calls=%fused_computation.1 | convolution fusion | flops 2824863744 | bytes 23232512 | tf_op jit(solution)/shard_map/rf,df->rd/dot_general | solution.py:77
  231.0 8.7 %copy.67 = bf16[768,4096]{0,1:T(8,128)(2,1)} copy(bf16[768,4096]{1,0:T(8,128)(2,1)} %add_convert_fusion) | data formatting | bytes 12582912 | tf_op jit(solution)/shard_map/stack;reshape | solution.py:78
  239.7 10.8 %pad_maximum_fusion = bf16[768,8,2,512]{0,3,2,1:T(8,128)(2,1)} fusion(bf16[768,8,1,512]{0,3,2,1:T(8,128)(2,1)} %bitcast.112, bf16[768,8,1,512]{0,3,2,1:T(8,128)(2,1)} %bitcast.111), kind=kLoop, calls=%fused_computation | loop fusion | flops 6291456 | bytes 25165824 | tf_op jit(solution)/shard_map/stack | solution.py:78
  250.5 16.7 %copy.70 = bf16[768,8192]{1,0:T(8,128)(2,1)} copy(bf16[768,8192]{0,1:T(8,128)(2,1)} %bitcast.110) | data formatting | bytes 25165824
  267.4 8.0 %fusion.21 = bf16[1,448,4096]{2,1,0:T(8,128)(2,1)} fusion(bf16[768,448]{0,1:T(8,128)(2,1)} %copy-done.9, bf16[1,768,4096]{2,1,0:T(8,128)(2,1)} %all-gather.4.cloned.1.call-done), kind=kOutput, calls=%fused_computation.18 | convolution fusion | flops 2820407296 | bytes 10649600 | tf_op jit(solution)/shard_map/rf,rd->fd/dot_general | solution.py:73
  275.4 4.4 %fusion.24 = bf16[1,4096,448]{1,2,0:T(8,128)(2,1)} fusion(bf16[768,448]{0,1:T(8,128)(2,1)S(1)} %get-tuple-element.32, bf16[1,768,4096]{2,1,0:T(8,128)(2,1)S(1)} %bitcast.125), kind=kOutput, calls=%fused_computation.19 | convolution fusion | flops 2820407296 | bytes 10649600 | tf_op jit(solution)/shard_map/rd,rf->df/dot_general | solution.py:71
  279.9 128.2 %reduce-scatter.4.cloned.1.call-done = bf16[48,8192]{1,0:T(8,128)(2,1)} async-done(((bf16[768,8192]{1,0:T(8,128)(2,1)}), bf16[48,8192]{1,0:T(8,128)(2,1)}) %reduce-scatter.4.cloned.1.call-update) | async-done | bytes 786448
  408.1 2.0 copy.71
  410.1 1.6 copy.58
  411.7 6.4 %all-to-all-start.3 = ((bf16[8,48,1024]{2,1,0:T(8,128)(2,1)}), bf16[8,48,1024]{2,1,0:T(8,128)(2,1)S(1)}, u32[]{:S(2)}, u32[]{:S(2)}) async-start(bf16[8,48,1024]{2,1,0:T(8,128)(2,1)} %copy.58), calls=%async_computation.3 | async-start | bytes 1572864 | tf_op jit(solution)/shard_map/all_to_all | solution.py:89
  418.1 7.9 %fusion.27 = bf16[1,4096,448]{1,2,0:T(8,128)(2,1)} fusion(bf16[768,448]{0,1:T(8,128)(2,1)} %copy-done.8, bf16[1,768,4096]{2,1,0:T(8,128)(2,1)} %all-gather.8.cloned.1.call-done), kind=kOutput, calls=%fused_computation.20 | convolution fusion | flops 2820407296 | bytes 10649600 | tf_op jit(solution)/shard_map/rd,rf->df/dot_general | solution.py:72
  426.0 3.9 all-to-all-done.3
  431.8 0.8 copy.62
  (66 shorter events, 7.8 us)
Async XLA Ops:
  7.2 126.7 %copy-start = (bf16[128,4096]{1,0:T(8,128)(2,1)S(1)}, bf16[128,4096]{1,0:T(8,128)(2,1)}, u32[]{:S(2)}) copy-start(bf16[128,4096]{1,0:T(8,128)(2,1)} %param.10) | copy-start | bytes 3145732
  7.2 86.3 %all-gather.4.cloned.1.call-start = ((), (), s32[]{:S(2)}) async-start(), calls=%async_computation.5 | async-start | bytes 6684672 | tf_op jit(solution)/shard_map/all_gather | solution.py:40
  30.5 103.4 %all-gather.6.cloned.1.call-start = ((), (), s32[]{:S(2)}) async-start(), calls=%async_computation.6 | async-start | bytes 4456448 | tf_op jit(solution)/shard_map/all_gather | solution.py:50
  37.5 56.0 %copy-start.3 = (bf16[128,512]{1,0:T(8,128)(2,1)S(1)}, bf16[128,512]{1,0:T(8,128)(2,1)}, u32[]{:S(2)}) copy-start(bf16[128,512]{1,0:T(8,128)(2,1)} %param.9) | copy-start | bytes 393220
  93.5 101.1 %all-gather.8.cloned.1.call-start = ((), (), s32[]{:S(2)}) async-start(), calls=%async_computation.7 | async-start | bytes 6684672 | tf_op jit(solution)/shard_map/all_gather | solution.py:64
  155.6 252.5 %reduce-scatter.4.cloned.1.call-start = ((), (), s32[]{:S(2)}) async-start(), calls=%async_computation.8 | async-start | bytes 13369344
  194.6 7.1 %copy-start.4 = (bf16[1,768,4096]{2,1,0:T(8,128)(2,1)S(1)}, bf16[1,768,4096]{2,1,0:T(8,128)(2,1)}, u32[]{:S(2)}) copy-start(bf16[1,768,4096]{2,1,0:T(8,128)(2,1)} %all-gather.8.cloned.1.call-done) | copy-start | bytes 18874372
  194.6 7.1 %copy-start.6 = (bf16[1,4096,448]{1,2,0:T(8,128)(2,1)S(1)}, bf16[1,4096,448]{1,2,0:T(8,128)(2,1)}, u32[]{:S(2)}) copy-start(bf16[1,4096,448]{1,2,0:T(8,128)(2,1)} %param.15) | copy-start | bytes 11010052
  194.6 7.1 %copy-start.10 = (f32[768,448]{0,1:T(8,128)S(1)}, f32[768,448]{0,1:T(8,128)}, u32[]{:S(2)}) copy-start(f32[768,448]{0,1:T(8,128)} %fusion.2) | copy-start | bytes 4128772
  201.7 3.6 copy-start.5
  205.2 5.6 %copy-start.9 = (bf16[768,448]{0,1:T(8,128)(2,1)}, bf16[768,448]{0,1:T(8,128)(2,1)S(1)}, u32[]{:S(2)}) copy-start(bf16[768,448]{0,1:T(8,128)(2,1)S(1)} %get-tuple-element.31) | copy-start | bytes 2064388
  205.3 20.0 %copy-start.8 = (bf16[768,448]{0,1:T(8,128)(2,1)}, bf16[768,448]{0,1:T(8,128)(2,1)S(1)}, u32[]{:S(2)}) copy-start(bf16[768,448]{0,1:T(8,128)(2,1)S(1)} %get-tuple-element.33) | copy-start | bytes 2064388
  219.5 5.7 %copy-start.7 = (bf16[1,4096,448]{1,2,0:T(8,128)(2,1)S(1)}, bf16[1,4096,448]{1,2,0:T(8,128)(2,1)}, u32[]{:S(2)}) copy-start(bf16[1,4096,448]{1,2,0:T(8,128)(2,1)} %param.15) | copy-start | bytes 11010052
  267.1 8.3 %slice-start = ((s8[6291456]{0:T(1024)(128)(4,1)}), s8[2097152]{0:T(1024)(128)(4,1)S(1)}, s32[]{:S(2)}) async-start(s8[6291456]{0:T(1024)(128)(4,1)} %bitcast.124), calls=%async_computation.9 | async-start | bytes 4194304
  267.4 8.0 %slice-start.1 = ((s8[6291456]{0:T(1024)(128)(4,1)}), s8[4194304]{0:T(1024)(128)(4,1)S(1)}, s32[]{:S(2)}) async-start(s8[6291456]{0:T(1024)(128)(4,1)} %bitcast.124), calls=%async_computation.10 | async-start | bytes 8388608
  411.7 18.3 %all-to-all-start.3 = ((bf16[8,48,1024]{2,1,0:T(8,128)(2,1)}), bf16[8,48,1024]{2,1,0:T(8,128)(2,1)S(1)}, u32[]{:S(2)}, u32[]{:S(2)}) async-start(bf16[8,48,1024]{2,1,0:T(8,128)(2,1)} %copy.58), calls=%async_computation.3 | async-start | bytes 1572864 | tf_op jit(solution)/shard_map/all_to_all | solution.py:89
  418.1 14.5 %copy-start.1 = (bf16[128,4096]{1,0:T(8,128)(2,1)S(1)}, bf16[128,4096]{1,0:T(8,128)(2,1)}, u32[]{:S(2)}) copy-start(bf16[128,4096]{1,0:T(8,128)(2,1)} %param.10) | copy-start | bytes 3145732
  426.0 4.9 %copy-start.2 = (bf16[128,512]{1,0:T(8,128)(2,1)S(1)}, bf16[128,512]{1,0:T(8,128)(2,1)}, u32[]{:S(2)}) copy-start(bf16[128,512]{1,0:T(8,128)(2,1)} %param.17) | copy-start | bytes 393220
Sparse Core Ops, SparseCore 0:
  30.7 62.7 all-gather.3
  95.7 38.1 all-gather.5
  155.8 38.7 all-gather.7
  267.3 140.8 reduce-scatter.3

commit v6 on v3

--- a/solution.py
+++ b/solution.py
@@ -81,8 +81,14 @@
     in_part = lax.psum_scatter(
         input_term.astype(jnp.bfloat16), "dp", scatter_dimension=0, tiled=True
     )
-    packed = jnp.stack([out_part, in_part], axis=1)[None]
-    returned = lax.all_to_all(packed, "branch", split_axis=3, concat_axis=0, tiled=True)
+    packed = jnp.stack(
+        [
+            out_part.reshape(capacity, n_branch, width),
+            in_part.reshape(capacity, n_branch, width),
+        ],
+        axis=2,
+    ).transpose(1, 0, 2, 3)
+    returned = lax.all_to_all(packed, "branch", split_axis=0, concat_axis=0, tiled=True)
     picked = jnp.einsum(
         "sr,sc->rc",
         placing,

time: 412 us -> 402 us (0.976)
  local copies, waits for them, and re-layouts: 27.1 us -> 17 us
    unnamed x33 -> x25, local copies, waits for them, and re-layouts: 13.3 us -> 8.24 us
  transfers between devices with their start and end apart: 6 -> 6, of which waited for: 6 -> 6; matrix products, arithmetic and copies ran while one was open for 12% -> 13% of each run, Pallas kernels for 0% -> 0%
where the time goes in v6:
time: 402 us; the launch traced here: 401 us
  waiting for transfers between devices  208 us (52%)
  blocking collectives  87 us (22%)
  matrix products  61.5 us (15%)
  local copies, waits for them, and re-layouts  17 us (4%)
  between operations  14.1 us (4%)
  starting transfers between devices  7.1 us (2%)
  other arithmetic  6.79 us (2%)
    reduce_scatter x1, waiting for transfers between devices, shards(): lax.psum_scatter(input_term.astype(jnp.bfloat16), 'dp', scatter_dimension...  77.8 us
    reduce_scatter x1, waiting for transfers between devices, shards(): lax.psum_scatter(output_term.astype(jnp.bfloat16), 'dp', scatter_dimensio...  53.6 us
    all_to_all x1, blocking collectives, shards(): lax.all_to_all(wo_local, 'branch', split_axis=1, concat_axis=0, tiled=True)  53.2 us
    all_gather x1, waiting for transfers between devices, shards(): lax.all_gather(mean_block, 'dp', axis=0, tiled=True)  40.3 us
    all_gather x1, waiting for transfers between devices, shards(): all_rows = lax.all_gather(got_rows, 'dp', axis=1, tiled=True)  30.7 us
    all_to_all x1, blocking collectives, shards(): lax.all_to_all(send_grads, 'branch', split_axis=0, concat_axis=2, tiled=T...  17 us
    all_to_all x1, blocking collectives, shards(): lax.all_to_all(send_rows, 'branch', split_axis=0, concat_axis=2, tiled=True)  16.8 us
    unnamed x25, local copies, waits for them, and re-layouts  8.24 us
  transfers between devices with their start and end apart: 6, of which 6 were waited for; matrix products, arithmetic and copies ran while one was open for 13% of the time, Pallas kernels for 0%

profile of v6, /device:TPU:0, one launch (start us, length us, event | category | flops | bytes accessed | tf_op | source)
XLA Modules:
  0.0 401.4 jit_solution(15935657919488470880)
XLA Ops:
  7.2 0.9 copy.43
  8.4 0.7 convert_reduce_fusion.1
  11.0 1.0 broadcast_in_dim.20
  12.7 17.0 %all_to_all.54 = bf16[8,48,512]{2,1,0:T(8,128)(2,1)S(1)} all-to-all(bf16[8,48,512]{2,1,0:T(8,128)(2,1)S(1)} %bitcast.120), channel_id=1, replica_groups=mesh['branch'=8,'dp'=16] {'branch'}, dimensions={0} | all-to-all | bytes 786432 | tf_op jit(solution)/shard_map/all_to_all | solution.py:39
  29.7 0.8 copy.60
  30.6 4.1 %copy.47 = bf16[1,256,4096]{1,2,0:T(8,128)(2,1)} copy(bf16[1,256,4096]{2,1,0:T(8,128)(2,1)} %param.11) | data formatting | bytes 4194304 | tf_op args[2]
  34.7 2.9 copy.48
  37.6 53.2 %all_to_all.55 = bf16[256,8,512]{2,0,1:T(8,128)(2,1)S(1)} all-to-all(bf16[256,8,512]{2,0,1:T(8,128)(2,1)S(1)} %copy.48), channel_id=1, replica_groups=mesh['branch'=8,'dp'=16] {'branch'}, dimensions={1} | all-to-all | bytes 4194304 | tf_op jit(solution)/shard_map/all_to_all | solution.py:42
  91.1 0.7 multiply_convert_fusion.3
  91.8 1.6 all-gather.4.cloned.1.call-done
  93.6 40.3 %all-gather.6.cloned.1.call-done = bf16[4096,512]{1,0:T(8,128)(2,1)} async-done(((bf16[256,512]{1,0:T(8,128)(2,1)}), bf16[4096,512]{1,0:T(8,128)(2,1)}) %all-gather.6.cloned.1.call-update) | async-done | bytes 4194320 | tf_op jit(solution)/shard_map/all_gather | solution.py:50
  133.9 3.5 fusion.39
  138.0 16.8 %all_to_all.56 = bf16[8,48,512]{2,1,0:T(8,128)(2,1)S(1)} all-to-all(bf16[8,48,512]{2,1,0:T(8,128)(2,1)S(1)} %bitcast.122), channel_id=1, replica_groups=mesh['branch'=8,'dp'=16] {'branch'}, dimensions={0} | all-to-all | bytes 786432 | tf_op jit(solution)/shard_map/all_to_all | solution.py:63
  154.8 0.8 copy.61
  155.9 8.0 %fusion.2 = f32[768,448]{0,1:T(8,128)} fusion(bf16[1,768,4096]{2,1,0:T(8,128)(2,1)} %all-gather.4.cloned.1.call-done, bf16[1,448,4096]{2,1,0:T(8,128)(2,1)} %param.16), kind=kOutput, calls=%fused_computation.4 | convolution fusion | flops 2818572288 | bytes 11337728 | tf_op jit(solution)/shard_map/rd,fd->rf/dot_general | solution.py:69
  163.8 30.7 %all-gather.8.cloned.1.call-done = bf16[1,768,4096]{2,1,0:T(8,128)(2,1)} async-done(((bf16[1,48,4096]{2,1,0:T(8,128)(2,1)}), bf16[1,768,4096]{2,1,0:T(8,128)(2,1)}) %all-gather.8.cloned.1.call-update) | async-done | bytes 6291472 | tf_op jit(solution)/shard_map/all_gather | solution.py:64
  194.6 7.0 %fusion.10 = f32[768,448]{0,1:T(8,128)S(1)} fusion(bf16[1,768,4096]{2,1,0:T(8,128)(2,1)} %all-gather.8.cloned.1.call-done, bf16[1,4096,448]{1,2,0:T(8,128)(2,1)} %param.14), kind=kOutput, calls=%fused_computation.12 | convolution fusion | flops 2818572288 | bytes 11337728 | tf_op jit(solution)/shard_map/dot_general | solution.py:67
  201.7 3.5 multiply_convert_fusion.2
  205.2 5.4 %convolution_convert_fusion = bf16[768,4096]{1,0:T(8,128)(2,1)} fusion(bf16[768,448]{0,1:T(8,128)(2,1)S(1)} %get-tuple-element.31, bf16[1,448,4096]{2,1,0:T(8,128)(2,1)S(1)} %copy-done.5), kind=kOutput, calls=%fused_computation.1 | convolution fusion | flops 2821718016 | bytes 10649600 | tf_op jit(solution)/shard_map/dot_general | solution.py:74
  210.9 5.7 %fusion.34 = f32[768,4096]{1,0:T(8,128)S(1)} fusion(bf16[768,448]{0,1:T(8,128)(2,1)S(1)} %get-tuple-element.32, bf16[1,4096,448]{1,2,0:T(8,128)(2,1)} %param.14), kind=kOutput, calls=%fused_computation.25 | convolution fusion | flops 2818572288 | bytes 16941056 | tf_op jit(solution)/shard_map/rf,df->rd/dot_general | solution.py:75
  216.6 5.4 %add_convert_fusion = bf16[768,4096]{1,0:T(8,128)(2,1)} fusion(f32[768,4096]{1,0:T(8,128)S(1)} %fusion.34, bf16[768,448]{0,1:T(8,128)(2,1)S(1)} %get-tuple-element.33, bf16[1,4096,448]{1,2,0:T(8,128)(2,1)S(1)} %copy-done.7), kind=kOutput, calls=%fused_computation | convolution fusion | flops 2824863744 | bytes 23232512 | tf_op jit(solution)/shard_map/rf,df->rd/dot_general | solution.py:77
  222.2 7.2 %fusion.21 = bf16[1,448,4096]{2,1,0:T(8,128)(2,1)} fusion(bf16[768,448]{0,1:T(8,128)(2,1)S(1)} %get-tuple-element.31, bf16[1,768,4096]{2,1,0:T(8,128)(2,1)} %all-gather.4.cloned.1.call-done), kind=kOutput, calls=%fused_computation.17 | convolution fusion | flops 2820407296 | bytes 10649600 | tf_op jit(solution)/shard_map/rf,rd->fd/dot_general | solution.py:73
  229.5 7.3 %fusion.24 = bf16[1,4096,448]{1,2,0:T(8,128)(2,1)} fusion(bf16[768,448]{0,1:T(8,128)(2,1)S(1)} %get-tuple-element.32, bf16[1,768,4096]{2,1,0:T(8,128)(2,1)} %all-gather.8.cloned.1.call-done), kind=kOutput, calls=%fused_computation.18 | convolution fusion | flops 2820407296 | bytes 10649600 | tf_op jit(solution)/shard_map/rd,rf->df/dot_general | solution.py:71
  236.8 53.6 %reduce-scatter.3.cloned.1.call-done = bf16[48,4096]{1,0:T(8,128)(2,1)} async-done(((bf16[768,4096]{1,0:T(8,128)(2,1)}), bf16[48,4096]{1,0:T(8,128)(2,1)}) %reduce-scatter.3.cloned.1.call-update) | async-done | bytes 393232 | tf_op jit(solution)/shard_map/reduce_scatter | solution.py:78
  290.4 1.1 copy.62
  292.2 77.8 %reduce-scatter.5.cloned.1.call-done = bf16[48,4096]{1,0:T(8,128)(2,1)} async-done(((bf16[768,4096]{1,0:T(8,128)(2,1)}), bf16[48,4096]{1,0:T(8,128)(2,1)}) %reduce-scatter.5.cloned.1.call-update) | async-done | bytes 393232 | tf_op jit(solution)/shard_map/reduce_scatter | solution.py:81
  370.0 1.1 copy.63
  371.7 2.7 maximum_bitcast_fusion
  374.4 6.5 %all-to-all-start.3 = ((bf16[8,48,2,512]{3,2,1,0:T(2,128)(2,1)}), bf16[8,48,2,512]{3,2,1,0:T(2,128)(2,1)S(1)}, u32[]{:S(2)}, u32[]{:S(2)}) async-start(bf16[8,48,2,512]{3,2,1,0:T(2,128)(2,1)} %maximum_bitcast_fusion), calls=%async_computation.5 | async-start | bytes 1572864 | tf_op jit(solution)/shard_map/all_to_all | solution.py:91
  380.9 7.4 %fusion.27 = bf16[1,4096,448]{1,2,0:T(8,128)(2,1)} fusion(bf16[768,448]{0,1:T(8,128)(2,1)S(1)} %get-tuple-element.33, bf16[1,768,4096]{2,1,0:T(8,128)(2,1)} %all-gather.8.cloned.1.call-done), kind=kOutput, calls=%fused_computation.19 | convolution fusion | flops 2820407296 | bytes 10649600 | tf_op jit(solution)/shard_map/rd,rf->df/dot_general | solution.py:72
  388.3 3.7 all-to-all-done.3
  394.1 0.8 copy.56
  (60 shorter events, 8.0 us)
Async XLA Ops:
  7.2 126.7 %copy-start = (bf16[128,4096]{1,0:T(8,128)(2,1)S(1)}, bf16[128,4096]{1,0:T(8,128)(2,1)}, u32[]{:S(2)}) copy-start(bf16[128,4096]{1,0:T(8,128)(2,1)} %param.10) | copy-start | bytes 3145732
  7.2 86.3 %all-gather.4.cloned.1.call-start = ((), (), s32[]{:S(2)}) async-start(), calls=%async_computation.6 | async-start | bytes 6684672 | tf_op jit(solution)/shard_map/all_gather | solution.py:40
  30.5 103.4 %all-gather.6.cloned.1.call-start = ((), (), s32[]{:S(2)}) async-start(), calls=%async_computation.7 | async-start | bytes 4456448 | tf_op jit(solution)/shard_map/all_gather | solution.py:50
  37.5 56.0 %copy-start.3 = (bf16[128,512]{1,0:T(8,128)(2,1)S(1)}, bf16[128,512]{1,0:T(8,128)(2,1)}, u32[]{:S(2)}) copy-start(bf16[128,512]{1,0:T(8,128)(2,1)} %param.9) | copy-start | bytes 393220
  93.5 101.1 %all-gather.8.cloned.1.call-start = ((), (), s32[]{:S(2)}) async-start(), calls=%async_computation.8 | async-start | bytes 6684672 | tf_op jit(solution)/shard_map/all_gather | solution.py:64
  155.6 134.8 %reduce-scatter.3.cloned.1.call-start = ((), (), s32[]{:S(2)}) async-start(), calls=%async_computation.9 | async-start | bytes 6684672 | tf_op jit(solution)/shard_map/reduce_scatter | solution.py:78
  194.6 7.1 %copy-start.4 = (bf16[1,768,4096]{2,1,0:T(8,128)(2,1)S(1)}, bf16[1,768,4096]{2,1,0:T(8,128)(2,1)}, u32[]{:S(2)}) copy-start(bf16[1,768,4096]{2,1,0:T(8,128)(2,1)} %all-gather.8.cloned.1.call-done) | copy-start | bytes 18874372
  194.6 7.1 %copy-start.6 = (bf16[1,4096,448]{1,2,0:T(8,128)(2,1)S(1)}, bf16[1,4096,448]{1,2,0:T(8,128)(2,1)}, u32[]{:S(2)}) copy-start(bf16[1,4096,448]{1,2,0:T(8,128)(2,1)} %param.15) | copy-start | bytes 11010052
  194.6 7.1 %copy-start.8 = (f32[768,448]{0,1:T(8,128)S(1)}, f32[768,448]{0,1:T(8,128)}, u32[]{:S(2)}) copy-start(f32[768,448]{0,1:T(8,128)} %fusion.2) | copy-start | bytes 4128772
  201.7 3.6 copy-start.5
  210.6 159.4 %reduce-scatter.5.cloned.1.call-start = ((), (), s32[]{:S(2)}) async-start(), calls=%async_computation.10 | async-start | bytes 6684672 | tf_op jit(solution)/shard_map/reduce_scatter | solution.py:81
  210.9 5.7 %copy-start.7 = (bf16[1,4096,448]{1,2,0:T(8,128)(2,1)S(1)}, bf16[1,4096,448]{1,2,0:T(8,128)(2,1)}, u32[]{:S(2)}) copy-start(bf16[1,4096,448]{1,2,0:T(8,128)(2,1)} %param.15) | copy-start | bytes 11010052
  374.4 17.6 %all-to-all-start.3 = ((bf16[8,48,2,512]{3,2,1,0:T(2,128)(2,1)}), bf16[8,48,2,512]{3,2,1,0:T(2,128)(2,1)S(1)}, u32[]{:S(2)}, u32[]{:S(2)}) async-start(bf16[8,48,2,512]{3,2,1,0:T(2,128)(2,1)} %maximum_bitcast_fusion), calls=%async_computation.5 | async-start | bytes 1572864 | tf_op jit(solution)/shard_map/all_to_all | solution.py:91
  388.3 4.9 %copy-start.2 = (bf16[128,512]{1,0:T(8,128)(2,1)S(1)}, bf16[128,512]{1,0:T(8,128)(2,1)}, u32[]{:S(2)}) copy-start(bf16[128,512]{1,0:T(8,128)(2,1)} %param.17) | copy-start | bytes 393220
  392.1 2.8 copy-start.1
Sparse Core Ops, SparseCore 0:
  30.7 62.7 all-gather.3
  95.7 38.1 all-gather.5
  155.8 38.7 all-gather.7
  210.7 79.6 reduce-scatter.2
  292.7 77.2 reduce-scatter.4

commit v7 on v6

--- a/solution.py
+++ b/solution.py
@@ -78,9 +78,13 @@
     out_part = lax.psum_scatter(
         output_term.astype(jnp.bfloat16), "dp", scatter_dimension=0, tiled=True
     )
-    in_part = lax.psum_scatter(
-        input_term.astype(jnp.bfloat16), "dp", scatter_dimension=0, tiled=True
+    grad_gate = grad_gate.astype(jnp.bfloat16)[None]
+    grad_up = grad_up.astype(jnp.bfloat16)[None]
+    grad_down = grad_down.astype(jnp.bfloat16)[None]
+    input_bf, grad_gate, grad_up, grad_down = lax.optimization_barrier(
+        (input_term.astype(jnp.bfloat16), grad_gate, grad_up, grad_down)
     )
+    in_part = lax.psum_scatter(input_bf, "dp", scatter_dimension=0, tiled=True)
     packed = jnp.stack(
         [
             out_part.reshape(capacity, n_branch, width),
@@ -105,9 +109,9 @@
     return (
         mixed,
         input_grad,
-        grad_gate.astype(jnp.bfloat16)[None],
-        grad_up.astype(jnp.bfloat16)[None],
-        grad_down.astype(jnp.bfloat16)[None],
+        grad_gate,
+        grad_up,
+        grad_down,
     )
 
 

time: 402 us -> 402 us (level)
    all_to_all x1, waiting for transfers between devices: 3.73 us -> 11.3 us  [shards(): lax.all_to_all(packed, 'branch', split_axis=0, concat_axis=0, tiled=True)]
    reduce_scatter x1, waiting for transfers between devices: 53.6 us -> 49.3 us  [shards(): lax.psum_scatter(output_term.astype(jnp.bfloat16), 'dp', scatter_dimensio...]
    unnamed x25 -> x29, local copies, waits for them, and re-layouts: 8.24 us -> 8.25 us
  transfers between devices with their start and end apart: 6 -> 6, of which waited for: 6 -> 6; matrix products, arithmetic and copies ran while one was open for 13% -> 12% of each run, Pallas kernels for 0% -> 0%
where the time goes in v7:
time: 402 us
  waiting for transfers between devices  211 us (52%)
  blocking collectives  87 us (22%)
  matrix products  58.8 us (15%)
  local copies, waits for them, and re-layouts  17 us (4%)
  between operations  14.1 us (4%)
  other arithmetic  6.78 us (2%)
  starting transfers between devices  6.75 us (2%)
    reduce_scatter x1, waiting for transfers between devices, shards(): in_part = lax.psum_scatter(input_bf, 'dp', scatter_dimension=0, tiled=True)  77.9 us
    all_to_all x1, blocking collectives, shards(): lax.all_to_all(wo_local, 'branch', split_axis=1, concat_axis=0, tiled=True)  53.2 us
    reduce_scatter x1, waiting for transfers between devices, shards(): lax.psum_scatter(output_term.astype(jnp.bfloat16), 'dp', scatter_dimensio...  49.3 us
    all_gather x1, waiting for transfers between devices, shards(): lax.all_gather(mean_block, 'dp', axis=0, tiled=True)  40.3 us
    all_gather x1, waiting for transfers between devices, shards(): all_rows = lax.all_gather(got_rows, 'dp', axis=1, tiled=True)  30.7 us
    all_to_all x1, blocking collectives, shards(): lax.all_to_all(send_grads, 'branch', split_axis=0, concat_axis=2, tiled=T...  17 us
    all_to_all x1, blocking collectives, shards(): lax.all_to_all(send_rows, 'branch', split_axis=0, concat_axis=2, tiled=True)  16.8 us
    all_to_all x1, waiting for transfers between devices, shards(): lax.all_to_all(packed, 'branch', split_axis=0, concat_axis=0, tiled=True)  11.3 us
  transfers between devices with their start and end apart: 6, of which 6 were waited for; matrix products, arithmetic and copies ran while one was open for 12% of the time, Pallas kernels for 0%

profile of v7, /device:TPU:0, one launch (start us, length us, event | category | flops | bytes accessed | tf_op | source)
XLA Modules:
  0.0 401.6 jit_solution(10547546715018371084)
XLA Ops:
  7.2 0.9 copy.43
  8.4 0.7 convert_reduce_fusion.1
  11.0 1.0 broadcast_in_dim.20
  12.7 17.0 %all_to_all.54 = bf16[8,48,512]{2,1,0:T(8,128)(2,1)S(1)} all-to-all(bf16[8,48,512]{2,1,0:T(8,128)(2,1)S(1)} %bitcast.120), channel_id=1, replica_groups=mesh['branch'=8,'dp'=16] {'branch'}, dimensions={0} | all-to-all | bytes 786432 | tf_op jit(solution)/shard_map/all_to_all | solution.py:39
  29.7 0.8 copy.60
  30.6 4.1 %copy.47 = bf16[1,256,4096]{1,2,0:T(8,128)(2,1)} copy(bf16[1,256,4096]{2,1,0:T(8,128)(2,1)} %param.11) | data formatting | bytes 4194304 | tf_op args[2]
  34.7 2.9 copy.48
  37.6 53.2 %all_to_all.55 = bf16[256,8,512]{2,0,1:T(8,128)(2,1)S(1)} all-to-all(bf16[256,8,512]{2,0,1:T(8,128)(2,1)S(1)} %copy.48), channel_id=1, replica_groups=mesh['branch'=8,'dp'=16] {'branch'}, dimensions={1} | all-to-all | bytes 4194304 | tf_op jit(solution)/shard_map/all_to_all | solution.py:42
  91.1 0.7 multiply_convert_fusion.3
  91.8 1.6 all-gather.4.cloned.1.call-done
  93.6 40.3 %all-gather.6.cloned.1.call-done = bf16[4096,512]{1,0:T(8,128)(2,1)} async-done(((bf16[256,512]{1,0:T(8,128)(2,1)}), bf16[4096,512]{1,0:T(8,128)(2,1)}) %all-gather.6.cloned.1.call-update) | async-done | bytes 4194320 | tf_op jit(solution)/shard_map/all_gather | solution.py:50
  133.9 3.5 fusion.39
  138.0 16.8 %all_to_all.56 = bf16[8,48,512]{2,1,0:T(8,128)(2,1)S(1)} all-to-all(bf16[8,48,512]{2,1,0:T(8,128)(2,1)S(1)} %bitcast.122), channel_id=1, replica_groups=mesh['branch'=8,'dp'=16] {'branch'}, dimensions={0} | all-to-all | bytes 786432 | tf_op jit(solution)/shard_map/all_to_all | solution.py:63
  154.8 0.8 copy.61
  155.9 8.0 %fusion.2 = f32[768,448]{0,1:T(8,128)} fusion(bf16[1,768,4096]{2,1,0:T(8,128)(2,1)} %all-gather.4.cloned.1.call-done, bf16[1,448,4096]{2,1,0:T(8,128)(2,1)} %param.16), kind=kOutput, calls=%fused_computation.4 | convolution fusion | flops 2818572288 | bytes 11337728 | tf_op jit(solution)/shard_map/rd,fd->rf/dot_general | solution.py:69
  163.8 30.7 %all-gather.8.cloned.1.call-done = bf16[1,768,4096]{2,1,0:T(8,128)(2,1)} async-done(((bf16[1,48,4096]{2,1,0:T(8,128)(2,1)}), bf16[1,768,4096]{2,1,0:T(8,128)(2,1)}) %all-gather.8.cloned.1.call-update) | async-done | bytes 6291472 | tf_op jit(solution)/shard_map/all_gather | solution.py:64
  194.6 7.0 %fusion.10 = f32[768,448]{0,1:T(8,128)S(1)} fusion(bf16[1,768,4096]{2,1,0:T(8,128)(2,1)} %all-gather.8.cloned.1.call-done, bf16[1,4096,448]{1,2,0:T(8,128)(2,1)} %param.14), kind=kOutput, calls=%fused_computation.12 | convolution fusion | flops 2818572288 | bytes 11337728 | tf_op jit(solution)/shard_map/dot_general | solution.py:67
  201.7 3.5 multiply_convert_fusion.2
  205.2 5.4 %convolution_convert_fusion = bf16[768,4096]{1,0:T(8,128)(2,1)} fusion(bf16[768,448]{0,1:T(8,128)(2,1)S(1)} %get-tuple-element.39, bf16[1,448,4096]{2,1,0:T(8,128)(2,1)S(1)} %copy-done.5), kind=kOutput, calls=%fused_computation.1 | convolution fusion | flops 2821718016 | bytes 10649600 | tf_op jit(solution)/shard_map/dot_general | solution.py:74
  210.7 5.5 %fusion.34 = f32[768,4096]{1,0:T(8,128)S(1)} fusion(bf16[768,448]{0,1:T(8,128)(2,1)S(1)} %get-tuple-element.40, bf16[1,4096,448]{1,2,0:T(8,128)(2,1)} %param.14), kind=kOutput, calls=%fused_computation.25 | convolution fusion | flops 2818572288 | bytes 16941056 | tf_op jit(solution)/shard_map/rf,df->rd/dot_general | solution.py:75
  216.2 7.6 %fusion.21 = bf16[1,448,4096]{2,1,0:T(8,128)(2,1)} fusion(bf16[768,448]{0,1:T(8,128)(2,1)S(1)} %get-tuple-element.39, bf16[1,768,4096]{2,1,0:T(8,128)(2,1)} %all-gather.4.cloned.1.call-done), kind=kOutput, calls=%fused_computation.17 | convolution fusion | flops 2820407296 | bytes 10649600 | tf_op jit(solution)/shard_map/rf,rd->fd/dot_general | solution.py:73
  223.8 7.4 %fusion.24 = bf16[1,4096,448]{1,2,0:T(8,128)(2,1)} fusion(bf16[768,448]{0,1:T(8,128)(2,1)S(1)} %get-tuple-element.40, bf16[1,768,4096]{2,1,0:T(8,128)(2,1)} %all-gather.8.cloned.1.call-done), kind=kOutput, calls=%fused_computation.18 | convolution fusion | flops 2820407296 | bytes 10649600 | tf_op jit(solution)/shard_map/rd,rf->df/dot_general | solution.py:71
  231.2 4.5 %fusion.27 = bf16[1,4096,448]{1,2,0:T(8,128)(2,1)} fusion(bf16[768,448]{0,1:T(8,128)(2,1)S(1)} %get-tuple-element.41, bf16[1,768,4096]{2,1,0:T(8,128)(2,1)S(1)} %bitcast.130), kind=kOutput, calls=%fused_computation.19 | convolution fusion | flops 2820407296 | bytes 10649600 | tf_op jit(solution)/shard_map/rd,rf->df/dot_general | solution.py:72
  235.7 5.3 %add_convert_fusion = bf16[768,4096]{1,0:T(8,128)(2,1)} fusion(f32[768,4096]{1,0:T(8,128)S(1)} %fusion.34, bf16[768,448]{0,1:T(8,128)(2,1)S(1)} %get-tuple-element.41, bf16[1,4096,448]{1,2,0:T(8,128)(2,1)S(1)} %copy-done.7), kind=kOutput, calls=%fused_computation | convolution fusion | flops 2824863744 | bytes 23232512 | tf_op jit(solution)/shard_map/rf,df->rd/dot_general | solution.py:77
  241.1 49.3 %reduce-scatter.3.cloned.1.call-done = bf16[48,4096]{1,0:T(8,128)(2,1)} async-done(((bf16[768,4096]{1,0:T(8,128)(2,1)}), bf16[48,4096]{1,0:T(8,128)(2,1)}) %reduce-scatter.3.cloned.1.call-update) | async-done | bytes 393232 | tf_op jit(solution)/shard_map/reduce_scatter | solution.py:78
  290.3 1.1 copy.62
  292.1 77.9 %reduce-scatter.5.cloned.1.call-done = bf16[48,4096]{1,0:T(8,128)(2,1)} async-done(((bf16[768,4096]{1,0:T(8,128)(2,1)}), bf16[48,4096]{1,0:T(8,128)(2,1)}) %reduce-scatter.5.cloned.1.call-update) | async-done | bytes 393232 | tf_op jit(solution)/shard_map/reduce_scatter | solution.py:87
  370.0 1.1 copy.63
  371.7 2.7 maximum_bitcast_fusion
  374.4 6.4 %all-to-all-start.3 = ((bf16[8,48,2,512]{3,2,1,0:T(2,128)(2,1)}), bf16[8,48,2,512]{3,2,1,0:T(2,128)(2,1)S(1)}, u32[]{:S(2)}, u32[]{:S(2)}) async-start(bf16[8,48,2,512]{3,2,1,0:T(2,128)(2,1)} %maximum_bitcast_fusion), calls=%async_computation.5 | async-start | bytes 1572864 | tf_op jit(solution)/shard_map/all_to_all | solution.py:95
  381.0 11.3 %all-to-all-done.3 = bf16[8,48,2,512]{3,2,1,0:T(2,128)(2,1)S(1)} async-done(((bf16[8,48,2,512]{3,2,1,0:T(2,128)(2,1)}), bf16[8,48,2,512]{3,2,1,0:T(2,128)(2,1)S(1)}, u32[]{:S(2)}, u32[]{:S(2)}) %all-to-all-start.3) | async-done | bytes 786464 | tf_op jit(solution)/shard_map/all_to_all | solution.py:95
  394.3 0.8 copy.56
  (65 shorter events, 7.8 us)
Async XLA Ops:
  7.2 126.7 %copy-start = (bf16[128,4096]{1,0:T(8,128)(2,1)S(1)}, bf16[128,4096]{1,0:T(8,128)(2,1)}, u32[]{:S(2)}) copy-start(bf16[128,4096]{1,0:T(8,128)(2,1)} %param.10) | copy-start | bytes 3145732
  7.2 86.3 %all-gather.4.cloned.1.call-start = ((), (), s32[]{:S(2)}) async-start(), calls=%async_computation.6 | async-start | bytes 6684672 | tf_op jit(solution)/shard_map/all_gather | solution.py:40
  30.5 103.4 %all-gather.6.cloned.1.call-start = ((), (), s32[]{:S(2)}) async-start(), calls=%async_computation.7 | async-start | bytes 4456448 | tf_op jit(solution)/shard_map/all_gather | solution.py:50
  37.5 56.0 %copy-start.3 = (bf16[128,512]{1,0:T(8,128)(2,1)S(1)}, bf16[128,512]{1,0:T(8,128)(2,1)}, u32[]{:S(2)}) copy-start(bf16[128,512]{1,0:T(8,128)(2,1)} %param.9) | copy-start | bytes 393220
  93.5 101.1 %all-gather.8.cloned.1.call-start = ((), (), s32[]{:S(2)}) async-start(), calls=%async_computation.8 | async-start | bytes 6684672 | tf_op jit(solution)/shard_map/all_gather | solution.py:64
  155.6 134.7 %reduce-scatter.3.cloned.1.call-start = ((), (), s32[]{:S(2)}) async-start(), calls=%async_computation.9 | async-start | bytes 6684672 | tf_op jit(solution)/shard_map/reduce_scatter | solution.py:78
  194.6 7.1 %copy-start.4 = (bf16[1,768,4096]{2,1,0:T(8,128)(2,1)S(1)}, bf16[1,768,4096]{2,1,0:T(8,128)(2,1)}, u32[]{:S(2)}) copy-start(bf16[1,768,4096]{2,1,0:T(8,128)(2,1)} %all-gather.8.cloned.1.call-done) | copy-start | bytes 18874372
  194.6 7.1 %copy-start.6 = (bf16[1,4096,448]{1,2,0:T(8,128)(2,1)S(1)}, bf16[1,4096,448]{1,2,0:T(8,128)(2,1)}, u32[]{:S(2)}) copy-start(bf16[1,4096,448]{1,2,0:T(8,128)(2,1)} %param.15) | copy-start | bytes 11010052
  194.6 7.1 %copy-start.8 = (f32[768,448]{0,1:T(8,128)S(1)}, f32[768,448]{0,1:T(8,128)}, u32[]{:S(2)}) copy-start(f32[768,448]{0,1:T(8,128)} %fusion.2) | copy-start | bytes 4128772
  201.7 3.6 copy-start.5
  210.6 159.4 %reduce-scatter.5.cloned.1.call-start = ((), (), s32[]{:S(2)}) async-start(), calls=%async_computation.10 | async-start | bytes 6684672 | tf_op jit(solution)/shard_map/reduce_scatter | solution.py:87
  216.2 15.0 %slice-start = ((s8[6291456]{0:T(1024)(128)(4,1)}), s8[4194304]{0:T(1024)(128)(4,1)S(1)}, s32[]{:S(2)}) async-start(s8[6291456]{0:T(1024)(128)(4,1)} %bitcast.129), calls=%async_computation.11 | async-start | bytes 8388608
  223.8 7.4 %slice-start.1 = ((s8[6291456]{0:T(1024)(128)(4,1)}), s8[2097152]{0:T(1024)(128)(4,1)S(1)}, s32[]{:S(2)}) async-start(s8[6291456]{0:T(1024)(128)(4,1)} %bitcast.129), calls=%async_computation.12 | async-start | bytes 4194304
  231.2 4.5 %copy-start.7 = (bf16[1,4096,448]{1,2,0:T(8,128)(2,1)S(1)}, bf16[1,4096,448]{1,2,0:T(8,128)(2,1)}, u32[]{:S(2)}) copy-start(bf16[1,4096,448]{1,2,0:T(8,128)(2,1)} %param.15) | copy-start | bytes 11010052
  374.4 17.9 %all-to-all-start.3 = ((bf16[8,48,2,512]{3,2,1,0:T(2,128)(2,1)}), bf16[8,48,2,512]{3,2,1,0:T(2,128)(2,1)S(1)}, u32[]{:S(2)}, u32[]{:S(2)}) async-start(bf16[8,48,2,512]{3,2,1,0:T(2,128)(2,1)} %maximum_bitcast_fusion), calls=%async_computation.5 | async-start | bytes 1572864 | tf_op jit(solution)/shard_map/all_to_all | solution.py:95
  380.8 12.7 %copy-start.2 = (bf16[128,512]{1,0:T(8,128)(2,1)S(1)}, bf16[128,512]{1,0:T(8,128)(2,1)}, u32[]{:S(2)}) copy-start(bf16[128,512]{1,0:T(8,128)(2,1)} %param.17) | copy-start | bytes 393220
  392.3 2.8 copy-start.1
Sparse Core Ops, SparseCore 0:
  30.7 62.7 all-gather.3
  95.7 38.1 all-gather.5
  155.8 38.7 all-gather.7
  210.7 79.5 reduce-scatter.2
  292.6 77.3 reduce-scatter.4

commit v8 on v6

--- a/solution.py
+++ b/solution.py
@@ -36,20 +36,17 @@
         .astype(jnp.bfloat16)
         .reshape(n_branch, capacity, width)
     )
-    got_grads = lax.all_to_all(send_grads, "branch", split_axis=0, concat_axis=2, tiled=True)
-    all_grads = lax.all_gather(got_grads, "dp", axis=1, tiled=True)
-    got_grads, wo_local = lax.optimization_barrier((got_grads, branch_wo[0]))
-    pieces = lax.all_to_all(wo_local, "branch", split_axis=1, concat_axis=0, tiled=True)
+    pieces = lax.all_to_all(branch_wo[0], "branch", split_axis=1, concat_axis=0, tiled=True)
+    pieces, send_grads = lax.optimization_barrier((pieces, send_grads))
     summed = jnp.sum(
         pieces.reshape(n_branch, -1, width).astype(jnp.float32), axis=0
     )
     mean_block = (summed / n_branch).astype(jnp.bfloat16)
-    mean_block, all_grads = lax.optimization_barrier((mean_block, all_grads))
-    attended = jnp.dot(
-        context,
-        lax.all_gather(mean_block, "dp", axis=0, tiled=True),
-        preferred_element_type=jnp.float32,
-    )
+    wo_full = lax.all_gather(mean_block, "dp", axis=0, tiled=True)
+    got_grads = lax.all_to_all(send_grads, "branch", split_axis=0, concat_axis=2, tiled=True)
+    got_grads, wo_full = lax.optimization_barrier((got_grads, wo_full))
+    all_grads = lax.all_gather(got_grads, "dp", axis=1, tiled=True)
+    attended = jnp.dot(context, wo_full, preferred_element_type=jnp.float32)
     hidden = (hidden_in.astype(jnp.float32) + attended).astype(jnp.bfloat16)
     doubled = jnp.repeat(hidden, 2, axis=0)
     send_rows = (
@@ -61,6 +58,7 @@
     weight_up = w_up[0]
     weight_down = w_down[0]
     got_rows = lax.all_to_all(send_rows, "branch", split_axis=0, concat_axis=2, tiled=True)
+    got_rows, all_grads = lax.optimization_barrier((got_rows, all_grads))
     all_rows = lax.all_gather(got_rows, "dp", axis=1, tiled=True)
     rows_two = all_rows[0]
     grads_two = all_grads[0]

time: 402 us -> 390 us (0.970)
  blocking collectives: 87 us -> 36.6 us
  waiting for transfers between devices: 208 us -> 234 us
  starting transfers between devices: 7.1 us -> 14.2 us
  local copies, waits for them, and re-layouts: 17 us -> 21.9 us
    all_to_all x1 -> x0, blocking collectives: 53.2 us -> none  [shards(): lax.all_to_all(wo_local, 'branch', split_axis=1, concat_axis=0, tiled=True)]
    all_to_all x0 -> x1, waiting for transfers between devices: none -> 20.2 us  [shards(): lax.all_to_all(branch_wo[0], 'branch', split_axis=1, concat_axis=0, tiled...]
    all_gather x1, waiting for transfers between devices: 1.61 us -> 21.4 us  [shards(): all_grads = lax.all_gather(got_grads, 'dp', axis=1, tiled=True)]
    all_gather x1, waiting for transfers between devices: 40.3 us -> 22 us  [shards(): wo_full = lax.all_gather(mean_block, 'dp', axis=0, tiled=True)]
    all_to_all x0 -> x1, starting transfers between devices: none -> 7.04 us  [shards(): lax.all_to_all(branch_wo[0], 'branch', split_axis=1, concat_axis=0, tiled...]
    all_gather x1, waiting for transfers between devices: 30.7 us -> 36.7 us  [shards(): all_rows = lax.all_gather(got_rows, 'dp', axis=1, tiled=True)]
    all_to_all x1, blocking collectives: 16.8 us -> 21.7 us  [shards(): lax.all_to_all(send_rows, 'branch', split_axis=0, concat_axis=2, tiled=True)]
    unnamed x25 -> x35, local copies, waits for them, and re-layouts: 8.24 us -> 11.5 us
  transfers between devices with their start and end apart: 6 -> 7, of which waited for: 6 -> 7; matrix products, arithmetic and copies ran while one was open for 13% -> 14% of each run, Pallas kernels for 0% -> 0%
where the time goes in v8:
time: 390 us; the launch traced here: 389 us
  waiting for transfers between devices  234 us (60%)
  matrix products  62.9 us (16%)
  blocking collectives  36.6 us (9%)
  local copies, waits for them, and re-layouts  21.9 us (6%)
  starting transfers between devices  14.2 us (4%)
  between operations  14.1 us (4%)
  other arithmetic  5.42 us (1%)
    reduce_scatter x1, waiting for transfers between devices, shards(): lax.psum_scatter(input_term.astype(jnp.bfloat16), 'dp', scatter_dimension...  77.9 us
    reduce_scatter x1, waiting for transfers between devices, shards(): lax.psum_scatter(output_term.astype(jnp.bfloat16), 'dp', scatter_dimensio...  52.1 us
    all_gather x1, waiting for transfers between devices, shards(): all_rows = lax.all_gather(got_rows, 'dp', axis=1, tiled=True)  36.7 us
    all_gather x1, waiting for transfers between devices, shards(): wo_full = lax.all_gather(mean_block, 'dp', axis=0, tiled=True)  22 us
    all_to_all x1, blocking collectives, shards(): lax.all_to_all(send_rows, 'branch', split_axis=0, concat_axis=2, tiled=True)  21.7 us
    all_gather x1, waiting for transfers between devices, shards(): all_grads = lax.all_gather(got_grads, 'dp', axis=1, tiled=True)  21.4 us
    all_to_all x1, waiting for transfers between devices, shards(): lax.all_to_all(branch_wo[0], 'branch', split_axis=1, concat_axis=0, tiled...  20.2 us
    all_to_all x1, blocking collectives, shards(): lax.all_to_all(send_grads, 'branch', split_axis=0, concat_axis=2, tiled=T...  14.9 us
  transfers between devices with their start and end apart: 7, of which 7 were waited for; matrix products, arithmetic and copies ran while one was open for 14% of the time, Pallas kernels for 0%

profile of v8, /device:TPU:0, one launch (start us, length us, event | category | flops | bytes accessed | tf_op | source)
XLA Modules:
  0.0 389.5 jit_solution(17414942232911408846)
XLA Ops:
  7.2 4.2 %copy.44 = bf16[1,256,4096]{1,2,0:T(8,128)(2,1)} copy(bf16[1,256,4096]{2,1,0:T(8,128)(2,1)} %param.11) | data formatting | bytes 4194304 | tf_op args[2]
  11.4 7.0 %all-to-all-start = ((bf16[256,8,512]{0,2,1:T(8,128)(2,1)}), bf16[256,8,512]{0,2,1:T(8,128)(2,1)S(1)}, u32[]{:S(2)}, u32[]{:S(2)}) async-start(bf16[256,8,512]{0,2,1:T(8,128)(2,1)} %bitcast.118), calls=%async_computation | async-start | bytes 4194304 | tf_op jit(solution)/shard_map/all_to_all | solution.py:39
  20.0 0.9 broadcast_in_dim.20
  21.0 2.2 reshape.92
  23.3 1.4 convolution_convert_fusion.2
  24.6 20.2 %all-to-all-done = bf16[256,8,512]{0,2,1:T(8,128)(2,1)S(1)} async-done(((bf16[256,8,512]{0,2,1:T(8,128)(2,1)}), bf16[256,8,512]{0,2,1:T(8,128)(2,1)S(1)}, u32[]{:S(2)}, u32[]{:S(2)}) %all-to-all-start) | async-done | bytes 2097184 | tf_op jit(solution)/shard_map/all_to_all | solution.py:39
  44.8 1.3 copy-done.2
  46.2 2.9 copy.45
  50.1 14.9 %all_to_all.60 = bf16[8,48,512]{2,1,0:T(8,128)(2,1)S(1)} all-to-all(bf16[8,48,512]{2,1,0:T(8,128)(2,1)S(1)} %bitcast.123), channel_id=1, replica_groups=mesh['branch'=8,'dp'=16] {'branch'}, dimensions={0} | all-to-all | bytes 786432 | tf_op jit(solution)/shard_map/all_to_all | solution.py:46
  65.8 22.0 %all-gather.4.cloned.1.call-done = bf16[4096,512]{1,0:T(8,128)(2,1)} async-done(((bf16[256,512]{1,0:T(8,128)(2,1)}), bf16[4096,512]{1,0:T(8,128)(2,1)}) %all-gather.4.cloned.1.call-update) | async-done | bytes 4194320 | tf_op jit(solution)/shard_map/all_gather | solution.py:45
  87.9 1.0 copy.43
  88.9 3.5 fusion.39
  93.1 21.7 %all_to_all.61 = bf16[8,48,512]{2,1,0:T(8,128)(2,1)S(1)} all-to-all(bf16[8,48,512]{2,1,0:T(8,128)(2,1)S(1)} %bitcast.126), channel_id=1, replica_groups=mesh['branch'=8,'dp'=16] {'branch'}, dimensions={0} | all-to-all | bytes 786432 | tf_op jit(solution)/shard_map/all_to_all | solution.py:60
  115.5 21.4 %all-gather.6.cloned.1.call-done = bf16[1,768,4096]{2,1,0:T(8,128)(2,1)} async-done(((bf16[1,48,4096]{2,1,0:T(8,128)(2,1)}), bf16[1,768,4096]{2,1,0:T(8,128)(2,1)}) %all-gather.6.cloned.1.call-update) | async-done | bytes 6291472 | tf_op jit(solution)/shard_map/all_gather | solution.py:48
  137.2 8.0 %fusion.2 = f32[768,448]{0,1:T(8,128)} fusion(bf16[1,768,4096]{2,1,0:T(8,128)(2,1)} %all-gather.6.cloned.1.call-done, bf16[1,448,4096]{2,1,0:T(8,128)(2,1)} %param.16), kind=kOutput, calls=%fused_computation.4 | convolution fusion | flops 2818572288 | bytes 11337728 | tf_op jit(solution)/shard_map/rd,fd->rf/dot_general | solution.py:67
  145.2 36.7 %all-gather.8.cloned.1.call-done = bf16[1,768,4096]{2,1,0:T(8,128)(2,1)} async-done(((bf16[1,48,4096]{2,1,0:T(8,128)(2,1)}), bf16[1,768,4096]{2,1,0:T(8,128)(2,1)}) %all-gather.8.cloned.1.call-update) | async-done | bytes 6291472 | tf_op jit(solution)/shard_map/all_gather | solution.py:62
  181.9 7.0 %fusion.10 = f32[768,448]{0,1:T(8,128)S(1)} fusion(bf16[1,768,4096]{2,1,0:T(8,128)(2,1)} %all-gather.8.cloned.1.call-done, bf16[1,4096,448]{1,2,0:T(8,128)(2,1)} %param.14), kind=kOutput, calls=%fused_computation.12 | convolution fusion | flops 2818572288 | bytes 11337728 | tf_op jit(solution)/shard_map/dot_general | solution.py:65
  189.0 3.5 multiply_convert_fusion.2
  192.6 0.8 copy-done.11
  193.4 5.5 %convolution_convert_fusion = bf16[768,4096]{1,0:T(8,128)(2,1)} fusion(bf16[768,448]{0,1:T(8,128)(2,1)S(1)} %get-tuple-element.37, bf16[1,448,4096]{2,1,0:T(8,128)(2,1)S(1)} %copy-done.8), kind=kOutput, calls=%fused_computation.1 | convolution fusion | flops 2821718016 | bytes 10649600 | tf_op jit(solution)/shard_map/dot_general | solution.py:72
  199.2 5.7 %fusion.34 = f32[768,4096]{1,0:T(8,128)S(1)} fusion(bf16[768,448]{0,1:T(8,128)(2,1)S(1)} %get-tuple-element.38, bf16[1,4096,448]{1,2,0:T(8,128)(2,1)} %param.14), kind=kOutput, calls=%fused_computation.25 | convolution fusion | flops 2818572288 | bytes 16941056 | tf_op jit(solution)/shard_map/rf,df->rd/dot_general | solution.py:73
  204.9 5.7 %add_convert_fusion = bf16[768,4096]{1,0:T(8,128)(2,1)} fusion(f32[768,4096]{1,0:T(8,128)S(1)} %fusion.34, bf16[768,448]{0,1:T(8,128)(2,1)S(1)} %get-tuple-element.39, bf16[1,4096,448]{1,2,0:T(8,128)(2,1)S(1)} %copy-done.10), kind=kOutput, calls=%fused_computation | convolution fusion | flops 2824863744 | bytes 23232512 | tf_op jit(solution)/shard_map/rf,df->rd/dot_general | solution.py:75
  211.8 7.2 %fusion.21 = bf16[1,448,4096]{2,1,0:T(8,128)(2,1)} fusion(bf16[768,448]{0,1:T(8,128)(2,1)S(1)} %copy-done.12, bf16[1,768,4096]{2,1,0:T(8,128)(2,1)} %all-gather.6.cloned.1.call-done), kind=kOutput, calls=%fused_computation.17 | convolution fusion | flops 2820407296 | bytes 10649600 | tf_op jit(solution)/shard_map/rf,rd->fd/dot_general | solution.py:71
  219.0 7.3 %fusion.24 = bf16[1,4096,448]{1,2,0:T(8,128)(2,1)} fusion(bf16[768,448]{0,1:T(8,128)(2,1)S(1)} %get-tuple-element.38, bf16[1,768,4096]{2,1,0:T(8,128)(2,1)} %all-gather.8.cloned.1.call-done), kind=kOutput, calls=%fused_computation.18 | convolution fusion | flops 2820407296 | bytes 10649600 | tf_op jit(solution)/shard_map/rd,rf->df/dot_general | solution.py:69
  226.3 52.1 %reduce-scatter.3.cloned.1.call-done = bf16[48,4096]{1,0:T(8,128)(2,1)} async-done(((bf16[768,4096]{1,0:T(8,128)(2,1)}), bf16[48,4096]{1,0:T(8,128)(2,1)}) %reduce-scatter.3.cloned.1.call-update) | async-done | bytes 393232 | tf_op jit(solution)/shard_map/reduce_scatter | solution.py:76
  278.4 1.1 copy.63
  280.1 77.9 %reduce-scatter.5.cloned.1.call-done = bf16[48,4096]{1,0:T(8,128)(2,1)} async-done(((bf16[768,4096]{1,0:T(8,128)(2,1)}), bf16[48,4096]{1,0:T(8,128)(2,1)}) %reduce-scatter.5.cloned.1.call-update) | async-done | bytes 393232 | tf_op jit(solution)/shard_map/reduce_scatter | solution.py:79
  358.0 1.1 copy.64
  359.8 2.7 maximum_bitcast_fusion
  362.4 6.6 %all-to-all-start.3 = ((bf16[8,48,2,512]{3,2,1,0:T(2,128)(2,1)}), bf16[8,48,2,512]{3,2,1,0:T(2,128)(2,1)S(1)}, u32[]{:S(2)}, u32[]{:S(2)}) async-start(bf16[8,48,2,512]{3,2,1,0:T(2,128)(2,1)} %maximum_bitcast_fusion), calls=%async_computation.5 | async-start | bytes 1572864 | tf_op jit(solution)/shard_map/all_to_all | solution.py:89
  369.0 7.2 %fusion.27 = bf16[1,4096,448]{1,2,0:T(8,128)(2,1)} fusion(bf16[768,448]{0,1:T(8,128)(2,1)S(1)} %get-tuple-element.39, bf16[1,768,4096]{2,1,0:T(8,128)(2,1)} %all-gather.8.cloned.1.call-done), kind=kOutput, calls=%fused_computation.19 | convolution fusion | flops 2820407296 | bytes 10649600 | tf_op jit(solution)/shard_map/rd,rf->df/dot_general | solution.py:70
  376.2 3.9 %all-to-all-done.3 = bf16[8,48,2,512]{3,2,1,0:T(2,128)(2,1)S(1)} async-done(((bf16[8,48,2,512]{3,2,1,0:T(2,128)(2,1)}), bf16[8,48,2,512]{3,2,1,0:T(2,128)(2,1)S(1)}, u32[]{:S(2)}, u32[]{:S(2)}) %all-to-all-start.3) | async-done | bytes 786464 | tf_op jit(solution)/shard_map/all_to_all | solution.py:89
  (71 shorter events, 10.6 us)
Async XLA Ops:
  7.2 81.8 %copy-start = (bf16[128,4096]{1,0:T(8,128)(2,1)S(1)}, bf16[128,4096]{1,0:T(8,128)(2,1)}, u32[]{:S(2)}) copy-start(bf16[128,4096]{1,0:T(8,128)(2,1)} %param.10) | copy-start | bytes 3145732
  7.2 11.3 %copy-start.5 = (s32[128,2]{0,1:T(2,128)S(1)}, s32[128,2]{0,1:T(2,128)}, u32[]{:S(2)}) copy-start(s32[128,2]{0,1:T(2,128)} %param.12) | copy-start | bytes 3076
  7.2 12.5 %copy-start.6 = (s32[128,2]{0,1:T(2,128)S(1)}, s32[128,2]{0,1:T(2,128)}, u32[]{:S(2)}) copy-start(s32[128,2]{0,1:T(2,128)} %param.13) | copy-start | bytes 3076
  7.2 12.8 %copy-start.3 = (bf16[128,512]{1,0:T(8,128)(2,1)S(1)}, bf16[128,512]{1,0:T(8,128)(2,1)}, u32[]{:S(2)}) copy-start(bf16[128,512]{1,0:T(8,128)(2,1)} %param.17) | copy-start | bytes 393220
  11.4 33.5 %all-to-all-start = ((bf16[256,8,512]{0,2,1:T(8,128)(2,1)}), bf16[256,8,512]{0,2,1:T(8,128)(2,1)S(1)}, u32[]{:S(2)}, u32[]{:S(2)}) async-start(bf16[256,8,512]{0,2,1:T(8,128)(2,1)} %bitcast.118), calls=%async_computation | async-start | bytes 4194304 | tf_op jit(solution)/shard_map/all_to_all | solution.py:39
  18.4 69.4 %all-gather.4.cloned.1.call-start = ((), (), s32[]{:S(2)}) async-start(), calls=%async_computation.6 | async-start | bytes 4456448 | tf_op jit(solution)/shard_map/all_gather | solution.py:45
  44.8 1.3 copy-start.2
  50.1 86.9 %all-gather.6.cloned.1.call-start = ((), (), s32[]{:S(2)}) async-start(), calls=%async_computation.7 | async-start | bytes 6684672 | tf_op jit(solution)/shard_map/all_gather | solution.py:48
  87.8 94.1 %all-gather.8.cloned.1.call-start = ((), (), s32[]{:S(2)}) async-start(), calls=%async_computation.8 | async-start | bytes 6684672 | tf_op jit(solution)/shard_map/all_gather | solution.py:62
  137.0 141.4 %reduce-scatter.3.cloned.1.call-start = ((), (), s32[]{:S(2)}) async-start(), calls=%async_computation.9 | async-start | bytes 6684672 | tf_op jit(solution)/shard_map/reduce_scatter | solution.py:76
  181.9 7.1 %copy-start.7 = (bf16[1,768,4096]{2,1,0:T(8,128)(2,1)S(1)}, bf16[1,768,4096]{2,1,0:T(8,128)(2,1)}, u32[]{:S(2)}) copy-start(bf16[1,768,4096]{2,1,0:T(8,128)(2,1)} %all-gather.8.cloned.1.call-done) | copy-start | bytes 18874372
  181.9 7.1 %copy-start.9 = (bf16[1,4096,448]{1,2,0:T(8,128)(2,1)S(1)}, bf16[1,4096,448]{1,2,0:T(8,128)(2,1)}, u32[]{:S(2)}) copy-start(bf16[1,4096,448]{1,2,0:T(8,128)(2,1)} %param.15) | copy-start | bytes 11010052
  181.9 7.1 %copy-start.13 = (f32[768,448]{0,1:T(8,128)S(1)}, f32[768,448]{0,1:T(8,128)}, u32[]{:S(2)}) copy-start(f32[768,448]{0,1:T(8,128)} %fusion.2) | copy-start | bytes 4128772
  189.0 4.4 %copy-start.8 = (bf16[1,448,4096]{2,1,0:T(8,128)(2,1)S(1)}, bf16[1,448,4096]{2,1,0:T(8,128)(2,1)}, u32[]{:S(2)}) copy-start(bf16[1,448,4096]{2,1,0:T(8,128)(2,1)} %param.16) | copy-start | bytes 11010052
  192.6 0.8 copy-start.11
  198.9 159.1 %reduce-scatter.5.cloned.1.call-start = ((), (), s32[]{:S(2)}) async-start(), calls=%async_computation.10 | async-start | bytes 6684672 | tf_op jit(solution)/shard_map/reduce_scatter | solution.py:79
  199.2 5.7 %copy-start.10 = (bf16[1,4096,448]{1,2,0:T(8,128)(2,1)S(1)}, bf16[1,4096,448]{1,2,0:T(8,128)(2,1)}, u32[]{:S(2)}) copy-start(bf16[1,4096,448]{1,2,0:T(8,128)(2,1)} %param.15) | copy-start | bytes 11010052
  210.7 1.1 copy-start.12
  362.4 17.7 %all-to-all-start.3 = ((bf16[8,48,2,512]{3,2,1,0:T(2,128)(2,1)}), bf16[8,48,2,512]{3,2,1,0:T(2,128)(2,1)S(1)}, u32[]{:S(2)}, u32[]{:S(2)}) async-start(bf16[8,48,2,512]{3,2,1,0:T(2,128)(2,1)} %maximum_bitcast_fusion), calls=%async_computation.5 | async-start | bytes 1572864 | tf_op jit(solution)/shard_map/all_to_all | solution.py:89
  376.2 5.1 %copy-start.4 = (bf16[128,512]{1,0:T(8,128)(2,1)S(1)}, bf16[128,512]{1,0:T(8,128)(2,1)}, u32[]{:S(2)}) copy-start(bf16[128,512]{1,0:T(8,128)(2,1)} %param.17) | copy-start | bytes 393220
  380.2 2.8 copy-start.1
Sparse Core Ops, SparseCore 0:
  50.2 37.5 all-gather.3
  90.1 46.8 all-gather.5
  139.2 42.6 all-gather.7
  199.0 79.2 reduce-scatter.2
  280.6 77.3 reduce-scatter.4

commit v9 on v8

--- a/solution.py
+++ b/solution.py
@@ -36,10 +36,10 @@
         .astype(jnp.bfloat16)
         .reshape(n_branch, capacity, width)
     )
-    pieces = lax.all_to_all(branch_wo[0], "branch", split_axis=1, concat_axis=0, tiled=True)
+    pieces = lax.all_to_all(branch_wo[0], "branch", split_axis=1, concat_axis=1, tiled=True)
     pieces, send_grads = lax.optimization_barrier((pieces, send_grads))
     summed = jnp.sum(
-        pieces.reshape(n_branch, -1, width).astype(jnp.float32), axis=0
+        pieces.reshape(-1, n_branch, width).astype(jnp.float32), axis=1
     )
     mean_block = (summed / n_branch).astype(jnp.bfloat16)
     wo_full = lax.all_gather(mean_block, "dp", axis=0, tiled=True)

time: 390 us -> 400 us (1.026)
  waiting for transfers between devices: 234 us -> 248 us
    all_gather x1, waiting for transfers between devices: 22 us -> 29.7 us  [shards(): wo_full = lax.all_gather(mean_block, 'dp', axis=0, tiled=True)]
    unnamed x35 -> x33, local copies, waits for them, and re-layouts: 11.5 us -> 9.36 us
  transfers between devices with their start and end apart: 7 -> 7, of which waited for: 7 -> 7; matrix products, arithmetic and copies ran while one was open for 14% -> 13% of each run, Pallas kernels for 0% -> 0%
where the time goes in v9:
time: 400 us; the launch traced here: 399 us
  waiting for transfers between devices  248 us (62%)
  matrix products  61.6 us (15%)
  blocking collectives  36.4 us (9%)
  local copies, waits for them, and re-layouts  19.6 us (5%)
  between operations  14.1 us (4%)
  starting transfers between devices  13.8 us (3%)
  other arithmetic  5.41 us (1%)
    reduce_scatter x1, waiting for transfers between devices, shards(): lax.psum_scatter(input_term.astype(jnp.bfloat16), 'dp', scatter_dimension...  78.2 us
    reduce_scatter x1, waiting for transfers between devices, shards(): lax.psum_scatter(output_term.astype(jnp.bfloat16), 'dp', scatter_dimensio...  52.2 us
    all_gather x1, waiting for transfers between devices, shards(): all_rows = lax.all_gather(got_rows, 'dp', axis=1, tiled=True)  36.5 us
    all_gather x1, waiting for transfers between devices, shards(): wo_full = lax.all_gather(mean_block, 'dp', axis=0, tiled=True)  29.7 us
    all_to_all x1, waiting for transfers between devices, shards(): lax.all_to_all(branch_wo[0], 'branch', split_axis=1, concat_axis=1, tiled...  23.9 us
    all_gather x1, waiting for transfers between devices, shards(): all_grads = lax.all_gather(got_grads, 'dp', axis=1, tiled=True)  23 us
    all_to_all x1, blocking collectives, shards(): lax.all_to_all(send_rows, 'branch', split_axis=0, concat_axis=2, tiled=True)  21.5 us
    all_to_all x1, blocking collectives, shards(): lax.all_to_all(send_grads, 'branch', split_axis=0, concat_axis=2, tiled=T...  14.9 us
  transfers between devices with their start and end apart: 7, of which 7 were waited for; matrix products, arithmetic and copies ran while one was open for 13% of the time, Pallas kernels for 0%

profile of v9, /device:TPU:0, one launch (start us, length us, event | category | flops | bytes accessed | tf_op | source)
XLA Modules:
  0.0 398.8 jit_solution(1686763570094163775)
XLA Ops:
  7.2 3.4 copy.59
  10.6 2.4 copy.60
  13.0 7.0 %all-to-all-start = ((bf16[256,8,512]{2,0,1:T(8,128)(2,1)}), bf16[256,8,512]{2,0,1:T(8,128)(2,1)}, u32[]{:S(2)}, u32[]{:S(2)}) async-start(bf16[256,8,512]{2,0,1:T(8,128)(2,1)} %copy.60), calls=%async_computation | async-start | bytes 4194304 | tf_op jit(solution)/shard_map/all_to_all | solution.py:39
  22.6 23.9 %all-to-all-done = bf16[256,8,512]{2,0,1:T(8,128)(2,1)} async-done(((bf16[256,8,512]{2,0,1:T(8,128)(2,1)}), bf16[256,8,512]{2,0,1:T(8,128)(2,1)}, u32[]{:S(2)}, u32[]{:S(2)}) %all-to-all-start) | async-done | bytes 2097184 | tf_op jit(solution)/shard_map/all_to_all | solution.py:39
  46.5 2.8 copy.61
  50.5 14.9 %all_to_all.53 = bf16[8,48,512]{2,1,0:T(8,128)(2,1)S(1)} all-to-all(bf16[8,48,512]{2,1,0:T(8,128)(2,1)S(1)} %bitcast.121), channel_id=1, replica_groups=mesh['branch'=8,'dp'=16] {'branch'}, dimensions={0} | all-to-all | bytes 786432 | tf_op jit(solution)/shard_map/all_to_all | solution.py:46
  65.4 0.8 copy.77
  66.2 29.7 %all-gather.4.cloned.1.call-done = bf16[4096,512]{0,1:T(8,128)(2,1)} async-done(((bf16[256,512]{0,1:T(8,128)(2,1)}), bf16[4096,512]{0,1:T(8,128)(2,1)}) %all-gather.4.cloned.1.call-update) | async-done | bytes 4194320 | tf_op jit(solution)/shard_map/all_gather | solution.py:45
  96.0 1.0 copy.58
  97.0 3.4 fusion.39
  101.1 21.5 %all_to_all.54 = bf16[8,48,512]{2,1,0:T(8,128)(2,1)S(1)} all-to-all(bf16[8,48,512]{2,1,0:T(8,128)(2,1)S(1)} %bitcast.124), channel_id=1, replica_groups=mesh['branch'=8,'dp'=16] {'branch'}, dimensions={0} | all-to-all | bytes 786432 | tf_op jit(solution)/shard_map/all_to_all | solution.py:60
  122.6 0.8 copy.78
  123.4 23.0 %all-gather.6.cloned.1.call-done = bf16[1,768,4096]{2,1,0:T(8,128)(2,1)} async-done(((bf16[1,48,4096]{2,1,0:T(8,128)(2,1)}), bf16[1,768,4096]{2,1,0:T(8,128)(2,1)}) %all-gather.6.cloned.1.call-update) | async-done | bytes 6291472 | tf_op jit(solution)/shard_map/all_gather | solution.py:48
  146.6 8.0 %fusion.2 = f32[768,448]{0,1:T(8,128)} fusion(bf16[1,768,4096]{2,1,0:T(8,128)(2,1)} %all-gather.6.cloned.1.call-done, bf16[1,448,4096]{2,1,0:T(8,128)(2,1)} %param.16), kind=kOutput, calls=%fused_computation.4 | convolution fusion | flops 2818572288 | bytes 11337728 | tf_op jit(solution)/shard_map/rd,fd->rf/dot_general | solution.py:67
  154.6 36.5 %all-gather.8.cloned.1.call-done = bf16[1,768,4096]{2,1,0:T(8,128)(2,1)} async-done(((bf16[1,48,4096]{2,1,0:T(8,128)(2,1)}), bf16[1,768,4096]{2,1,0:T(8,128)(2,1)}) %all-gather.8.cloned.1.call-update) | async-done | bytes 6291472 | tf_op jit(solution)/shard_map/all_gather | solution.py:62
  191.2 7.0 %fusion.10 = f32[768,448]{0,1:T(8,128)S(1)} fusion(bf16[1,768,4096]{2,1,0:T(8,128)(2,1)} %all-gather.8.cloned.1.call-done, bf16[1,4096,448]{1,2,0:T(8,128)(2,1)} %param.14), kind=kOutput, calls=%fused_computation.12 | convolution fusion | flops 2818572288 | bytes 11337728 | tf_op jit(solution)/shard_map/dot_general | solution.py:65
  198.3 3.5 multiply_convert_fusion.2
  201.8 0.8 copy-done.10
  202.7 5.3 %convolution_convert_fusion = bf16[768,4096]{1,0:T(8,128)(2,1)} fusion(bf16[768,448]{0,1:T(8,128)(2,1)S(1)} %get-tuple-element.42, bf16[1,448,4096]{2,1,0:T(8,128)(2,1)S(1)} %copy-done.7), kind=kOutput, calls=%fused_computation.1 | convolution fusion | flops 2821718016 | bytes 10649600 | tf_op jit(solution)/shard_map/dot_general | solution.py:72
  208.3 5.7 %fusion.34 = f32[768,4096]{1,0:T(8,128)S(1)} fusion(bf16[768,448]{0,1:T(8,128)(2,1)S(1)} %get-tuple-element.43, bf16[1,4096,448]{1,2,0:T(8,128)(2,1)} %param.14), kind=kOutput, calls=%fused_computation.25 | convolution fusion | flops 2818572288 | bytes 16941056 | tf_op jit(solution)/shard_map/rf,df->rd/dot_general | solution.py:73
  214.1 5.7 %add_convert_fusion = bf16[768,4096]{1,0:T(8,128)(2,1)} fusion(f32[768,4096]{1,0:T(8,128)S(1)} %fusion.34, bf16[768,448]{0,1:T(8,128)(2,1)S(1)} %get-tuple-element.44, bf16[1,4096,448]{1,2,0:T(8,128)(2,1)S(1)} %copy-done.9), kind=kOutput, calls=%fused_computation | convolution fusion | flops 2824863744 | bytes 23232512 | tf_op jit(solution)/shard_map/rf,df->rd/dot_general | solution.py:75
  220.0 0.8 copy-done.11
  220.9 7.2 %fusion.21 = bf16[1,448,4096]{2,1,0:T(8,128)(2,1)} fusion(bf16[768,448]{0,1:T(8,128)(2,1)S(1)} %copy-done.11, bf16[1,768,4096]{2,1,0:T(8,128)(2,1)} %all-gather.6.cloned.1.call-done), kind=kOutput, calls=%fused_computation.17 | convolution fusion | flops 2820407296 | bytes 10649600 | tf_op jit(solution)/shard_map/rf,rd->fd/dot_general | solution.py:71
  228.1 7.3 %fusion.24 = bf16[1,4096,448]{1,2,0:T(8,128)(2,1)} fusion(bf16[768,448]{0,1:T(8,128)(2,1)S(1)} %get-tuple-element.43, bf16[1,768,4096]{2,1,0:T(8,128)(2,1)} %all-gather.8.cloned.1.call-done), kind=kOutput, calls=%fused_computation.18 | convolution fusion | flops 2820407296 | bytes 10649600 | tf_op jit(solution)/shard_map/rd,rf->df/dot_general | solution.py:69
  235.4 52.2 %reduce-scatter.3.cloned.1.call-done = bf16[48,4096]{1,0:T(8,128)(2,1)} async-done(((bf16[768,4096]{1,0:T(8,128)(2,1)}), bf16[48,4096]{1,0:T(8,128)(2,1)}) %reduce-scatter.3.cloned.1.call-update) | async-done | bytes 393232 | tf_op jit(solution)/shard_map/reduce_scatter | solution.py:76
  287.6 1.1 copy.79
  289.4 78.2 %reduce-scatter.5.cloned.1.call-done = bf16[48,4096]{1,0:T(8,128)(2,1)} async-done(((bf16[768,4096]{1,0:T(8,128)(2,1)}), bf16[48,4096]{1,0:T(8,128)(2,1)}) %reduce-scatter.5.cloned.1.call-update) | async-done | bytes 393232 | tf_op jit(solution)/shard_map/reduce_scatter | solution.py:79
  367.6 1.1 copy.80
  369.3 2.7 maximum_bitcast_fusion
  372.0 6.1 %all-to-all-start.3 = ((bf16[8,48,2,512]{3,2,1,0:T(2,128)(2,1)}), bf16[8,48,2,512]{3,2,1,0:T(2,128)(2,1)S(1)}, u32[]{:S(2)}, u32[]{:S(2)}) async-start(bf16[8,48,2,512]{3,2,1,0:T(2,128)(2,1)} %maximum_bitcast_fusion), calls=%async_computation.5 | async-start | bytes 1572864 | tf_op jit(solution)/shard_map/all_to_all | solution.py:89
  378.1 7.2 %fusion.27 = bf16[1,4096,448]{1,2,0:T(8,128)(2,1)} fusion(bf16[768,448]{0,1:T(8,128)(2,1)S(1)} %get-tuple-element.44, bf16[1,768,4096]{2,1,0:T(8,128)(2,1)} %all-gather.8.cloned.1.call-done), kind=kOutput, calls=%fused_computation.19 | convolution fusion | flops 2820407296 | bytes 10649600 | tf_op jit(solution)/shard_map/rd,rf->df/dot_general | solution.py:70
  385.3 4.2 %all-to-all-done.3 = bf16[8,48,2,512]{3,2,1,0:T(2,128)(2,1)S(1)} async-done(((bf16[8,48,2,512]{3,2,1,0:T(2,128)(2,1)}), bf16[8,48,2,512]{3,2,1,0:T(2,128)(2,1)S(1)}, u32[]{:S(2)}, u32[]{:S(2)}) %all-to-all-start.3) | async-done | bytes 786464 | tf_op jit(solution)/shard_map/all_to_all | solution.py:89
  (70 shorter events, 9.0 us)
Async XLA Ops:
  7.2 89.9 %copy-start = (bf16[128,4096]{1,0:T(8,128)(2,1)S(1)}, bf16[128,4096]{1,0:T(8,128)(2,1)}, u32[]{:S(2)}) copy-start(bf16[128,4096]{1,0:T(8,128)(2,1)} %param.10) | copy-start | bytes 3145732
  10.6 9.5 %copy-start.4 = (s32[128,2]{0,1:T(2,128)S(1)}, s32[128,2]{0,1:T(2,128)}, u32[]{:S(2)}) copy-start(s32[128,2]{0,1:T(2,128)} %param.12) | copy-start | bytes 3076
  10.6 10.8 %copy-start.5 = (s32[128,2]{0,1:T(2,128)S(1)}, s32[128,2]{0,1:T(2,128)}, u32[]{:S(2)}) copy-start(s32[128,2]{0,1:T(2,128)} %param.13) | copy-start | bytes 3076
  10.6 11.1 %copy-start.2 = (bf16[128,512]{1,0:T(8,128)(2,1)S(1)}, bf16[128,512]{1,0:T(8,128)(2,1)}, u32[]{:S(2)}) copy-start(bf16[128,512]{1,0:T(8,128)(2,1)} %param.17) | copy-start | bytes 393220
  13.0 33.6 %all-to-all-start = ((bf16[256,8,512]{2,0,1:T(8,128)(2,1)}), bf16[256,8,512]{2,0,1:T(8,128)(2,1)}, u32[]{:S(2)}, u32[]{:S(2)}) async-start(bf16[256,8,512]{2,0,1:T(8,128)(2,1)} %copy.60), calls=%async_computation | async-start | bytes 4194304 | tf_op jit(solution)/shard_map/all_to_all | solution.py:39
  20.0 75.9 %all-gather.4.cloned.1.call-start = ((), (), s32[]{:S(2)}) async-start(), calls=%async_computation.6 | async-start | bytes 4456448 | tf_op jit(solution)/shard_map/all_gather | solution.py:45
  50.5 95.9 %all-gather.6.cloned.1.call-start = ((), (), s32[]{:S(2)}) async-start(), calls=%async_computation.7 | async-start | bytes 6684672 | tf_op jit(solution)/shard_map/all_gather | solution.py:48
  95.9 95.2 %all-gather.8.cloned.1.call-start = ((), (), s32[]{:S(2)}) async-start(), calls=%async_computation.8 | async-start | bytes 6684672 | tf_op jit(solution)/shard_map/all_gather | solution.py:62
  146.4 141.2 %reduce-scatter.3.cloned.1.call-start = ((), (), s32[]{:S(2)}) async-start(), calls=%async_computation.9 | async-start | bytes 6684672 | tf_op jit(solution)/shard_map/reduce_scatter | solution.py:76
  191.2 7.1 %copy-start.6 = (bf16[1,768,4096]{2,1,0:T(8,128)(2,1)S(1)}, bf16[1,768,4096]{2,1,0:T(8,128)(2,1)}, u32[]{:S(2)}) copy-start(bf16[1,768,4096]{2,1,0:T(8,128)(2,1)} %all-gather.8.cloned.1.call-done) | copy-start | bytes 18874372
  191.2 7.1 %copy-start.8 = (bf16[1,4096,448]{1,2,0:T(8,128)(2,1)S(1)}, bf16[1,4096,448]{1,2,0:T(8,128)(2,1)}, u32[]{:S(2)}) copy-start(bf16[1,4096,448]{1,2,0:T(8,128)(2,1)} %param.15) | copy-start | bytes 11010052
  191.2 7.1 %copy-start.12 = (f32[768,448]{0,1:T(8,128)S(1)}, f32[768,448]{0,1:T(8,128)}, u32[]{:S(2)}) copy-start(f32[768,448]{0,1:T(8,128)} %fusion.2) | copy-start | bytes 4128772
  198.3 4.4 %copy-start.7 = (bf16[1,448,4096]{2,1,0:T(8,128)(2,1)S(1)}, bf16[1,448,4096]{2,1,0:T(8,128)(2,1)}, u32[]{:S(2)}) copy-start(bf16[1,448,4096]{2,1,0:T(8,128)(2,1)} %param.16) | copy-start | bytes 11010052
  201.8 0.8 copy-start.10
  208.0 159.6 %reduce-scatter.5.cloned.1.call-start = ((), (), s32[]{:S(2)}) async-start(), calls=%async_computation.10 | async-start | bytes 6684672 | tf_op jit(solution)/shard_map/reduce_scatter | solution.py:79
  208.3 5.7 %copy-start.9 = (bf16[1,4096,448]{1,2,0:T(8,128)(2,1)S(1)}, bf16[1,4096,448]{1,2,0:T(8,128)(2,1)}, u32[]{:S(2)}) copy-start(bf16[1,4096,448]{1,2,0:T(8,128)(2,1)} %param.15) | copy-start | bytes 11010052
  219.8 1.1 copy-start.11
  372.0 17.5 %all-to-all-start.3 = ((bf16[8,48,2,512]{3,2,1,0:T(2,128)(2,1)}), bf16[8,48,2,512]{3,2,1,0:T(2,128)(2,1)S(1)}, u32[]{:S(2)}, u32[]{:S(2)}) async-start(bf16[8,48,2,512]{3,2,1,0:T(2,128)(2,1)} %maximum_bitcast_fusion), calls=%async_computation.5 | async-start | bytes 1572864 | tf_op jit(solution)/shard_map/all_to_all | solution.py:89
  385.3 5.3 %copy-start.3 = (bf16[128,512]{1,0:T(8,128)(2,1)S(1)}, bf16[128,512]{1,0:T(8,128)(2,1)}, u32[]{:S(2)}) copy-start(bf16[128,512]{1,0:T(8,128)(2,1)} %param.17) | copy-start | bytes 393220
  389.5 2.8 copy-start.1
Sparse Core Ops, SparseCore 0:
  50.6 45.2 all-gather.3
  98.2 48.1 all-gather.5
  148.7 42.4 all-gather.7
  208.2 79.4 reduce-scatter.2
  289.9 77.6 reduce-scatter.4
